TPU v7x, 32 devices: a whole 2x2x4 slice. The times are simulated.
32 devices in a mesh: grp: 4 (over y, x), dp: 8 (over z, core).
Axes of the slice: x: 2, y: 2, z: 4, core: 2. Of those that a mesh axis runs over, the one named last changes fastest.
Arguments:
- inputs: bfloat16 [32768, 384], P(('grp', 'dp'))
- cotangent: bfloat16 [32768, 384], P(('grp', 'dp')), may hold values from -6 to 6
- group_interval: int32 [4], replicated, may hold values from 0 to 2, as said below
- sample_counts: int32 [4], replicated, may hold values from 100 to 999
- rollout_start: int32 [4], replicated, may hold values from 0 to 18, as said below
- lead_table: float32 [3, 384], replicated, may hold values from -5 to 5
- qkv_master: float32 [442368], P('dp'), may hold values from -0.3125 to 0.3125
- proj_master: float32 [147456], P('dp'), may hold values from -1.25 to 1.25
- up_master: float32 [589824], P('dp'), may hold values from -0.3125 to 0.3125
- down_master: float32 [589824], P('dp'), may hold values from -0.15625 to 0.15625
- ada_master: float32 [884736], P('dp'), may hold values from -0.3125 to 0.3125
- bias_master: float32 [5376], P('dp'), may hold values from -0.6 to 0.6
- qkv_first: float32 [442368], P('dp'), may hold values from -4 to 4
- proj_first: float32 [147456], P('dp'), may hold values from -4 to 4
- up_first: float32 [589824], P('dp'), may hold values from -4 to 4
- down_first: float32 [589824], P('dp'), may hold values from -4 to 4
- ada_first: float32 [884736], P('dp'), may hold values from -4 to 4
- bias_first: float32 [5376], P('dp'), may hold values from -4 to 4
- qkv_second: float32 [442368], P('dp'), may hold values from 1 to 4
- proj_second: float32 [147456], P('dp'), may hold values from 1 to 4
- up_second: float32 [589824], P('dp'), may hold values from 1 to 4
- down_second: float32 [589824], P('dp'), may hold values from 1 to 4
- ada_second: float32 [884736], P('dp'), may hold values from 1 to 4
- bias_second: float32 [5376], P('dp'), may hold values from 1 to 4
Outputs:
- block_output: float32 [32768, 384], P(('grp', 'dp'))
- input_grad: float32 [32768, 384], P(('grp', 'dp'))
- grad_norm: float32 [], replicated
- qkv_new: float32 [442368], P('dp')
- proj_new: float32 [147456], P('dp')
- up_new: float32 [589824], P('dp')
- down_new: float32 [589824], P('dp')
- ada_new: float32 [884736], P('dp')
- bias_new: float32 [5376], P('dp')
- qkv_first_new: float32 [442368], P('dp')
- proj_first_new: float32 [147456], P('dp')
- up_first_new: float32 [589824], P('dp')
- down_first_new: float32 [589824], P('dp')
- ada_first_new: float32 [884736], P('dp')
- bias_first_new: float32 [5376], P('dp')
- qkv_second_new: float32 [442368], P('dp')
- proj_second_new: float32 [147456], P('dp')
- up_second_new: float32 [589824], P('dp')
- down_second_new: float32 [589824], P('dp')
- ada_second_new: float32 [884736], P('dp')
- bias_second_new: float32 [5376], P('dp')
- qkv_copy: bfloat16 [442368], P('dp')
- proj_copy: bfloat16 [147456], P('dp')
- up_copy: bfloat16 [589824], P('dp')
- down_copy: bfloat16 [589824], P('dp')
- ada_copy: bfloat16 [884736], P('dp')
- bias_copy: bfloat16 [5376], P('dp')
Inputs may be any that keep to these rules, and one draw needn't show every extreme that they name: `group_interval`: every interval 0 to 2 is used by some group. `rollout_start`: even numbers; both 0 and 18 occur.
All inputs are finite; a program needn't handle non-finite values.
Results may differ from a plain program's by a relative error of at most 0.015.
The roundings to bfloat16 on the way count: a program that leaves them out, or rounds other values in their place, can miss the bound.
Values may be sent and summed in bfloat16 or wider, within the bound.
A program may use at most 192 MiB of HBM per device.

v0:
```python
import math

import jax
import jax.numpy as jnp
from jax import lax
from jax.sharding import PartitionSpec as P

D = 384
HEADS = 6
FF = 1536
ROLLOUT = 2
INTERVALS = 3
ADAM_STEP = 10
HEAD_DIM = 64
NPARAM = 2659584


norm_eps = 1e-06
learn_rate = 0.05
adam_eps = 1e-08


def times_t(left, right):
    return lax.dot_general(
        left, right, (((0,), (0,)), ((), ())), preferred_element_type=jnp.float32
    )


def times_back(left, right):
    return lax.dot_general(
        left, right, (((1,), (1,)), ((), ())), preferred_element_type=jnp.float32
    )


def layer_norm(stream):
    centred = stream - jnp.mean(stream, axis=-1, keepdims=True)
    inverse = lax.rsqrt(jnp.mean(centred * centred, axis=-1, keepdims=True) + norm_eps)
    return (centred * inverse, inverse)


def norm_back(normed, inverse, grad_out):
    mean_grad = jnp.mean(grad_out, axis=-1, keepdims=True)
    mean_prod = jnp.mean(grad_out * normed, axis=-1, keepdims=True)
    return inverse * (grad_out - mean_grad - normed * mean_prod)


def exact_gelu(value):
    return jax.nn.gelu(value, approximate=False)


def step_embedding(moment):
    half_width = D // 2
    freqs = jnp.exp(-math.log(10000.0) * jnp.arange(half_width, dtype=jnp.float32) / half_width)
    angles = moment * freqs
    return jnp.concatenate([jnp.sin(angles), jnp.cos(angles)])


def attend(queries, key_rows, value_rows):
    length = queries.shape[0]
    block_rows = min(512, length)
    block_count = length // block_rows
    score_scale = HEAD_DIM ** (-0.5)
    query_blocks = queries.reshape(block_count, block_rows, HEADS, HEAD_DIM)

    def block_scores(query_block):
        scores = (
            jnp.einsum("qhd,khd->hqk", query_block, key_rows, preferred_element_type=jnp.float32)
            * score_scale
        )
        top_score = jnp.max(scores, axis=-1, keepdims=True)
        log_total = top_score + jnp.log(
            jnp.sum(jnp.exp(scores - top_score), axis=-1, keepdims=True)
        )
        weights_low = jnp.exp(scores - log_total).astype(jnp.bfloat16)
        mixed = jnp.einsum(
            "hqk,khd->qhd", weights_low, value_rows, preferred_element_type=jnp.float32
        )
        return (mixed.astype(jnp.bfloat16), log_total)

    mixed, log_total = lax.map(block_scores, query_blocks)
    return (mixed.reshape(length, HEADS * HEAD_DIM), log_total)


def attend_back(queries, key_rows, value_rows, log_total, out_grad):
    length = queries.shape[0]
    block_rows = min(512, length)
    block_count = length // block_rows
    score_scale = HEAD_DIM ** (-0.5)
    query_blocks = queries.reshape(block_count, block_rows, HEADS, HEAD_DIM)
    grad_blocks = out_grad.reshape(block_count, block_rows, HEADS, HEAD_DIM)

    def block_back(running, pieces):
        query_block, total_block, grad_block = pieces
        scores = (
            jnp.einsum("qhd,khd->hqk", query_block, key_rows, preferred_element_type=jnp.float32)
            * score_scale
        )
        weights_soft = jnp.exp(scores - total_block)
        weights_low = weights_soft.astype(jnp.bfloat16)
        weight_grad = jnp.einsum(
            "qhd,khd->hqk", grad_block, value_rows, preferred_element_type=jnp.float32
        )
        row_delta = jnp.sum(weights_soft * weight_grad, axis=-1, keepdims=True)
        score_grad = (weights_soft * (weight_grad - row_delta)).astype(jnp.bfloat16)
        query_grad = (
            jnp.einsum("hqk,khd->qhd", score_grad, key_rows, preferred_element_type=jnp.float32)
            * score_scale
        )
        key_grad = (
            running[0]
            + jnp.einsum(
                "hqk,qhd->khd", score_grad, query_block, preferred_element_type=jnp.float32
            )
            * score_scale
        )
        value_grad = running[1] + jnp.einsum(
            "hqk,qhd->khd", weights_low, grad_block, preferred_element_type=jnp.float32
        )
        return ((key_grad, value_grad), query_grad)

    zero_rows = jnp.zeros((length, HEADS, HEAD_DIM), jnp.float32)
    (key_grad, value_grad), query_grad = lax.scan(
        block_back, (zero_rows, zero_rows), (query_blocks, log_total, grad_blocks)
    )
    return (
        query_grad.reshape(length, D),
        key_grad.reshape(length, D),
        value_grad.reshape(length, D),
    )


def advance(stream, condition, matrices, biases):
    w_qkv, w_proj, w_up, w_down, w_ada = matrices
    b_query, b_value, b_proj, b_up, b_down, b_ada = biases
    modulation = jnp.dot(condition[None, :], w_ada, preferred_element_type=jnp.float32)[0] + b_ada
    shift_one, scale_one, gate_one, shift_two, scale_two, gate_two = jnp.split(modulation, 6)
    normed_one, inverse_one = layer_norm(stream)
    hidden_one = (normed_one * (1.0 + scale_one) + shift_one).astype(jnp.bfloat16)
    zero_bias = jnp.zeros_like(b_query)
    qkv_low = (
        jnp.dot(hidden_one, w_qkv, preferred_element_type=jnp.float32)
        + jnp.concatenate([b_query, zero_bias, b_value])
    ).astype(jnp.bfloat16)
    length = stream.shape[0]
    queries = qkv_low[:, :D].reshape(length, HEADS, HEAD_DIM)
    key_rows = qkv_low[:, D : 2 * D].reshape(length, HEADS, HEAD_DIM)
    value_rows = qkv_low[:, 2 * D :].reshape(length, HEADS, HEAD_DIM)
    attended, log_total = attend(queries, key_rows, value_rows)
    branch_one = jnp.dot(attended, w_proj, preferred_element_type=jnp.float32) + b_proj
    middle = stream + gate_one * branch_one
    normed_two, inverse_two = layer_norm(middle)
    hidden_two = (normed_two * (1.0 + scale_two) + shift_two).astype(jnp.bfloat16)
    upward = jnp.dot(hidden_two, w_up, preferred_element_type=jnp.float32) + b_up
    act_low = exact_gelu(upward).astype(jnp.bfloat16)
    branch_two = jnp.dot(act_low, w_down, preferred_element_type=jnp.float32) + b_down
    result = middle + gate_two * branch_two
    saved_values = (
        gate_one,
        gate_two,
        scale_one,
        scale_two,
        normed_one,
        inverse_one,
        hidden_one,
        queries,
        key_rows,
        value_rows,
        log_total,
        attended,
        branch_one,
        normed_two,
        inverse_two,
        hidden_two,
        upward,
        act_low,
        branch_two,
    )
    return (result, saved_values)


def retreat(saved_values, grad_out, condition, matrices):
    (
        gate_one,
        gate_two,
        scale_one,
        scale_two,
        normed_one,
        inverse_one,
        hidden_one,
        queries,
        key_rows,
        value_rows,
        log_total,
        attended,
        branch_one,
        normed_two,
        inverse_two,
        hidden_two,
        upward,
        act_low,
        branch_two,
    ) = saved_values
    w_qkv, w_proj, w_up, w_down, w_ada = matrices
    down_grad = (gate_two * grad_out).astype(jnp.bfloat16)
    gate_two_grad = jnp.sum(grad_out * branch_two, axis=0)
    down_w_grad = times_t(act_low, down_grad)
    down_b_grad = jnp.sum(down_grad.astype(jnp.float32), axis=0)
    act_grad = times_back(down_grad, w_down)
    unused_value, gelu_pull = jax.vjp(exact_gelu, upward)
    up_grad = gelu_pull(act_grad)[0].astype(jnp.bfloat16)
    up_w_grad = times_t(hidden_two, up_grad)
    up_b_grad = jnp.sum(up_grad.astype(jnp.float32), axis=0)
    hidden_two_grad = times_back(up_grad, w_up)
    shift_two_grad = jnp.sum(hidden_two_grad, axis=0)
    scale_two_grad = jnp.sum(hidden_two_grad * normed_two, axis=0)
    middle_grad = grad_out + norm_back(normed_two, inverse_two, hidden_two_grad * (1.0 + scale_two))
    proj_grad = (gate_one * middle_grad).astype(jnp.bfloat16)
    gate_one_grad = jnp.sum(middle_grad * branch_one, axis=0)
    proj_w_grad = times_t(attended, proj_grad)
    proj_b_grad = jnp.sum(proj_grad.astype(jnp.float32), axis=0)
    attended_grad = times_back(proj_grad, w_proj).astype(jnp.bfloat16)
    query_grad, key_grad, value_grad = attend_back(
        queries, key_rows, value_rows, log_total, attended_grad
    )
    qkv_grad = jnp.concatenate([query_grad, key_grad, value_grad], axis=1).astype(jnp.bfloat16)
    qkv_w_grad = times_t(hidden_one, qkv_grad)
    qkv_b_sum = jnp.sum(qkv_grad.astype(jnp.float32), axis=0)
    hidden_one_grad = times_back(qkv_grad, w_qkv)
    shift_one_grad = jnp.sum(hidden_one_grad, axis=0)
    scale_one_grad = jnp.sum(hidden_one_grad * normed_one, axis=0)
    stream_grad = middle_grad + norm_back(
        normed_one, inverse_one, hidden_one_grad * (1.0 + scale_one)
    )
    modulation_grad = jnp.concatenate(
        [
            shift_one_grad,
            scale_one_grad,
            gate_one_grad,
            shift_two_grad,
            scale_two_grad,
            gate_two_grad,
        ]
    )
    ada_w_grad = condition.astype(jnp.float32)[:, None] * modulation_grad[None, :]
    bias_grad = jnp.concatenate(
        [qkv_b_sum[:D], qkv_b_sum[2 * D :], proj_b_grad, up_b_grad, down_b_grad, modulation_grad]
    )
    return (stream_grad, (qkv_w_grad, proj_w_grad, up_w_grad, down_w_grad, ada_w_grad, bias_grad))


def per_device(
    inputs,
    cotangent,
    group_interval,
    sample_counts,
    rollout_start,
    lead_table,
    qkv_master,
    proj_master,
    up_master,
    down_master,
    ada_master,
    bias_master,
    qkv_first,
    proj_first,
    up_first,
    down_first,
    ada_first,
    bias_first,
    qkv_second,
    proj_second,
    up_second,
    down_second,
    ada_second,
    bias_second,
):
    masters = (qkv_master, proj_master, up_master, down_master, ada_master, bias_master)
    firsts = (qkv_first, proj_first, up_first, down_first, ada_first, bias_first)
    seconds = (qkv_second, proj_second, up_second, down_second, ada_second, bias_second)
    gathered = (
        lax.all_gather(qkv_master.astype(jnp.bfloat16), "dp", axis=0, tiled=True),
        lax.all_gather(proj_master.astype(jnp.bfloat16), "dp", axis=0, tiled=True),
        lax.all_gather(up_master.astype(jnp.bfloat16), "dp", axis=0, tiled=True),
        lax.all_gather(down_master.astype(jnp.bfloat16), "dp", axis=0, tiled=True),
        lax.all_gather(ada_master.astype(jnp.bfloat16), "dp", axis=0, tiled=True),
        lax.all_gather(bias_master.astype(jnp.bfloat16), "dp", axis=0, tiled=True),
    )
    matrices = (
        gathered[0].reshape(D, 3 * D),
        gathered[1].reshape(D, D),
        gathered[2].reshape(D, FF),
        gathered[3].reshape(FF, D),
        gathered[4].reshape(D, 6 * D),
    )
    bias_full = gathered[5].astype(jnp.float32)
    biases = (
        bias_full[0:D],
        bias_full[D : 2 * D],
        bias_full[2 * D : 3 * D],
        bias_full[3 * D : 3 * D + FF],
        bias_full[3 * D + FF : 4 * D + FF],
        bias_full[4 * D + FF :],
    )
    group_index = lax.axis_index("grp")
    group_total = lax.axis_size("grp")
    own_group = jnp.arange(group_total) == group_index
    interval = jnp.sum(jnp.where(own_group, group_interval, 0))
    start_step = jnp.sum(jnp.where(own_group, rollout_start, 0)).astype(jnp.float32)
    own_count = jnp.sum(jnp.where(own_group, sample_counts, 0)).astype(jnp.float32)
    group_share = group_total * own_count / jnp.sum(sample_counts.astype(jnp.float32))
    lead_row = jnp.sum(
        jnp.where((jnp.arange(INTERVALS) == interval)[:, None], lead_table, 0.0), axis=0
    )
    conditions = [
        jax.nn.silu(lead_row + step_embedding(start_step + offset)).astype(jnp.bfloat16)
        for offset in range(ROLLOUT)
    ]
    streams = [inputs.astype(jnp.float32)]
    for offset in range(ROLLOUT):
        advanced, kept_values = advance(streams[-1], conditions[offset], matrices, biases)
        streams.append(advanced)
    block_output = streams[-1]
    grad_stream = cotangent.astype(jnp.float32)
    totals = None
    for offset in reversed(range(ROLLOUT)):
        unused, kept_values = advance(streams[offset], conditions[offset], matrices, biases)
        grad_stream, grad_parts = retreat(kept_values, grad_stream, conditions[offset], matrices)
        if totals is None:
            totals = grad_parts
        else:
            totals = tuple(
                (total_part + grad_part for total_part, grad_part in zip(totals, grad_parts))
            )
    flat_qkv = totals[0].reshape(-1) * group_share
    flat_proj = totals[1].reshape(-1) * group_share
    flat_up = totals[2].reshape(-1) * group_share
    flat_down = totals[3].reshape(-1) * group_share
    flat_ada = totals[4].reshape(-1) * group_share
    flat_bias = totals[5] * group_share
    summed = (
        lax.psum(flat_qkv.astype(jnp.bfloat16), "grp").astype(jnp.float32),
        lax.psum(flat_proj.astype(jnp.bfloat16), "grp").astype(jnp.float32),
        lax.psum(flat_up.astype(jnp.bfloat16), "grp").astype(jnp.float32),
        lax.psum(flat_down.astype(jnp.bfloat16), "grp").astype(jnp.float32),
        lax.psum(flat_ada.astype(jnp.bfloat16), "grp").astype(jnp.float32),
        lax.psum(flat_bias.astype(jnp.bfloat16), "grp").astype(jnp.float32),
    )
    shares = (
        lax.psum_scatter(summed[0], "dp", scatter_dimension=0, tiled=True),
        lax.psum_scatter(summed[1], "dp", scatter_dimension=0, tiled=True),
        lax.psum_scatter(summed[2], "dp", scatter_dimension=0, tiled=True),
        lax.psum_scatter(summed[3], "dp", scatter_dimension=0, tiled=True),
        lax.psum_scatter(summed[4], "dp", scatter_dimension=0, tiled=True),
        lax.psum_scatter(summed[5], "dp", scatter_dimension=0, tiled=True),
    )
    local_square = sum((jnp.sum(piece * piece) for piece in shares))
    total_square = lax.psum(local_square, "dp")
    grad_norm = jnp.sqrt(total_square)
    limit = math.sqrt(NPARAM)
    clip_scale = limit / jnp.maximum(grad_norm, limit)
    correction = 1.0 - 0.5**ADAM_STEP
    decays = [0.1, 0.1, 0.1, 0.1, 0.1, 0.0]
    news = []
    first_news = []
    second_news = []
    copies = []
    for index_w in range(6):
        clipped = shares[index_w] * clip_scale
        first_new = 0.5 * firsts[index_w] + 0.5 * clipped
        second_new = 0.5 * seconds[index_w] + 0.5 * clipped * clipped
        update = first_new / correction / (jnp.sqrt(second_new / correction) + adam_eps)
        new_master = masters[index_w] - learn_rate * (update + decays[index_w] * masters[index_w])
        news.append(new_master)
        first_news.append(first_new)
        second_news.append(second_new)
        copies.append(new_master.astype(jnp.bfloat16))
    return (
        block_output,
        grad_stream,
        grad_norm,
        news[0],
        news[1],
        news[2],
        news[3],
        news[4],
        news[5],
        first_news[0],
        first_news[1],
        first_news[2],
        first_news[3],
        first_news[4],
        first_news[5],
        second_news[0],
        second_news[1],
        second_news[2],
        second_news[3],
        second_news[4],
        second_news[5],
        copies[0],
        copies[1],
        copies[2],
        copies[3],
        copies[4],
        copies[5],
    )


def solution(mesh):
    placed = (
        P(("grp", "dp"), None),
        P(("grp", "dp"), None),
        P(),
        P(),
        P(),
        P(),
        P("dp"),
        P("dp"),
        P("dp"),
        P("dp"),
        P("dp"),
        P("dp"),
        P("dp"),
        P("dp"),
        P("dp"),
        P("dp"),
        P("dp"),
        P("dp"),
        P("dp"),
        P("dp"),
        P("dp"),
        P("dp"),
        P("dp"),
        P("dp"),
    )
    return jax.shard_map(
        per_device,
        mesh=mesh,
        in_specs=placed,
        out_specs=(
            P(("grp", "dp"), None),
            P(("grp", "dp"), None),
            P(),
            P("dp"),
            P("dp"),
            P("dp"),
            P("dp"),
            P("dp"),
            P("dp"),
            P("dp"),
            P("dp"),
            P("dp"),
            P("dp"),
            P("dp"),
            P("dp"),
            P("dp"),
            P("dp"),
            P("dp"),
            P("dp"),
            P("dp"),
            P("dp"),
            P("dp"),
            P("dp"),
            P("dp"),
            P("dp"),
            P("dp"),
            P("dp"),
        ),
        check_vma=False,
    )
```

profile of v0, /device:TPU:0, one launch (start us, length us, event | category | flops | bytes accessed | tf_op | source)
XLA Modules:
  0.0 905.8 jit_solution(14121447913624149790)
XLA Ops:
  15.5 30.4 %all-reduce = bf16[5376]{0:T(1024)(128)(2,1)S(1)} all-reduce(bf16[5376]{0:T(1024)(128)(2,1)S(1)} %dynamic-update-slice), channel_id=1, replica_groups=mesh['grp'=4,'dp'=8] {'dp'}, use_global_device_ids=true, to_apply=%add | all-reduce | flops 5376 | bytes 21504
  54.3 15.7 %all_gather.20 = bf16[442368]{0:T(1024)(128)(2,1)S(1)} all-gather(bf16[55296]{0:T(1024)(128)(2,1)S(1)} %convert_element_type.282), channel_id=1, replica_groups=mesh['grp'=4,'dp'=8] {'dp'}, dimensions={0}, use_global_device_ids=true | all-gather | bytes 995328 | tf_op jit(solution)/shard_map/all_gather | solution.py:281
  72.0 15.2 %all_gather.21 = bf16[147456]{0:T(1024)(128)(2,1)S(1)} all-gather(bf16[18432]{0:T(1024)(128)(2,1)S(1)} %convert_element_type.284), channel_id=1, replica_groups=mesh['grp'=4,'dp'=8] {'dp'}, dimensions={0}, use_global_device_ids=true | all-gather | bytes 331776 | tf_op jit(solution)/shard_map/all_gather | solution.py:282
  94.3 3.7 reshape.422
  101.0 3.6 reshape.416
  115.4 18.3 %while.77 = (s32[]{:T(128)}, bf16[2,512,6,64]{1,3,2,0:T(8,128)(2,1)}, f32[2,6,512,1]{2,1,3,0:T(8,128)S(1)}, bf16[2,512,6,64]{1,3,2,0:T(8,128)(2,1)}, bf16[1024,6...) while((s32[]{:T(128)}, bf16[2,512,6,64]{1,3,2,0:T(8,128)(2,1)}, ...), condition=%wide.region_35.36_spmd, body=%wide.region_32.35_spmd.sunk | while | flops 830665728 | bytes 40223824 | solution.py:80
  120.9 3.4 fusion.388
  129.9 3.4 fusion.388
  135.8 3.3 fusion.263
  142.1 18.0 %while.74 = (s32[]{:T(128)}, bf16[2,512,6,64]{1,3,2,0:T(8,128)(2,1)}, bf16[2,512,6,64]{1,3,2,0:T(8,128)(2,1)}, bf16[1024,6,64]{0,2,1:T(8,128)(2,1)S(1)}, bf16[1024,6,64]{0,2,1:T(8,128)(2,1)S(1)}, /*index=5*/s32[]{:T(128)}) while((s32[]{:T(128)}, bf16[2,512,6,64]{1,3,2,0:T(8,128)(2,1)}, bf16[2,512,6,64]{1,3,2,0:T(8,128)(2,1)}, ...), condition=%wide.region_8.9_spmd, body=%wide.region_5.8_spmd.sunk | while | flops 830665728 | bytes 40195140 | solution.py:80
  147.6 3.4 fusion.379
  156.6 3.4 fusion.379
  166.0 19.9 %fusion.272 = (f32[1024]{0:T(1024)S(1)}, f32[1024,384]{0,1:T(8,128)}) fusion(f32[1024,384]{0,1:T(8,128)} %copy-done.38, f32[384]{0:T(512)S(1)} %get-tuple-element.706, bf16[1536,384]{1,0:T(8,128)(2,1)} %reshape.423, bf16[384,1536]{1,0:T(8,128)(2,1)S(1)} %copy-done.39, f32[1536]{0:T(1024)S(1)} %slice.77, f32[384]{0:T(512)S(1)} %get-tuple-element.701, ...), kind=kOutput, calls=%fused_computation.479 | convolution fusion | flops 2523266048 | bytes 5529600 | tf_op jit(solution)/shard_map/dot_general | solution.py:155
  188.1 3.3 fusion.117
  197.9 18.2 %while.76 = (s32[]{:T(128)}, bf16[2,512,6,64]{1,3,2,0:T(8,128)(2,1)}, f32[2,6,512,1]{2,1,3,0:T(8,128)S(1)}, bf16[2,512,6,64]{1,3,2,0:T(8,128)(2,1)}, bf16[1024,6...) while((s32[]{:T(128)}, bf16[2,512,6,64]{1,3,2,0:T(8,128)(2,1)}, ...), condition=%wide.region_22.23_spmd, body=%wide.region_19.22_spmd.sunk | while | flops 830665728 | bytes 40223824 | solution.py:80
  203.7 3.4 fusion.385
  212.7 3.4 fusion.385
  218.2 3.6 fusion.264
  225.1 30.5 %multiply_convert_fusion.2 = (bf16[1024,1536]{1,0:T(8,128)(2,1)}, f32[1024,1536]{1,0:T(8,128)}, bf16[1024,1536]{1,0:T(8,128)(2,1)}, f32[1024,1536]{1,0:T(8,128)S(1)}, f32[1024,1536]{1,0:T(8,128)}) fusion(f32[1536]{0:T(1024)S(1)} %slice.77, f32[1024,1536]{1,0:T(8,128)S(1)} %fusion.243, bf16[384,1536]{1,0:T(8,128)(2,1)S(1)} %copy-done.40, ...), kind=kOutput, calls=%fused_computation.124 | convolution fusion | flops 1417543680 | bytes 34227200 | tf_op jit(solution)/shard_map/dot_general | solution.py:153
  255.6 4.8 convert_reduce_fusion.1
  260.4 3.5 fusion.277
  269.9 4.5 convert_reduce_fusion.8
  285.6 55.0 %while.78 = (s32[]{:T(128)}, f32[1024,6,64]{0,2,1:T(8,128)}, f32[1024,6,64]{0,2,1:T(8,128)}, bf16[2,512,6,64]{1,3,2,0:T(8,128)(2,1)}, bf16[2,512,6,64]{1,3,2,0:T...) while((s32[]{:T(128)}, f32[1024,6,64]{0,2,1:T(8,128)}, ...), condition=%wide.region_29.30_spmd.clone, body=%wide.region_27.29_spmd.clone.sunk | while | flops 2053174272 | bytes 209282288 | solution.py:122
  287.5 4.9 multiply_reduce_fusion.40
  292.4 4.7 multiply_convert_fusion.14
  297.1 5.4 bitcast_add_fusion.8
  302.5 6.2 fusion.399
  308.6 3.6 bitcast_add_fusion.9
  314.1 4.9 multiply_reduce_fusion.40
  319.1 4.7 multiply_convert_fusion.14
  323.7 5.8 bitcast_add_fusion.8
  329.5 6.2 fusion.399
  335.7 4.7 bitcast_add_fusion.9
  348.0 3.3 fusion.276
  355.9 4.4 convert_reduce_fusion.5
  360.4 7.6 convert_reduce_fusion
  368.1 3.5 fusion.275
  374.6 3.8 convert_reduce_fusion.6
  381.2 3.6 reshape.433
  387.1 53.9 %while.79 = (s32[]{:T(128)}, f32[1024,6,64]{0,2,1:T(8,128)}, f32[1024,6,64]{0,2,1:T(8,128)}, bf16[2,512,6,64]{1,3,2,0:T(8,128)(2,1)}, bf16[2,512,6,64]{1,3,2,0:T...) while((s32[]{:T(128)}, f32[1024,6,64]{0,2,1:T(8,128)}, ...), condition=%wide.region_42.43_spmd.clone, body=%wide.region_40.42_spmd.clone.sunk | while | flops 2053174272 | bytes 206140112 | solution.py:122
  389.0 4.3 multiply_reduce_fusion.41
  393.5 4.6 multiply_convert_fusion.15
  398.1 5.3 bitcast_add_fusion.10
  403.4 6.2 fusion.410
  409.6 3.5 bitcast_add_fusion.11
  415.1 4.3 multiply_reduce_fusion.41
  419.6 4.6 multiply_convert_fusion.15
  424.2 5.8 bitcast_add_fusion.10
  430.0 6.2 fusion.410
  436.2 4.7 bitcast_add_fusion.11
  451.6 3.4 fusion.234
  466.9 4.0 multiply_reduce_fusion.8
  475.4 4.8 fusion.123
  481.9 5.3 fusion.122
  487.2 3.5 convert_element_type.314
  493.5 4.5 fusion.121
  501.7 18.0 %while.75 = (s32[]{:T(128)}, bf16[2,512,6,64]{1,3,2,0:T(8,128)(2,1)}, bf16[2,512,6,64]{1,3,2,0:T(8,128)(2,1)}, bf16[1024,6,64]{0,2,1:T(8,128)(2,1)S(1)}, bf16[1024,6,64]{0,2,1:T(8,128)(2,1)S(1)}, /*index=5*/s32[]{:T(128)}) while((s32[]{:T(128)}, bf16[2,512,6,64]{1,3,2,0:T(8,128)(2,1)}, bf16[2,512,6,64]{1,3,2,0:T(8,128)(2,1)}, ...), condition=%wide.region_16.17_spmd, body=%wide.region_13.16_spmd.sunk | while | flops 830665728 | bytes 40195140 | solution.py:80
  507.3 3.4 fusion.382
  516.3 3.4 fusion.382
  520.4 16.5 %psum.54 = bf16[5376]{0:T(1024)(128)(2,1)S(1)} all-reduce(bf16[5376]{0:T(1024)(128)(2,1)S(1)} %multiply_convert_fusion.8), channel_id=1, replica_groups=mesh['grp'=4,'dp'=8] {'grp'}, use_global_device_ids=true, to_apply=%region_82.83 | all-reduce | flops 5376 | bytes 21504 | tf_op jit(solution)/shard_map/psum | solution.py:346
  541.7 19.2 %multiply_add_fusion.3 = f32[1024,384]{0,1:T(8,128)} fusion(f32[1024,384]{0,1:T(8,128)S(1)} %get-tuple-element.745, bf16[1536,384]{1,0:T(8,128)(2,1)} %reshape.423, bf16[384,1536]{1,0:T(8,128)(2,1)} %reshape.422, f32[1536]{0:T(1024)S(1)} %copy-done.146, f32[384]{0:T(512)S(1)} %copy-done.122, f32[384]{0:T(512)S(1)} %copy-done.93, ...), kind=kOutput, calls=%fused_computation.248 | convolution fusion | flops 2522873856 | bytes 5525504 | tf_op jit(solution)/shard_map/dot_general | solution.py:155
  560.9 83.4 %all-reduce.12.cloned.1.call-done = (bf16[442368]{0:T(1024)(128)(2,1)}, bf16[147456]{0:T(1024)(128)(2,1)}, bf16[589824]{0:T(1024)(128)(2,1)}, bf16[589824]{0:T(1024)(128)(2,1)}, bf16[884736]{0:T(1024)(128)(2,1)}) async-done(((bf16[442368]{0:T(1024)(128)(2,1)}, bf16[147456]{0:T(1024)(128)(2,1)}, bf16[589824]{0:T(1024)(128)(2,1)}, bf16[589824]{0:T(1024)(128)(2,1)}, bf16[884736]{0:T(1024)(128)(2,1)}), ...) | async-done | bytes 5308432 | tf_op jit(solution)/shard_map/psum | solution.py:341
  644.3 213.1 %all-reduce.13 = (f32[442368]{0:T(1024)}, f32[147456]{0:T(1024)}, f32[589824]{0:T(1024)}, f32[589824]{0:T(1024)}, f32[884736]{0:T(1024)}, /*index=5*/f32[5376]{0:T(1024)S(1)}) all-reduce(bf16[442368]{0:T(1024)(128)(2,1)} %get-tuple-element.616, ...), channel_id=2, replica_groups=mesh['grp'=4,'dp'=8] {'dp'}, use_global_device_ids=true, to_apply=%region_48.49.clone | all-reduce | flops 2659584 | bytes 15957504
  871.9 14.2 %psum.55 = f32[]{:T(128)} all-reduce(f32[]{:T(128)S(6)} %add.592), channel_id=1, replica_groups=mesh['grp'=4,'dp'=8] {'dp'}, use_global_device_ids=true, to_apply=%region_85.86 | all-reduce | flops 1 | bytes 8 | tf_op jit(solution)/shard_map/psum | solution.py:357
  (570 shorter events, 208.6 us)
Async XLA Ops:
  7.2 85.2 %copy-start.164 = (s32[4]{0:T(128)S(1)}, s32[4]{0:T(128)}, u32[]{:S(2)}) copy-start(s32[4]{0:T(128)} %param.39) | copy-start | bytes 52
  7.2 64.7 %copy-start.69 = (f32[18432]{0:T(1024)S(1)}, f32[18432]{0:T(1024)}, u32[]{:S(2)}) copy-start(f32[18432]{0:T(1024)} %param.43) | copy-start | bytes 221188
  7.2 80.1 %copy-start.64 = (bf16[1024,384]{1,0:T(8,128)(2,1)S(1)}, bf16[1024,384]{1,0:T(8,128)(2,1)}, u32[]{:S(2)}) copy-start(bf16[1024,384]{1,0:T(8,128)(2,1)} %param.37) | copy-start | bytes 2359300
  7.2 87.0 %all-gather.6.cloned.1.call-start = ((), (), s32[]{:S(2)}) async-start(), calls=%async_computation.1 | async-start | bytes 1327104 | tf_op jit(solution)/shard_map/all_gather | solution.py:283
  9.0 88.9 %all-gather.8.cloned.1.call-start = ((), (), s32[]{:S(2)}) async-start(), calls=%async_computation.2 | async-start | bytes 1327104 | tf_op jit(solution)/shard_map/all_gather | solution.py:284
  10.7 90.3 %all-gather.4.cloned.1.call-start = ((), (), s32[]{:S(2)}) async-start(), calls=%async_computation | async-start | bytes 1990656 | tf_op jit(solution)/shard_map/all_gather | solution.py:285
  12.5 631.8 %all-reduce.12.cloned.1.call-start = ((), (), s32[]{:S(2)}) async-start(), calls=%async_computation.3 | async-start | bytes 10616832 | tf_op jit(solution)/shard_map/psum | solution.py:341
  45.9 209.6 %copy-start.144 = (f32[1536]{0:T(1024)}, f32[1536]{0:T(1024)S(1)}, u32[]{:S(2)}) copy-start(f32[1536]{0:T(1024)S(1)} %slice.77) | copy-start | bytes 18436
  53.0 52.9 %copy-start.19 = (bf16[1024,384]{0,1:T(8,128)(2,1)}, bf16[1024,384]{0,1:T(8,128)(2,1)S(1)}, u32[]{:S(2)}) copy-start(bf16[1024,384]{0,1:T(8,128)(2,1)S(1)} %copy.129) | copy-start | bytes 2359300
  87.3 187.2 %copy-start.26 = (bf16[384,384]{1,0:T(8,128)(2,1)}, bf16[384,384]{1,0:T(8,128)(2,1)S(1)}, u32[]{:S(2)}) copy-start(bf16[384,384]{1,0:T(8,128)(2,1)S(1)} %reshape.421) | copy-start | bytes 884740
  93.8 72.2 %copy-start.161 = (f32[384]{0:T(512)}, f32[384]{0:T(512)S(1)}, u32[]{:S(2)}) copy-start(f32[384]{0:T(512)S(1)} %get-tuple-element.706) | copy-start | bytes 4612
  93.8 124.4 %copy-start.90 = (f32[384]{0:T(512)}, f32[384]{0:T(512)S(1)}, u32[]{:S(2)}) copy-start(f32[384]{0:T(512)S(1)} %get-tuple-element.707) | copy-start | bytes 4612
  93.8 12.2 %copy-start.142 = (f32[1152]{0:T(1024)}, f32[1152]{0:T(1024)S(1)}, u32[]{:S(2)}) copy-start(f32[1152]{0:T(1024)S(1)} %pad_maximum_fusion.2) | copy-start | bytes 13828
  94.0 12.0 %copy-start.88 = (f32[1024]{0:T(1024)}, f32[1024]{0:T(1024)S(1)}, u32[]{:S(2)}) copy-start(f32[1024]{0:T(1024)S(1)} %broadcast_multiply_fusion.13) | copy-start | bytes 12292
  94.2 11.8 %copy-start.101 = (f32[1024]{0:T(1024)}, f32[1024]{0:T(1024)S(1)}, u32[]{:S(2)}) copy-start(f32[1024]{0:T(1024)S(1)} %add_rsqrt_fusion.5) | copy-start | bytes 12292
  105.9 56.8 %copy-start.104 = (f32[384]{0:T(512)}, f32[384]{0:T(512)S(1)}, u32[]{:S(2)}) copy-start(f32[384]{0:T(512)S(1)} %get-tuple-element.705) | copy-start | bytes 4612
  105.9 60.0 %copy-start.132 = (f32[384]{0:T(512)}, f32[384]{0:T(512)S(1)}, u32[]{:S(2)}) copy-start(f32[384]{0:T(512)S(1)} %get-tuple-element.700) | copy-start | bytes 4612
  105.9 119.0 %copy-start.118 = (f32[384]{0:T(512)}, f32[384]{0:T(512)S(1)}, u32[]{:S(2)}) copy-start(f32[384]{0:T(512)S(1)} %get-tuple-element.702) | copy-start | bytes 4612
  106.0 119.0 %copy-start.155 = (f32[384]{0:T(512)}, f32[384]{0:T(512)S(1)}, u32[]{:S(2)}) copy-start(f32[384]{0:T(512)S(1)} %get-tuple-element.701) | copy-start | bytes 4612
  160.0 25.8 %copy-start.6 = (bf16[1024,6,64]{0,2,1:T(8,128)(2,1)}, bf16[1024,6,64]{0,2,1:T(8,128)(2,1)S(1)}, u32[]{:S(2)}) copy-start(bf16[1024,6,64]{0,2,1:T(8,128)(2,1)S(1)} %get-tuple-element.1201) | copy-start | bytes 2359300
  160.0 25.8 %copy-start.10 = (bf16[1024,6,64]{0,2,1:T(8,128)(2,1)}, bf16[1024,6,64]{0,2,1:T(8,128)(2,1)S(1)}, u32[]{:S(2)}) copy-start(bf16[1024,6,64]{0,2,1:T(8,128)(2,1)S(1)} %get-tuple-element.1205) | copy-start | bytes 2359300
  165.9 21.5 %copy-start.94 = (f32[2304]{0:T(1024)S(1)}, f32[2304]{0:T(1024)}, u32[]{:S(2)}) copy-start(f32[2304]{0:T(1024)} %get-tuple-element.692) | copy-start | bytes 27652
  165.9 22.1 %copy-start.143 = (f32[1152]{0:T(1024)S(1)}, f32[1152]{0:T(1024)}, u32[]{:S(2)}) copy-start(f32[1152]{0:T(1024)} %copy-done.142) | copy-start | bytes 13828
  188.1 34.0 %copy-start.120 = (f32[384]{0:T(512)}, f32[384]{0:T(512)S(1)}, u32[]{:S(2)}) copy-start(f32[384]{0:T(512)S(1)} %get-tuple-element.695) | copy-start | bytes 4612
  188.1 81.9 %copy-start.92 = (f32[384]{0:T(512)}, f32[384]{0:T(512)S(1)}, u32[]{:S(2)}) copy-start(f32[384]{0:T(512)S(1)} %get-tuple-element.696) | copy-start | bytes 4612
  188.1 81.9 %copy-start.106 = (f32[384]{0:T(512)}, f32[384]{0:T(512)S(1)}, u32[]{:S(2)}) copy-start(f32[384]{0:T(512)S(1)} %get-tuple-element.699) | copy-start | bytes 4612
  221.8 48.1 %copy-start.73 = (f32[1024]{0:T(1024)}, f32[1024]{0:T(1024)S(1)}, u32[]{:S(2)}) copy-start(f32[1024]{0:T(1024)S(1)} %broadcast_multiply_fusion.9) | copy-start | bytes 12292
  222.0 47.9 %copy-start.77 = (f32[1024]{0:T(1024)}, f32[1024]{0:T(1024)S(1)}, u32[]{:S(2)}) copy-start(f32[1024]{0:T(1024)S(1)} %add_rsqrt_fusion.1) | copy-start | bytes 12292
  225.0 30.5 %copy-start.51 = (bf16[1024,384]{0,1:T(8,128)(2,1)S(1)}, bf16[1024,384]{0,1:T(8,128)(2,1)}, u32[]{:S(2)}) copy-start(bf16[1024,384]{0,1:T(8,128)(2,1)} %copy.142) | copy-start | bytes 2359300
  225.0 30.5 %copy-start.55 = (bf16[1536,384]{1,0:T(8,128)(2,1)S(1)}, bf16[1536,384]{1,0:T(8,128)(2,1)}, u32[]{:S(2)}) copy-start(bf16[1536,384]{1,0:T(8,128)(2,1)} %reshape.423) | copy-start | bytes 3538948
  225.1 30.5 %copy-start.129 = (f32[384]{0:T(512)S(1)}, f32[384]{0:T(512)}, u32[]{:S(2)}) copy-start(f32[384]{0:T(512)} %get-tuple-element.694) | copy-start | bytes 4612
  274.5 11.2 %copy-start.12 = (bf16[2,512,6,64]{1,3,2,0:T(8,128)(2,1)S(1)}, bf16[2,512,6,64]{1,3,2,0:T(8,128)(2,1)}, u32[]{:S(2)}) copy-start(bf16[2,512,6,64]{1,3,2,0:T(8,128)(2,1)} %get-tuple-element.1206) | copy-start | bytes 2359300
  297.1 11.5 %copy-start.1 = (f32[6,512,1024]{2,1,0:T(8,128)S(1)}, f32[6,512,1024]{2,1,0:T(8,128)}, u32[]{:S(2)}) copy-start(f32[6,512,1024]{2,1,0:T(8,128)} %copy-done) | copy-start | bytes 37748740 | tf_op jit(solution)/shard_map/while
  323.7 12.0 %copy-start.1 = (f32[6,512,1024]{2,1,0:T(8,128)S(1)}, f32[6,512,1024]{2,1,0:T(8,128)}, u32[]{:S(2)}) copy-start(f32[6,512,1024]{2,1,0:T(8,128)} %copy-done) | copy-start | bytes 37748740 | tf_op jit(solution)/shard_map/while
  378.4 8.7 copy-start.7
  378.4 8.7 copy-start.11
  378.4 8.7 copy-start.13
  378.4 8.7 copy-start.68
  398.1 11.5 %copy-start.3 = (f32[6,512,1024]{2,1,0:T(8,128)S(1)}, f32[6,512,1024]{2,1,0:T(8,128)}, u32[]{:S(2)}) copy-start(f32[6,512,1024]{2,1,0:T(8,128)} %copy-done.2) | copy-start | bytes 37748740 | tf_op jit(solution)/shard_map/while
  424.2 12.0 %copy-start.3 = (f32[6,512,1024]{2,1,0:T(8,128)S(1)}, f32[6,512,1024]{2,1,0:T(8,128)}, u32[]{:S(2)}) copy-start(f32[6,512,1024]{2,1,0:T(8,128)} %copy-done.2) | copy-start | bytes 37748740 | tf_op jit(solution)/shard_map/while
  481.9 8.8 copy-start.30
  493.5 8.2 copy-start.5
  519.7 17.3 %copy-start.37 = (f32[1024,384]{0,1:T(8,128)S(1)}, f32[1024,384]{0,1:T(8,128)}, u32[]{:S(2)}) copy-start(f32[1024,384]{0,1:T(8,128)} %get-tuple-element.690) | copy-start | bytes 4718596
  519.7 21.0 %copy-start.18 = (f32[1024,384]{0,1:T(8,128)S(1)}, f32[1024,384]{0,1:T(8,128)}, u32[]{:S(2)}) copy-start(f32[1024,384]{0,1:T(8,128)} %get-tuple-element.743) | copy-start | bytes 4718596
  519.7 21.0 %copy-start.28 = (bf16[384,384]{1,0:T(8,128)(2,1)S(1)}, bf16[384,384]{1,0:T(8,128)(2,1)}, u32[]{:S(2)}) copy-start(bf16[384,384]{1,0:T(8,128)(2,1)} %copy-done.26) | copy-start | bytes 884740
  519.7 21.0 %copy-start.91 = (f32[384]{0:T(512)S(1)}, f32[384]{0:T(512)}, u32[]{:S(2)}) copy-start(f32[384]{0:T(512)} %copy-done.90) | copy-start | bytes 4612
  519.7 21.0 %copy-start.107 = (f32[384]{0:T(512)S(1)}, f32[384]{0:T(512)}, u32[]{:S(2)}) copy-start(f32[384]{0:T(512)} %copy-done.106) | copy-start | bytes 4612
  560.9 309.3 %copy-start.54 = (f32[1024,384]{0,1:T(8,128)S(1)}, f32[1024,384]{0,1:T(8,128)}, u32[]{:S(2)}) copy-start(f32[1024,384]{0,1:T(8,128)} %multiply_add_fusion.3) | copy-start | bytes 4718596
  644.3 242.6 %copy-start.126 = (f32[672]{0:T(1024)S(1)}, f32[672]{0:T(1024)}, u32[]{:S(2)}) copy-start(f32[672]{0:T(1024)} %param.47) | copy-start | bytes 8068
  644.3 242.6 %copy-start.151 = (f32[672]{0:T(1024)S(1)}, f32[672]{0:T(1024)}, u32[]{:S(2)}) copy-start(f32[672]{0:T(1024)} %param.53) | copy-start | bytes 8068
  644.3 242.6 %copy-start.152 = (f32[672]{0:T(1024)S(1)}, f32[672]{0:T(1024)}, u32[]{:S(2)}) copy-start(f32[672]{0:T(1024)} %param.59) | copy-start | bytes 8068
  644.3 243.3 %copy-start.53 = (f32[110592]{0:T(1024)S(1)}, f32[110592]{0:T(1024)}, u32[]{:S(2)}) copy-start(f32[110592]{0:T(1024)} %param.46) | copy-start | bytes 1327108
  644.3 243.3 %copy-start.65 = (f32[110592]{0:T(1024)S(1)}, f32[110592]{0:T(1024)}, u32[]{:S(2)}) copy-start(f32[110592]{0:T(1024)} %param.52) | copy-start | bytes 1327108
  644.3 243.3 %copy-start.66 = (f32[110592]{0:T(1024)S(1)}, f32[110592]{0:T(1024)}, u32[]{:S(2)}) copy-start(f32[110592]{0:T(1024)} %param.58) | copy-start | bytes 1327108
  857.5 32.6 %copy-start.58 = (f32[73728]{0:T(1024)S(1)}, f32[73728]{0:T(1024)}, u32[]{:S(2)}) copy-start(f32[73728]{0:T(1024)} %param.45) | copy-start | bytes 884740
  861.5 30.8 %copy-start.59 = (f32[73728]{0:T(1024)S(1)}, f32[73728]{0:T(1024)}, u32[]{:S(2)}) copy-start(f32[73728]{0:T(1024)} %param.44) | copy-start | bytes 884740
  871.9 20.4 %copy-start.71 = (f32[73728]{0:T(1024)S(1)}, f32[73728]{0:T(1024)}, u32[]{:S(2)}) copy-start(f32[73728]{0:T(1024)} %param.50) | copy-start | bytes 884740
  871.9 20.4 %copy-start.72 = (f32[73728]{0:T(1024)S(1)}, f32[73728]{0:T(1024)}, u32[]{:S(2)}) copy-start(f32[73728]{0:T(1024)} %param.56) | copy-start | bytes 884740
  871.9 22.5 %copy-start.70 = (f32[18432]{0:T(1024)S(1)}, f32[18432]{0:T(1024)}, u32[]{:S(2)}) copy-start(f32[18432]{0:T(1024)} %param.43) | copy-start | bytes 221188
  871.9 22.5 %copy-start.79 = (f32[18432]{0:T(1024)S(1)}, f32[18432]{0:T(1024)}, u32[]{:S(2)}) copy-start(f32[18432]{0:T(1024)} %param.49) | copy-start | bytes 221188
  871.9 22.5 %copy-start.80 = (f32[18432]{0:T(1024)S(1)}, f32[18432]{0:T(1024)}, u32[]{:S(2)}) copy-start(f32[18432]{0:T(1024)} %param.55) | copy-start | bytes 221188
  871.9 24.1 %copy-start.62 = (f32[55296]{0:T(1024)S(1)}, f32[55296]{0:T(1024)}, u32[]{:S(2)}) copy-start(f32[55296]{0:T(1024)} %param.42) | copy-start | bytes 663556
  871.9 24.1 %copy-start.75 = (f32[55296]{0:T(1024)S(1)}, f32[55296]{0:T(1024)}, u32[]{:S(2)}) copy-start(f32[55296]{0:T(1024)} %param.48) | copy-start | bytes 663556
  871.9 24.1 %copy-start.76 = (f32[55296]{0:T(1024)S(1)}, f32[55296]{0:T(1024)}, u32[]{:S(2)}) copy-start(f32[55296]{0:T(1024)} %param.54) | copy-start | bytes 663556
  (115 other events, 463.1 us)
Sparse Core Ops, SparseCore 0:
  10.3 25.5 all-gather.5
  38.1 25.1 all-gather.7
  65.5 27.3 all-gather.3
  519.9 124.3 all-reduce.11
where the time goes:
time: 913 us; the launch traced here: 906 us
  blocking collectives  305 us (33%)
  matrix products  285 us (31%)
  other arithmetic  110 us (12%)
  local copies, waits for them, and re-layouts  92.4 us (10%)
  waiting for transfers between devices  83.5 us (9%)
  between operations  28 us (3%)
    unnamed x2, blocking collectives  244 us
    psum x1, waiting for transfers between devices, per_device(): lax.psum(flat_qkv.astype(jnp.bfloat16), 'grp').astype(jnp.float32)  83.4 us
    dot_general x4, matrix products, advance(): jnp.dot(act_low, w_down, preferred_element_type=jnp.float32) + b_down  42.1 us
    dot_general x2, matrix products, advance(): jnp.dot(hidden_two, w_up, preferred_element_type=jnp.float32) + b_up  32.5 us
    dot_general x8, matrix products, times_back(): lax.dot_general(left, right, (((1,), (1,)), ((), ())), preferred_element_...  27.9 us
    dot_general x8, matrix products, block_scores(): jnp.einsum('hqk,khd->qhd', weights_low, value_rows, preferred_element_typ...  27.3 us
    dot_general x8, matrix products, times_t(): lax.dot_general(left, right, (((0,), (0,)), ((), ())), preferred_element_...  26.8 us
    dot_general x4, matrix products, block_back(): jnp.einsum('hqk,khd->qhd', score_grad, key_rows, preferred_element_type=j...  24.8 us
  transfers between devices with their start and end apart: 4, of which 1 were waited for; matrix products, arithmetic and copies ran while one was open for 5% of the time, Pallas kernels for 0%

commit v1 on v0

v1 whole, which is shorter than its diff:
```python
import functools
import math

import jax
import jax.numpy as jnp
from jax import lax
from jax.experimental import pallas as pl
from jax.experimental.pallas import tpu as pltpu
from jax.sharding import PartitionSpec as P

D = 384
HEADS = 6
FF = 1536
ROLLOUT = 2
INTERVALS = 3
ADAM_STEP = 10
HEAD_DIM = 64
NPARAM = 2659584

norm_eps = 1e-06
learn_rate = 0.05
adam_eps = 1e-08

BF = jnp.bfloat16
F32 = jnp.float32
NN = (((1,), (0,)), ((), ()))
NT = (((1,), (1,)), ((), ()))
TN = (((0,), (0,)), ((), ()))

ROWS = 256
SHIFT1, SCALE1, GATE1, SHIFT2, SCALE2, GATE2 = range(6)


def dot(left, right, dims=NN):
    return lax.dot_general(left, right, dims, preferred_element_type=F32)


def layer_norm(stream):
    centred = stream - jnp.mean(stream, axis=-1, keepdims=True)
    inverse = lax.rsqrt(jnp.mean(centred * centred, axis=-1, keepdims=True) + norm_eps)
    return (centred * inverse, inverse)


def norm_back(normed, inverse, grad_out):
    mean_grad = jnp.mean(grad_out, axis=-1, keepdims=True)
    mean_prod = jnp.mean(grad_out * normed, axis=-1, keepdims=True)
    return inverse * (grad_out - mean_grad - normed * mean_prod)


def col_sum(value):
    return jnp.sum(value, axis=0, keepdims=True)


def modulated(normed, mods, scale_row, shift_row):
    return (normed * (1.0 + mods(scale_row)) + mods(shift_row)).astype(BF)


def mod_reader(mod_ref, step):
    return lambda row: mod_ref[pl.ds(8 * step + row, 1), :]


def gelu_pair(value):
    cdf = 0.5 + 0.5 * lax.erf(value * (2.0**-0.5))
    density = jnp.exp(-0.5 * value * value) * (1.0 / math.sqrt(2.0 * math.pi))
    return (value * cdf, cdf + value * density)


def first_kernel(x_ref, mod_ref, wqkv_ref, bqkv_ref, qkv_ref):
    mods = mod_reader(mod_ref, 0)
    normed, _ = layer_norm(x_ref[...].astype(F32))
    hidden = modulated(normed, mods, SCALE1, SHIFT1)
    qkv_ref[...] = (dot(hidden, wqkv_ref[...]) + bqkv_ref[...]).astype(BF)


def middle_kernel(
    x_ref, att_ref, mod_ref, wproj_ref, wup_ref, wdown_ref, wqkv_ref,
    bproj_ref, bup_ref, bdown_ref, bqkv_ref,
    a_ref, gp_ref, act_ref, f_ref, next_ref, qkv_ref,
):
    mods = mod_reader(mod_ref, 0)
    later = mod_reader(mod_ref, 1)
    branch = dot(att_ref[...], wproj_ref[...]) + bproj_ref[...]
    a_ref[...] = branch
    middle = x_ref[...].astype(F32) + mods(GATE1) * branch
    normed, _ = layer_norm(middle)
    hidden = modulated(normed, mods, SCALE2, SHIFT2)
    upward = dot(hidden, wup_ref[...]) + bup_ref[...]
    act, slope = gelu_pair(upward)
    gp_ref[...] = slope
    act = act.astype(BF)
    act_ref[...] = act
    branch = dot(act, wdown_ref[...]) + bdown_ref[...]
    f_ref[...] = branch
    stream = middle + mods(GATE2) * branch
    next_ref[...] = stream
    normed, _ = layer_norm(stream)
    hidden = modulated(normed, later, SCALE1, SHIFT1)
    qkv_ref[...] = (dot(hidden, wqkv_ref[...]) + bqkv_ref[...]).astype(BF)


def ffn_back(
    mods, grad, branch_two, act, slope, normed, inverse, hidden, branch_one, att,
    wproj_ref, wup_ref, wdown_ref, gdown_ref, gup_ref, gproj_ref, wide_ref, narrow_ref,
    dmid_ref, datt_ref,
):
    df = (mods(GATE2) * grad).astype(BF)
    narrow_ref[pl.ds(GATE2, 1), :] += col_sum(grad * branch_two)
    narrow_ref[pl.ds(7, 1), :] += col_sum(df.astype(F32))
    gdown_ref[...] += dot(act, df, TN)
    dact = dot(df, wdown_ref[...], NT)
    du = (dact * slope).astype(BF)
    wide_ref[pl.ds(0, 1), :] += col_sum(du.astype(F32))
    gup_ref[...] += dot(hidden, du, TN)
    dh = dot(du, wup_ref[...], NT)
    narrow_ref[pl.ds(SHIFT2, 1), :] += col_sum(dh)
    narrow_ref[pl.ds(SCALE2, 1), :] += col_sum(dh * normed)
    dmid = grad + norm_back(normed, inverse, dh * (1.0 + mods(SCALE2)))
    dmid_ref[...] = dmid
    da = (mods(GATE1) * dmid).astype(BF)
    narrow_ref[pl.ds(GATE1, 1), :] += col_sum(dmid * branch_one)
    narrow_ref[pl.ds(6, 1), :] += col_sum(da.astype(F32))
    gproj_ref[...] += dot(att, da, TN)
    datt_ref[...] = dot(da, wproj_ref[...], NT).astype(BF)


def turn_kernel(
    x_ref, att_ref, cot_ref, mod_ref, wproj_ref, wup_ref, wdown_ref,
    bproj_ref, bup_ref, bdown_ref,
    out_ref, dmid_ref, datt_ref, gdown_ref, gup_ref, gproj_ref, wide_ref, narrow_ref,
):
    @pl.when(pl.program_id(0) == 0)
    def _():
        for ref in (gdown_ref, gup_ref, gproj_ref, wide_ref, narrow_ref):
            ref[...] = jnp.zeros_like(ref)

    mods = mod_reader(mod_ref, 1)
    att = att_ref[...]
    branch_one = dot(att, wproj_ref[...]) + bproj_ref[...]
    middle = x_ref[...] + mods(GATE1) * branch_one
    normed, inverse = layer_norm(middle)
    hidden = modulated(normed, mods, SCALE2, SHIFT2)
    act, slope = gelu_pair(dot(hidden, wup_ref[...]) + bup_ref[...])
    act = act.astype(BF)
    branch_two = dot(act, wdown_ref[...]) + bdown_ref[...]
    out_ref[...] = middle + mods(GATE2) * branch_two
    ffn_back(
        mods, cot_ref[...].astype(F32), branch_two, act, slope, normed, inverse, hidden,
        branch_one, att, wproj_ref, wup_ref, wdown_ref, gdown_ref, gup_ref, gproj_ref,
        wide_ref, narrow_ref, dmid_ref, datt_ref,
    )


def qkv_back(mods, stream, dmid, dqkv, wqkv_ref, gqkv_ref, narrow_ref, bias_ref):
    normed, inverse = layer_norm(stream)
    hidden = modulated(normed, mods, SCALE1, SHIFT1)
    bias_ref[pl.ds(0, 1), :] += col_sum(dqkv.astype(F32))
    gqkv_ref[...] += dot(hidden, dqkv, TN)
    dh = dot(dqkv, wqkv_ref[...], NT)
    narrow_ref[pl.ds(SHIFT1, 1), :] += col_sum(dh)
    narrow_ref[pl.ds(SCALE1, 1), :] += col_sum(dh * normed)
    return dmid + norm_back(normed, inverse, dh * (1.0 + mods(SCALE1)))


def join_kernel(
    dq_ref, dk_ref, dv_ref, x1_ref, dmid1_ref, x0_ref, a_ref, gp_ref, act_ref, f_ref, att_ref,
    mod_ref, wproj_ref, wup_ref, wdown_ref, wqkv_ref, gdown_in, gup_in, gproj_in,
    dmid_ref, datt_ref, gqkv_ref, gdown_ref, gup_ref, gproj_ref, wide_ref, narrow1_ref,
    narrow_ref, bias_ref,
):
    @pl.when(pl.program_id(0) == 0)
    def _():
        for ref in (gqkv_ref, wide_ref, narrow1_ref, narrow_ref, bias_ref):
            ref[...] = jnp.zeros_like(ref)
        gdown_ref[...] = gdown_in[...]
        gup_ref[...] = gup_in[...]
        gproj_ref[...] = gproj_in[...]

    dqkv = jnp.concatenate([dq_ref[...], dk_ref[...], dv_ref[...]], axis=1)
    grad = qkv_back(
        mod_reader(mod_ref, 1), x1_ref[...], dmid1_ref[...], dqkv, wqkv_ref, gqkv_ref,
        narrow1_ref, bias_ref,
    )
    mods = mod_reader(mod_ref, 0)
    branch_one = a_ref[...]
    middle = x0_ref[...].astype(F32) + mods(GATE1) * branch_one
    normed, inverse = layer_norm(middle)
    hidden = modulated(normed, mods, SCALE2, SHIFT2)
    ffn_back(
        mods, grad, f_ref[...], act_ref[...], gp_ref[...], normed, inverse, hidden,
        branch_one, att_ref[...], wproj_ref, wup_ref, wdown_ref, gdown_ref, gup_ref, gproj_ref,
        wide_ref, narrow_ref, dmid_ref, datt_ref,
    )


def last_kernel(
    dq_ref, dk_ref, dv_ref, x_ref, dmid_ref, mod_ref, wqkv_ref, gqkv_in,
    dx_ref, gqkv_ref, narrow_ref, bias_ref,
):
    @pl.when(pl.program_id(0) == 0)
    def _():
        narrow_ref[...] = jnp.zeros_like(narrow_ref)
        bias_ref[...] = jnp.zeros_like(bias_ref)
        gqkv_ref[...] = gqkv_in[...]

    dqkv = jnp.concatenate([dq_ref[...], dk_ref[...], dv_ref[...]], axis=1)
    dx_ref[...] = qkv_back(
        mod_reader(mod_ref, 0), x_ref[...].astype(F32), dmid_ref[...], dqkv, wqkv_ref,
        gqkv_ref, narrow_ref, bias_ref,
    )


def rows_call(kernel, name, row_args, whole_args, row_outs, whole_outs):
    length = row_args[0].shape[0]
    row_spec = lambda width: pl.BlockSpec((ROWS, width), lambda i: (i, 0))
    whole_in = lambda shape: pl.BlockSpec(shape, lambda i: (0, 0), pipeline_mode=pl.Buffered(1))
    whole_out = lambda shape: pl.BlockSpec(shape, lambda i: (0, 0))
    return pl.pallas_call(
        kernel,
        grid=(length // ROWS,),
        in_specs=[row_spec(a.shape[1]) for a in row_args] + [whole_in(a.shape) for a in whole_args],
        out_specs=[row_spec(w) for w, _ in row_outs] + [whole_out(s) for s in whole_outs],
        out_shape=[jax.ShapeDtypeStruct((length, w), t) for w, t in row_outs]
        + [jax.ShapeDtypeStruct(s, F32) for s in whole_outs],
        name=name,
    )(*row_args, *whole_args)


def head_lanes(rows):
    lane = lax.broadcasted_iota(jnp.int32, (rows, 2 * HEAD_DIM), 1)
    return (lane < HEAD_DIM, lane >= HEAD_DIM)


def turned_heads(rows_f32, out_ref):
    turned = jnp.transpose(rows_f32)
    row = lax.broadcasted_iota(jnp.int32, turned.shape, 0)
    out_ref[0] = jnp.where(row < HEAD_DIM, turned, 0.0).astype(BF)
    out_ref[1] = jnp.where(row >= HEAD_DIM, turned, 0.0).astype(BF)


score_scale = HEAD_DIM**-0.5


def attend_kernel(q_ref, k_ref, v_ref, o_ref, p_ref, vt_ref):
    @pl.when(pl.program_id(1) == 0)
    def _():
        turned_heads(v_ref[...].astype(F32), vt_ref)

    queries = q_ref[...] * BF(score_scale)
    mixed = None
    for half, lanes in enumerate(head_lanes(queries.shape[0])):
        scores = dot(k_ref[...], jnp.where(lanes, queries, BF(0)), NT)
        top = jnp.max(scores, axis=0, keepdims=True)
        weights = jnp.exp(scores - top)
        total = jnp.sum(weights, axis=0, keepdims=True)
        low = (weights * (1.0 / total)).astype(BF)
        p_ref[half] = low
        part = dot(vt_ref[half], low)
        mixed = part if mixed is None else mixed + part
    o_ref[...] = jnp.transpose(mixed).astype(BF)


def attend(qkv, block):
    length = qkv.shape[0]
    pairs = HEADS // 2
    return pl.pallas_call(
        attend_kernel,
        grid=(pairs, length // block),
        in_specs=[
            pl.BlockSpec((block, 128), lambda h, i: (i, h)),
            pl.BlockSpec((length, 128), lambda h, i: (0, pairs + h)),
            pl.BlockSpec((length, 128), lambda h, i: (0, 2 * pairs + h)),
        ],
        out_specs=[
            pl.BlockSpec((block, 128), lambda h, i: (i, h)),
            pl.BlockSpec((2, length, block), lambda h, i: (h, 0, i)),
        ],
        out_shape=[
            jax.ShapeDtypeStruct((length, D), BF),
            jax.ShapeDtypeStruct((HEADS, length, length), BF),
        ],
        scratch_shapes=[pltpu.VMEM((2, 128, length), BF)],
        name="attend",
    )(qkv, qkv, qkv)


def attend_back_kernel(
    q_ref, k_ref, v_ref, do_ref, p_ref, dq_ref, dk_ref, dv_ref, kt_ref, dk_sum, dv_sum
):
    block_id = pl.program_id(1)

    @pl.when(block_id == 0)
    def _():
        turned_heads(k_ref[...].astype(F32) * score_scale, kt_ref)
        dk_sum[...] = jnp.zeros_like(dk_sum)
        dv_sum[...] = jnp.zeros_like(dv_sum)

    queries = q_ref[...] * BF(score_scale)
    grads = do_ref[...]
    dq_turned = None
    for half, lanes in enumerate(head_lanes(queries.shape[0])):
        grad = jnp.where(lanes, grads, BF(0))
        query = jnp.where(lanes, queries, BF(0))
        low = p_ref[half]
        weight_grad = dot(v_ref[...], grad, NT)
        weights = low.astype(F32)
        delta = jnp.sum(weights * weight_grad, axis=0, keepdims=True)
        score_grad = (weights * (weight_grad - delta)).astype(BF)
        dk_sum[...] += dot(score_grad, query)
        dv_sum[...] += dot(low, grad)
        part = dot(kt_ref[half], score_grad)
        dq_turned = part if dq_turned is None else dq_turned + part
    dq_ref[...] = jnp.transpose(dq_turned).astype(BF)

    @pl.when(block_id == pl.num_programs(1) - 1)
    def _():
        dk_ref[...] = dk_sum[...].astype(BF)
        dv_ref[...] = dv_sum[...].astype(BF)


def attend_back(qkv, grads, weights, block):
    length = qkv.shape[0]
    pairs = HEADS // 2
    return pl.pallas_call(
        attend_back_kernel,
        grid=(pairs, length // block),
        in_specs=[
            pl.BlockSpec((block, 128), lambda h, i: (i, h)),
            pl.BlockSpec((length, 128), lambda h, i: (0, pairs + h)),
            pl.BlockSpec((length, 128), lambda h, i: (0, 2 * pairs + h)),
            pl.BlockSpec((block, 128), lambda h, i: (i, h)),
            pl.BlockSpec((2, length, block), lambda h, i: (h, 0, i)),
        ],
        out_specs=[
            pl.BlockSpec((block, 128), lambda h, i: (i, h)),
            pl.BlockSpec((length, 128), lambda h, i: (0, h)),
            pl.BlockSpec((length, 128), lambda h, i: (0, h)),
        ],
        out_shape=[jax.ShapeDtypeStruct((length, D), BF)] * 3,
        scratch_shapes=[
            pltpu.VMEM((2, 128, length), BF),
            pltpu.VMEM((length, 128), F32),
            pltpu.VMEM((length, 128), F32),
        ],
        name="attend_back",
    )(qkv, qkv, qkv, grads, weights)


def step_embedding(moment):
    half_width = D // 2
    freqs = jnp.exp(-math.log(10000.0) * jnp.arange(half_width, dtype=F32) / half_width)
    angles = moment[:, None] * freqs[None, :]
    return jnp.concatenate([jnp.sin(angles), jnp.cos(angles)], axis=1)


def all_conditions(group_interval, rollout_start, lead_table):
    chosen = group_interval[:, None] == jnp.arange(INTERVALS)[None, :]
    lead_rows = jnp.sum(jnp.where(chosen[:, :, None], lead_table[None], 0.0), axis=1)
    start = rollout_start.astype(F32)
    rows = [lead_rows + step_embedding(start + offset) for offset in range(ROLLOUT)]
    return jax.nn.silu(jnp.stack(rows, axis=1)).astype(BF)


def block_pass(inputs, cotangent, mods, matrices, biases):
    w_qkv, w_proj, w_up, w_down = matrices
    b_qkv, b_proj, b_up, b_down = biases
    block = inputs.shape[0]
    (qkv0,) = rows_call(
        first_kernel, "first", [inputs], [mods, w_qkv, b_qkv], [(3 * D, BF)], []
    )
    att0, p0 = attend(qkv0, block)
    a0, gp0, act0, f0, x1, qkv1 = rows_call(
        middle_kernel, "middle", [inputs, att0],
        [mods, w_proj, w_up, w_down, w_qkv, b_proj, b_up, b_down, b_qkv],
        [(D, F32), (FF, F32), (FF, BF), (D, F32), (D, F32), (3 * D, BF)], [],
    )
    att1, p1 = attend(qkv1, block)
    result, dmid1, datt1, gdown, gup, gproj, wide1, narrow1 = rows_call(
        turn_kernel, "turn", [x1, att1, cotangent],
        [mods, w_proj, w_up, w_down, b_proj, b_up, b_down],
        [(D, F32), (D, F32), (D, BF)],
        [(FF, D), (D, FF), (D, D), (8, FF), (8, D)],
    )
    dq, dk, dv = attend_back(qkv1, datt1, p1, block)
    dmid0, datt0, gqkv, gdown, gup, gproj, wide0, narrow1b, narrow0, bias1 = rows_call(
        join_kernel, "join",
        [dq, dk, dv, x1, dmid1, inputs, a0, gp0, act0, f0, att0],
        [mods, w_proj, w_up, w_down, w_qkv, gdown, gup, gproj],
        [(D, F32), (D, BF)],
        [(D, 3 * D), (FF, D), (D, FF), (D, D), (8, FF), (8, D), (8, D), (8, 3 * D)],
    )
    dq, dk, dv = attend_back(qkv0, datt0, p0, block)
    input_grad, gqkv, narrow0b, bias0 = rows_call(
        last_kernel, "last", [dq, dk, dv, inputs, dmid0], [mods, w_qkv, gqkv],
        [(D, F32)], [(D, 3 * D), (8, D), (8, 3 * D)],
    )
    narrow = jnp.stack([narrow0 + narrow0b, narrow1 + narrow1b])
    both = narrow[0] + narrow[1]
    qkv_bias = bias0[0] + bias1[0]
    branch_bias = jnp.concatenate(
        [qkv_bias[:D], qkv_bias[2 * D :], both[6], wide0[0] + wide1[0], both[7]]
    )
    dmod = narrow[:, :6].reshape(ROLLOUT, 6 * D)
    return (result, input_grad, (gqkv, gproj, gup, gdown), branch_bias, dmod)


def per_device(
    inputs,
    cotangent,
    group_interval,
    sample_counts,
    rollout_start,
    lead_table,
    *state,
):
    masters, firsts, seconds = (state[0:6], state[6:12], state[12:18])
    low = [master.astype(BF) for master in masters]
    group_index = lax.axis_index("grp")
    owner = lax.axis_index("dp")
    owners = lax.axis_size("dp")
    groups = lax.axis_size("grp")
    own_rows = D // owners
    counts = sample_counts.astype(F32)
    share = lax.dynamic_index_in_dim(groups * counts / jnp.sum(counts), group_index, keepdims=False)
    conditions = all_conditions(group_interval, rollout_start, lead_table)
    owner_columns = lax.dynamic_slice_in_dim(conditions, owner * own_rows, own_rows, axis=2)
    own_condition = lax.dynamic_index_in_dim(owner_columns, group_index, keepdims=False)

    part = dot(own_condition, low[4].reshape(own_rows, 6 * D))
    modulation = lax.psum(part, "dp")
    gathered = [lax.all_gather(low[index], "dp", axis=0, tiled=True) for index in (0, 1, 2, 3, 5)]
    matrices = (
        gathered[0].reshape(D, 3 * D),
        gathered[1].reshape(D, D),
        gathered[2].reshape(D, FF),
        gathered[3].reshape(FF, D),
    )
    bias = gathered[4].astype(F32)
    modulation = modulation + bias[4 * D + FF :][None]
    mods = jnp.pad(modulation.reshape(ROLLOUT, 6, D), ((0, 0), (0, 2), (0, 0))).reshape(-1, D)
    b_qkv = jnp.concatenate([bias[:D], jnp.zeros((D,), F32), bias[D : 2 * D]])
    biases = (
        b_qkv[None],
        bias[2 * D : 3 * D][None],
        bias[3 * D : 3 * D + FF][None],
        bias[3 * D + FF : 4 * D + FF][None],
    )
    result, input_grad, grads, branch_bias, dmod = block_pass(
        inputs, cotangent, mods, matrices, biases
    )

    dmod = lax.psum(dmod * share, "dp")
    dmod_all = lax.all_gather(dmod, "grp")
    vectors = jnp.concatenate([branch_bias * share, jnp.zeros((6 * D,), F32)])
    bias_sum = lax.psum(vectors, ("grp", "dp"))
    bias_sum = bias_sum + jnp.pad(jnp.sum(dmod_all, axis=(0, 1)), (4 * D + FF, 0))
    bias_grad = lax.dynamic_slice_in_dim(bias_sum, owner * masters[5].shape[0], masters[5].shape[0])
    ada_grad = jnp.einsum(
        "gsr,gsc->rc", owner_columns.astype(F32), dmod_all, precision=lax.Precision.HIGHEST
    )
    shares = []
    for grad in grads:
        summed = lax.psum((grad * share).astype(BF).reshape(-1), "grp").astype(F32)
        shares.append(lax.psum_scatter(summed, "dp", scatter_dimension=0, tiled=True))
    shares = shares + [ada_grad.reshape(-1), bias_grad]

    local_square = sum((jnp.sum(piece * piece) for piece in shares))
    grad_norm = jnp.sqrt(lax.psum(local_square, "dp"))
    limit = math.sqrt(NPARAM)
    clip_scale = limit / jnp.maximum(grad_norm, limit)
    correction = 1.0 - 0.5**ADAM_STEP
    decays = [0.1, 0.1, 0.1, 0.1, 0.1, 0.0]
    news = []
    first_news = []
    second_news = []
    copies = []
    for index_w in range(6):
        clipped = shares[index_w] * clip_scale
        first_new = 0.5 * firsts[index_w] + 0.5 * clipped
        second_new = 0.5 * seconds[index_w] + 0.5 * clipped * clipped
        update = first_new / correction / (jnp.sqrt(second_new / correction) + adam_eps)
        new_master = masters[index_w] - learn_rate * (update + decays[index_w] * masters[index_w])
        news.append(new_master)
        first_news.append(first_new)
        second_news.append(second_new)
        copies.append(new_master.astype(BF))
    return (result, input_grad, grad_norm, *news, *first_news, *second_news, *copies)


def solution(mesh):
    rows = P(("grp", "dp"), None)
    return jax.shard_map(
        per_device,
        mesh=mesh,
        in_specs=(rows, rows, P(), P(), P(), P(), *[P("dp")] * 18),
        out_specs=(rows, rows, P(), *[P("dp")] * 24),
        check_vma=False,
    )
```

time: 913 us -> 562 us (0.62)
  matrix products: 285 us -> 1.26 us
  Pallas kernels: 0 us -> 134 us
  other arithmetic: 110 us -> 30.3 us
  local copies, waits for them, and re-layouts: 92.4 us -> 21 us
  waiting for transfers between devices: 83.5 us -> 50.1 us
  blocking collectives: 305 us -> 294 us
    dot_general x66 -> x2, matrix products: 285 us -> 1.26 us  [the longest x1 1.12 us: per_device(): jnp.einsum('gsr,gsc->rc', owner_columns.astype(F32), dmod_all, precision=...]
    pallas_call x0 -> x9, Pallas kernels: none -> 134 us  [the longest x5 67.4 us: rows_call(): pl.pallas_call(kernel, grid=(length // ROWS,), in_specs=[row_spec(a.shape...]
    unnamed x2, blocking collectives: 244 us -> 176 us
    reduce_sum x29 -> x3, other arithmetic: 53.1 us -> 0.72 us  [the longest x1 0.6 us: per_device(): jnp.sum(counts)]
    psum x2 -> x3, blocking collectives: 30.7 us -> 79.5 us  [the longest x1 39.3 us: per_device(): bias_sum = lax.psum(vectors, ('grp', 'dp'))]
    psum x1, waiting for transfers between devices: 83.4 us -> 50.1 us  [per_device(): summed = lax.psum((grad * share).astype(BF).reshape(-1), 'grp').astype(F32)]
    convert_element_type x20 -> x18, other arithmetic: 37.8 us -> 19.7 us  [the longest x6 9.89 us: per_device(): copies.append(new_master.astype(BF))]
    unnamed x365 -> x69, local copies, waits for them, and re-layouts: 18.6 us -> 1.02 us
  transfers between devices with their start and end apart: 4 -> 3, of which waited for: 1 -> 1; matrix products, arithmetic and copies ran while one was open for 5% -> 4% of each run, Pallas kernels for 0% -> 3%
where the time goes in v1:
time: 562 us; the launch traced here: 555 us
  blocking collectives  294 us (52%)
  Pallas kernels  134 us (24%)
  waiting for transfers between devices  50.1 us (9%)
  other arithmetic  30.3 us (5%)
  between operations  23.2 us (4%)
  local copies, waits for them, and re-layouts  21 us (4%)
    unnamed x2, blocking collectives  176 us
    pallas_call x5, Pallas kernels, rows_call(): pl.pallas_call(kernel, grid=(length // ROWS,), in_specs=[row_spec(a.shape...  67.4 us
    psum x1, waiting for transfers between devices, per_device(): summed = lax.psum((grad * share).astype(BF).reshape(-1), 'grp').astype(F32)  50.1 us
    psum x1, blocking collectives, per_device(): bias_sum = lax.psum(vectors, ('grp', 'dp'))  39.3 us
    pallas_call x2, Pallas kernels, attend_back(): pl.pallas_call(attend_back_kernel, grid=(pairs, length // block), in_spec...  39.2 us
    all_gather x2, blocking collectives, per_device(): lax.all_gather(low[index], 'dp', axis=0, tiled=True)  30.3 us
    pallas_call x2, Pallas kernels, attend(): pl.pallas_call(attend_kernel, grid=(pairs, length // block), in_specs=[pl...  27.6 us
    psum x1, blocking collectives, per_device(): modulation = lax.psum(part, 'dp')  26.1 us
  transfers between devices with their start and end apart: 3, of which 1 were waited for; matrix products, arithmetic and copies ran while one was open for 4% of the time, Pallas kernels for 3%

profile of v1, /device:TPU:0, one launch (start us, length us, event | category | flops | bytes accessed | tf_op | source)
XLA Modules:
  0.0 554.6 jit_solution(15185697671063821197)
XLA Ops:
  7.3 1.7 convert_element_type.84
  9.1 1.6 convert_element_type.85
  10.8 0.7 broadcast_add_fusion.1
  11.5 0.7 convert_element_type.77
  12.1 0.7 iota_compare_fusion
  12.8 1.0 convert_element_type.79
  13.8 0.3 reshape.289
  14.2 0.1 fusion.8
  14.5 0.1 fusion.15
  14.7 0.6 fusion.33
  16.0 0.2 dynamic-update-slice
  16.2 30.5 %all-reduce.3 = bf16[5376]{0:T(1024)(128)(2,1)S(1)} all-reduce(bf16[5376]{0:T(1024)(128)(2,1)S(1)} %dynamic-update-slice), channel_id=1, replica_groups=mesh['grp'=4,'dp'=8] {'dp'}, use_global_device_ids=true, to_apply=%add.3 | all-reduce | flops 5376 | bytes 21504
  46.7 26.1 %psum.56 = f32[2,2304]{1,0:T(2,128)S(1)} all-reduce(f32[2,2304]{1,0:T(2,128)S(1)} %fusion.15), channel_id=1, replica_groups=mesh['grp'=4,'dp'=8] {'dp'}, use_global_device_ids=true, to_apply=%region_1.2 | all-reduce | flops 4608 | bytes 36864 | tf_op jit(solution)/shard_map/psum | solution.py:429
  72.9 0.6 broadcast_in_dim.49.bqkv_ref
  73.5 15.9 %all_gather.22 = bf16[442368]{0:T(1024)(128)(2,1)S(1)} all-gather(bf16[55296]{0:T(1024)(128)(2,1)S(1)} %convert_element_type.82), channel_id=1, replica_groups=mesh['grp'=4,'dp'=8] {'dp'}, dimensions={0}, use_global_device_ids=true | all-gather | bytes 995328 | tf_op jit(solution)/shard_map/all_gather | solution.py:430
  89.4 1.9 reshape.292.wqkv_ref
  91.3 0.6 pad_bitcast_fusion.mod_ref
  91.9 5.3 first.1.q_ref.k_ref.v_ref
  97.2 13.8 %attend.2 = (bf16[1024,384]{1,0:T(8,128)(2,1)}, bf16[6,1024,1024]{2,1,0:T(8,128)(2,1)}) custom-call(bf16[1024,1152]{1,0:T(8,128)(2,1)} %first.1.q_ref.k_ref.v_ref, bf16[1024,1152]{1,0:T(8,128)(2,1)} %first.1.q_ref.k_ref.v_ref, bf16[1024,1152]{1,0:T(8,128)(2,1)} %first.1.q_ref.k_ref.v_ref), custom_call_target="tpu_custom_call" | custom-call | tf_op jit(solution)/shard_map/attend/pallas_call | solution.py:265
  111.1 0.6 broadcast_in_dim.50.bproj_ref
  111.6 0.6 broadcast_in_dim.52.bdown_ref
  112.2 0.6 broadcast_in_dim.51.bup_ref
  112.8 14.4 %all_gather.23 = bf16[147456]{0:T(1024)(128)(2,1)S(1)} all-gather(bf16[18432]{0:T(1024)(128)(2,1)S(1)} %convert_element_type.83), channel_id=1, replica_groups=mesh['grp'=4,'dp'=8] {'dp'}, dimensions={0}, use_global_device_ids=true | all-gather | bytes 331776 | tf_op jit(solution)/shard_map/all_gather | solution.py:430
  127.2 0.9 reshape.293.wproj_ref
  128.1 0.6 convert_reduce_fusion
  128.7 0.6 multiply_divide_fusion
  129.3 0.6 dynamic_slice.16
  129.9 3.5 reshape.294.wup_ref
  133.4 3.1 reshape.295.wdown_ref
  136.5 12.3 %middle.1 = (f32[1024,384]{1,0:T(8,128)}, f32[1024,1536]{1,0:T(8,128)}, bf16[1024,1536]{1,0:T(8,128)(2,1)}, f32[1024,384]{1,0:T(8,128)}, f32[1024,384]{1,0:T(8,128)}, /*index=5*/bf16[1024,1152]{1,0:T(8,128)(2,1)}) custom-call(bf16[1024,384]{1,0:T(8,128)(2,1)} %x_ref.5, bf16[1024,384]{1,0:T(8,128)(2,1)} %get-tuple-element.65.att_ref, ...), custom_call_target="tpu_custom_call" | custom-call | tf_op jit(solution)/shard_map/middle/pallas_call | solution.py:217
  148.8 13.8 %attend.3 = (bf16[1024,384]{1,0:T(8,128)(2,1)}, bf16[6,1024,1024]{2,1,0:T(8,128)(2,1)}) custom-call(bf16[1024,1152]{1,0:T(8,128)(2,1)} %get-tuple-element.67.q_ref.k_ref.v_ref, bf16[1024,1152]{1,0:T(8,128)(2,1)} %get-tuple-element.67.q_ref.k_ref.v_ref, bf16[1024,1152]{1,0:T(8,128)(2,1)} %get-tuple-element.67.q_ref.k_ref.v_ref), custom_call_target="tpu_custom_call" | custom-call | tf_op jit(solution)/shard_map/attend/pallas_call | solution.py:265
  162.6 18.4 %turn.1 = (f32[1024,384]{1,0:T(8,128)}, f32[1024,384]{1,0:T(8,128)}, bf16[1024,384]{1,0:T(8,128)(2,1)}, f32[1536,384]{1,0:T(8,128)}, f32[384,1536]{1,0:T(8,128)}...) custom-call(f32[1024,384]{1,0:T(8,128)} %get-tuple-element.66.x_ref.x1_ref, ...), custom_call_target="tpu_custom_call" | custom-call | tf_op jit(solution)/shard_map/turn/pallas_call | solution.py:217
  181.0 19.6 %attend_back.2 = (bf16[1024,384]{1,0:T(8,128)(2,1)}, bf16[1024,384]{1,0:T(8,128)(2,1)}, bf16[1024,384]{1,0:T(8,128)(2,1)}) custom-call(bf16[1024,1152]{1,0:T(8,128)(2,1)} %get-tuple-element.67.q_ref.k_ref.v_ref, bf16[1024,1152]{1,0:T(8,128)(2,1)} %get-tuple-element.67.q_ref.k_ref.v_ref, bf16[1024,1152]{1,0:T(8,128)(2,1)} %get-tuple-element.67.q_ref.k_ref.v_ref, ...), custom_call_target="tpu_custom_call" | custom-call | tf_op jit(solution)/shard_map/attend_back/pallas_call | solution.py:323
  200.6 23.1 %join.1 = (f32[1024,384]{1,0:T(8,128)}, bf16[1024,384]{1,0:T(8,128)(2,1)}, f32[384,1152]{1,0:T(8,128)}, f32[1536,384]{1,0:T(8,128)}, f32[384,1536]{1,0:T(8,128)}...) custom-call(bf16[1024,384]{1,0:T(8,128)(2,1)} %get-tuple-element.72.dq, ...), custom_call_target="tpu_custom_call" | custom-call | tf_op jit(solution)/shard_map/join/pallas_call | solution.py:217
  223.7 19.6 %attend_back.3 = (bf16[1024,384]{1,0:T(8,128)(2,1)}, bf16[1024,384]{1,0:T(8,128)(2,1)}, bf16[1024,384]{1,0:T(8,128)(2,1)}) custom-call(bf16[1024,1152]{1,0:T(8,128)(2,1)} %first.1.q_ref.k_ref.v_ref, bf16[1024,1152]{1,0:T(8,128)(2,1)} %first.1.q_ref.k_ref.v_ref, bf16[1024,1152]{1,0:T(8,128)(2,1)} %first.1.q_ref.k_ref.v_ref, ...), custom_call_target="tpu_custom_call" | custom-call | tf_op jit(solution)/shard_map/attend_back/pallas_call | solution.py:323
  243.3 8.3 %last.1 = (f32[1024,384]{1,0:T(8,128)}, f32[384,1152]{1,0:T(8,128)}, f32[8,384]{1,0:T(8,128)}, f32[8,1152]{1,0:T(8,128)}) custom-call(bf16[1024,384]{1,0:T(8,128)(2,1)} %get-tuple-element.85.dq_ref, bf16[1024,384]{1,0:T(8,128)(2,1)} %get-tuple-element.86.dk_ref, bf16[1024,384]{1,0:T(8,128)(2,1)} %get-tuple-element.87.dv_ref, bf16[1024,384]{1,0:T(8,128)(2,1)} %x_ref.5, ...), custom_call_target="tpu_custom_call" | custom-call | tf_op jit(solution)/shard_map/last/pallas_call | solution.py:217
  251.6 2.4 multiply_convert_fusion.2
  254.0 1.8 reshape.296
  255.8 0.8 multiply_convert_fusion.1
  256.7 2.4 reshape.298
  259.1 0.8 multiply_convert_fusion
  259.9 1.6 reshape.299
  261.5 0.7 multiply_convert_fusion.3
  262.2 0.9 reshape.297
  265.0 0.8 slice_add_fusion
  265.9 0.8 add_reduce_fusion
  266.8 0.7 broadcast_multiply_fusion.1
  267.5 0.7 fusion.6
  268.2 39.3 %psum.62 = f32[5376]{0:T(1024)S(1)} all-reduce(f32[5376]{0:T(1024)S(1)} %concatenate.45), channel_id=1, replica_groups=mesh['grp'=4,'dp'=8] {'grp','dp'}, use_global_device_ids=true, to_apply=%region_17.18 | all-reduce | flops 5376 | bytes 43008 | tf_op jit(solution)/shard_map/psum | solution.py:454
  307.5 50.1 %all-reduce.13.cloned.1.call-done = (bf16[442368]{0:T(1024)(128)(2,1)}, bf16[147456]{0:T(1024)(128)(2,1)}, bf16[589824]{0:T(1024)(128)(2,1)}, bf16[589824]{0:T(1024)(128)(2,1)}) async-done(((bf16[442368]{0:T(1024)(128)(2,1)}, bf16[147456]{0:T(1024)(128)(2,1)}, bf16[589824]{0:T(1024)(128)(2,1)}, bf16[589824]{0:T(1024)(128)(2,1)}), (bf16[442368]{0:T(1024)(128)(2,1)}, bf16[147456]{0:T(1024)(128)(2,1)}, ...) | async-done | bytes 3538960 | tf_op jit(solution)/shard_map/psum | solution.py:462
  357.6 145.6 %all-reduce.14 = (f32[442368]{0:T(1024)S(1)}, f32[147456]{0:T(1024)}, f32[589824]{0:T(1024)}, f32[589824]{0:T(1024)}, f32[1,2,2304]{2,1,0:T(2,128)S(1)}) all-reduce(bf16[442368]{0:T(1024)(128)(2,1)} %get-tuple-element.112, bf16[147456]{0:T(1024)(128)(2,1)} %get-tuple-element.113, ...), channel_id=2, replica_groups=mesh['grp'=4,'dp'=8] {'dp'}, use_global_device_ids=true, to_apply=%region_4.5.clone | all-reduce | flops 1774080 | bytes 10653696
  503.2 8.5 %all_gather.27 = f32[4,2,2304]{2,1,0:T(2,128)S(1)} all-gather(f32[1,2,2304]{2,1,0:T(2,128)S(1)} %get-tuple-element.111), channel_id=1, replica_groups=mesh['grp'=4,'dp'=8] {'grp'}, dimensions={0}, use_global_device_ids=true | all-gather | bytes 92160 | tf_op jit(solution)/shard_map/all_gather | solution.py:452
  511.8 1.1 multiply_reduce_fusion
  512.9 1.5 multiply_reduce_fusion.4
  514.4 0.7 multiply_reduce_fusion.3
  516.4 1.7 multiply_reduce_fusion.1
  520.1 0.7 multiply_reduce_fusion.5
  521.4 14.1 %psum.63 = f32[]{:T(128)} all-reduce(f32[]{:T(128)S(6)} %add.221), channel_id=1, replica_groups=mesh['grp'=4,'dp'=8] {'dp'}, use_global_device_ids=true, to_apply=%region_20.21 | all-reduce | flops 1 | bytes 8 | tf_op jit(solution)/shard_map/psum | solution.py:467
  536.4 2.1 fusion.23
  538.7 2.2 fusion.25
  540.9 1.6 fusion.27
  542.5 1.9 fusion.29
  544.5 0.6 fusion.19
  545.1 1.4 fusion.21
  (100 shorter events, 0.9 us)
Async XLA Ops:
  7.2 7.5 %copy-start.29 = (u32[32]{0:T(128)S(1)}, u32[32]{0:T(128)}, u32[]{:S(2)}) copy-start(u32[32]{0:T(128)} %constant.112) | copy-start | bytes 388
  7.2 6.9 %copy-start.26 = (f32[3,384]{1,0:T(4,128)S(1)}, f32[3,384]{1,0:T(4,128)}, u32[]{:S(2)}) copy-start(f32[3,384]{1,0:T(4,128)} %param.29) | copy-start | bytes 13828
  7.2 7.5 %copy-start.21 = (f32[672]{0:T(1024)S(1)}, f32[672]{0:T(1024)}, u32[]{:S(2)}) copy-start(f32[672]{0:T(1024)} %param.35) | copy-start | bytes 8068
  7.2 66.2 %copy-start.5 = (f32[55296]{0:T(1024)S(1)}, f32[55296]{0:T(1024)}, u32[]{:S(2)}) copy-start(f32[55296]{0:T(1024)} %param.30) | copy-start | bytes 663556
  7.2 122.7 %all-gather.3.cloned.1.call-start = ((), (), s32[]{:S(2)}) async-start(), calls=%async_computation | async-start | bytes 1327104 | tf_op jit(solution)/shard_map/all_gather | solution.py:430
  9.0 124.4 %all-gather.5.cloned.1.call-start = ((), (), s32[]{:S(2)}) async-start(), calls=%async_computation.1 | async-start | bytes 1327104 | tf_op jit(solution)/shard_map/all_gather | solution.py:430
  10.7 346.9 %all-reduce.13.cloned.1.call-start = ((), (), s32[]{:S(2)}) async-start(), calls=%async_computation.2 | async-start | bytes 7077888 | tf_op jit(solution)/shard_map/psum | solution.py:462
  97.2 15.6 %copy-start.10 = (f32[18432]{0:T(1024)S(1)}, f32[18432]{0:T(1024)}, u32[]{:S(2)}) copy-start(f32[18432]{0:T(1024)} %param.31) | copy-start | bytes 221188
  97.2 30.8 %copy-start.30 = (s32[4]{0:T(128)S(1)}, s32[4]{0:T(128)}, u32[]{:S(2)}) copy-start(s32[4]{0:T(128)} %param.27) | copy-start | bytes 52
  251.6 4.2 copy-start.1
  256.7 2.4 copy-start
  259.9 1.6 copy-start.7
  263.0 2.8 copy-start.22
  263.0 2.9 copy-start.23
  263.0 2.9 copy-start.24
  263.0 2.9 copy-start.25
  503.2 33.0 %copy-start.18 = (f32[442368]{0:T(1024)}, f32[442368]{0:T(1024)S(1)}, u32[]{:S(2)}) copy-start(f32[442368]{0:T(1024)S(1)} %get-tuple-element.107) | copy-start | bytes 5308420
  503.2 33.1 %copy-start.3 = (f32[73728]{0:T(1024)S(1)}, f32[73728]{0:T(1024)}, u32[]{:S(2)}) copy-start(f32[73728]{0:T(1024)} %param.33) | copy-start | bytes 884740
  503.2 33.1 %copy-start.12 = (f32[73728]{0:T(1024)S(1)}, f32[73728]{0:T(1024)}, u32[]{:S(2)}) copy-start(f32[73728]{0:T(1024)} %param.39) | copy-start | bytes 884740
  503.2 33.1 %copy-start.13 = (f32[73728]{0:T(1024)S(1)}, f32[73728]{0:T(1024)}, u32[]{:S(2)}) copy-start(f32[73728]{0:T(1024)} %param.45) | copy-start | bytes 884740
  536.3 2.3 copy-start.4
  536.3 2.3 copy-start.14
  536.3 2.3 copy-start.15
  536.4 4.5 copy-start.11
  536.4 4.5 copy-start.19
  536.4 4.5 copy-start.20
  538.6 3.9 copy-start.6
  538.6 3.9 copy-start.16
  538.6 3.9 copy-start.17
  538.6 5.8 %copy-start.27 = (f32[672]{0:T(1024)S(1)}, f32[672]{0:T(1024)}, u32[]{:S(2)}) copy-start(f32[672]{0:T(1024)} %param.41) | copy-start | bytes 8068
  538.6 5.8 %copy-start.28 = (f32[672]{0:T(1024)S(1)}, f32[672]{0:T(1024)}, u32[]{:S(2)}) copy-start(f32[672]{0:T(1024)} %param.47) | copy-start | bytes 8068
  538.7 6.4 %copy-start.2 = (f32[110592]{0:T(1024)S(1)}, f32[110592]{0:T(1024)}, u32[]{:S(2)}) copy-start(f32[110592]{0:T(1024)} %param.34) | copy-start | bytes 1327108
  538.7 6.4 %copy-start.8 = (f32[110592]{0:T(1024)S(1)}, f32[110592]{0:T(1024)}, u32[]{:S(2)}) copy-start(f32[110592]{0:T(1024)} %param.40) | copy-start | bytes 1327108
  538.7 6.4 %copy-start.9 = (f32[110592]{0:T(1024)S(1)}, f32[110592]{0:T(1024)}, u32[]{:S(2)}) copy-start(f32[110592]{0:T(1024)} %param.46) | copy-start | bytes 1327108
Sparse Core Ops, SparseCore 0:
  10.3 25.5 all-gather.2
  38.1 22.5 all-gather.4
  263.2 94.3 all-reduce.12

commit v2 on v1

v2 whole, which is shorter than its diff:
```python
import functools
import math

import jax
import jax.numpy as jnp
from jax import lax
from jax.experimental import pallas as pl
from jax.experimental.pallas import tpu as pltpu
from jax.sharding import PartitionSpec as P

D = 384
HEADS = 6
FF = 1536
ROLLOUT = 2
INTERVALS = 3
ADAM_STEP = 10
HEAD_DIM = 64
NPARAM = 2659584

norm_eps = 1e-06
learn_rate = 0.05
adam_eps = 1e-08

BF = jnp.bfloat16
F32 = jnp.float32
NN = (((1,), (0,)), ((), ()))
NT = (((1,), (1,)), ((), ()))
TN = (((0,), (0,)), ((), ()))

ROWS = 256
SLAB = 48
PART = 384
ROW_SHARE = 6
ROW_BQKV, ROW_BPROJ, ROW_BUP, ROW_BDOWN = 16, 19, 20, 24
SHIFT1, SCALE1, GATE1, SHIFT2, SCALE2, GATE2 = range(6)


def dot(left, right, dims=NN):
    return lax.dot_general(left, right, dims, preferred_element_type=F32)


def layer_norm(stream):
    centred = stream - jnp.mean(stream, axis=-1, keepdims=True)
    inverse = lax.rsqrt(jnp.mean(centred * centred, axis=-1, keepdims=True) + norm_eps)
    return (centred * inverse, inverse)


def norm_back(normed, inverse, grad_out):
    mean_grad = jnp.mean(grad_out, axis=-1, keepdims=True)
    mean_prod = jnp.mean(grad_out * normed, axis=-1, keepdims=True)
    return inverse * (grad_out - mean_grad - normed * mean_prod)


def col_sum(value):
    return jnp.sum(value, axis=0, keepdims=True)


def modulated(normed, mods, scale_row, shift_row):
    return (normed * (1.0 + mods(scale_row)) + mods(shift_row)).astype(BF)


def mod_reader(mod_ref, step):
    return lambda row: mod_ref[pl.ds(8 * step + row, 1), :]


def gelu_pair(value):
    cdf = 0.5 + 0.5 * lax.erf(value * (2.0**-0.5))
    density = jnp.exp(-0.5 * value * value) * (1.0 / math.sqrt(2.0 * math.pi))
    return (value * cdf, cdf + value * density)


def side_by_side(ref, first, count):
    return jnp.concatenate([ref[row : row + 1, :] for row in range(first, first + count)], axis=1)


def first_kernel(x_ref, rows_ref, wa_ref, qkv_ref):
    mods = mod_reader(rows_ref, 0)
    normed, _ = layer_norm(x_ref[...].astype(F32))
    hidden = modulated(normed, mods, SCALE1, SHIFT1)
    qkv = dot(hidden, wa_ref[:, : 3 * D]) + side_by_side(rows_ref, ROW_BQKV, 3)
    qkv_ref[...] = qkv.astype(BF)


def middle_kernel(
    x_ref, att_ref, rows_ref, wa_ref, wup_ref, wdown_ref,
    a_ref, gp_ref, act_ref, f_ref, next_ref, qkv_ref,
):
    mods = mod_reader(rows_ref, 0)
    later = mod_reader(rows_ref, 1)
    branch = dot(att_ref[...], wa_ref[:, 3 * D :]) + mods(ROW_BPROJ)
    a_ref[...] = branch
    middle = x_ref[...].astype(F32) + mods(GATE1) * branch
    normed, _ = layer_norm(middle)
    hidden = modulated(normed, mods, SCALE2, SHIFT2)
    upward = dot(hidden, wup_ref[...]) + side_by_side(rows_ref, ROW_BUP, 4)
    act, slope = gelu_pair(upward)
    gp_ref[...] = slope
    act = act.astype(BF)
    act_ref[...] = act
    branch = dot(act, wdown_ref[...]) + mods(ROW_BDOWN)
    f_ref[...] = branch
    stream = middle + mods(GATE2) * branch
    next_ref[...] = stream
    normed, _ = layer_norm(stream)
    hidden = modulated(normed, later, SCALE1, SHIFT1)
    qkv = dot(hidden, wa_ref[:, : 3 * D]) + side_by_side(rows_ref, ROW_BQKV, 3)
    qkv_ref[...] = qkv.astype(BF)


def ffn_back(
    mods, grad, branch_two, act, slope, normed, inverse, hidden, branch_one, att,
    wa_ref, wup_ref, wdown_ref, gdown_ref, gup_ref, gproj_ref, wide_ref, narrow_ref,
    dmid_ref, datt_ref,
):
    df = (mods(GATE2) * grad).astype(BF)
    narrow_ref[pl.ds(GATE2, 1), :] += col_sum(grad * branch_two)
    narrow_ref[pl.ds(7, 1), :] += col_sum(df.astype(F32))
    gdown_ref[...] += dot(act, df, TN)
    dact = dot(df, wdown_ref[...], NT)
    du = (dact * slope).astype(BF)
    wide_ref[pl.ds(0, 1), :] += col_sum(du.astype(F32))
    gup_ref[...] += dot(hidden, du, TN)
    dh = dot(du, wup_ref[...], NT)
    narrow_ref[pl.ds(SHIFT2, 1), :] += col_sum(dh)
    narrow_ref[pl.ds(SCALE2, 1), :] += col_sum(dh * normed)
    dmid = grad + norm_back(normed, inverse, dh * (1.0 + mods(SCALE2)))
    dmid_ref[...] = dmid
    da = (mods(GATE1) * dmid).astype(BF)
    narrow_ref[pl.ds(GATE1, 1), :] += col_sum(dmid * branch_one)
    narrow_ref[pl.ds(6, 1), :] += col_sum(da.astype(F32))
    gproj_ref[...] += dot(att, da, TN)
    datt_ref[...] = dot(da, wa_ref[:, 3 * D :], NT).astype(BF)


def turn_kernel(
    x_ref, att_ref, cot_ref, rows_ref, wa_ref, wup_ref, wdown_ref,
    out_ref, dmid_ref, datt_ref, gdown_ref, gup_ref, gproj_ref, wide_ref, narrow_ref,
):
    @pl.when(pl.program_id(0) == 0)
    def _():
        for ref in (gdown_ref, gup_ref, gproj_ref, wide_ref, narrow_ref):
            ref[...] = jnp.zeros_like(ref)

    mods = mod_reader(rows_ref, 1)
    shared = mod_reader(rows_ref, 0)
    att = att_ref[...]
    branch_one = dot(att, wa_ref[:, 3 * D :]) + shared(ROW_BPROJ)
    middle = x_ref[...] + mods(GATE1) * branch_one
    normed, inverse = layer_norm(middle)
    hidden = modulated(normed, mods, SCALE2, SHIFT2)
    upward = dot(hidden, wup_ref[...]) + side_by_side(rows_ref, ROW_BUP, 4)
    act, slope = gelu_pair(upward)
    act = act.astype(BF)
    branch_two = dot(act, wdown_ref[...]) + shared(ROW_BDOWN)
    out_ref[...] = middle + mods(GATE2) * branch_two
    ffn_back(
        mods, cot_ref[...].astype(F32), branch_two, act, slope, normed, inverse, hidden,
        branch_one, att, wa_ref, wup_ref, wdown_ref, gdown_ref, gup_ref, gproj_ref,
        wide_ref, narrow_ref, dmid_ref, datt_ref,
    )


def qkv_back(mods, stream, dmid, dqkv, wa_ref, gqkv_ref, narrow_ref, bias_ref):
    normed, inverse = layer_norm(stream)
    hidden = modulated(normed, mods, SCALE1, SHIFT1)
    bias_ref[pl.ds(0, 1), :] += col_sum(dqkv.astype(F32))
    gqkv_ref[...] += dot(hidden, dqkv, TN)
    dh = dot(dqkv, wa_ref[:, : 3 * D], NT)
    narrow_ref[pl.ds(SHIFT1, 1), :] += col_sum(dh)
    narrow_ref[pl.ds(SCALE1, 1), :] += col_sum(dh * normed)
    return dmid + norm_back(normed, inverse, dh * (1.0 + mods(SCALE1)))


def join_kernel(
    dq_ref, dk_ref, dv_ref, x1_ref, dmid1_ref, x0_ref, a_ref, gp_ref, act_ref, f_ref, att_ref,
    rows_ref, wa_ref, wup_ref, wdown_ref, gproj_in, gdown_in, gup_in,
    dmid_ref, datt_ref, gqkv_ref, gproj_ref, wide_ref, narrow1_ref, narrow_ref, bias_ref,
    up_blocks, down_blocks,
    gdown_sum, gup_sum, gdown_before, gup_before, sems,
):
    before = [
        pltpu.make_async_copy(gdown_in, gdown_before, sems.at[0]),
        pltpu.make_async_copy(gup_in, gup_before, sems.at[1]),
    ]

    @pl.when(pl.program_id(0) == 0)
    def _():
        for copy in before:
            copy.start()
        for ref in (gqkv_ref, wide_ref, narrow1_ref, narrow_ref, bias_ref, gdown_sum, gup_sum):
            ref[...] = jnp.zeros_like(ref)
        gproj_ref[...] = gproj_in[...]

    dqkv = jnp.concatenate([dq_ref[...], dk_ref[...], dv_ref[...]], axis=1)
    grad = qkv_back(
        mod_reader(rows_ref, 1), x1_ref[...], dmid1_ref[...], dqkv, wa_ref, gqkv_ref,
        narrow1_ref, bias_ref,
    )
    mods = mod_reader(rows_ref, 0)
    branch_one = a_ref[...]
    middle = x0_ref[...].astype(F32) + mods(GATE1) * branch_one
    normed, inverse = layer_norm(middle)
    hidden = modulated(normed, mods, SCALE2, SHIFT2)
    ffn_back(
        mods, grad, f_ref[...], act_ref[...], gp_ref[...], normed, inverse, hidden,
        branch_one, att_ref[...], wa_ref, wup_ref, wdown_ref, gdown_sum, gup_sum, gproj_ref,
        wide_ref, narrow_ref, dmid_ref, datt_ref,
    )

    @pl.when(pl.program_id(0) == pl.num_programs(0) - 1)
    def _():
        for copy in before:
            copy.wait()
        share = rows_ref[ROW_SHARE : ROW_SHARE + 1, :]
        for d in range(8):
            for g in range(4):
                rows, columns = (slice(SLAB * d, SLAB * (d + 1)), slice(PART * g, PART * (g + 1)))
                up_blocks[d, g] = ((gup_sum[rows, columns] + gup_before[rows, columns]) * share).astype(BF)
                first = SLAB * (4 * d + g)
                rows = slice(first, first + SLAB)
                down_blocks[d, g] = ((gdown_sum[rows, :] + gdown_before[rows, :]) * share).astype(BF)


def last_kernel(
    dq_ref, dk_ref, dv_ref, x_ref, dmid_ref, rows_ref, wa_ref, gqkv_in, gproj_in,
    wide1, narrow1, wide0, narrow1b, narrow0, bias1,
    dx_ref, vec_ref, qkv_blocks, gqkv_ref, narrow_ref, bias_ref,
):
    @pl.when(pl.program_id(0) == 0)
    def _():
        narrow_ref[...] = jnp.zeros_like(narrow_ref)
        bias_ref[...] = jnp.zeros_like(bias_ref)
        gqkv_ref[...] = gqkv_in[...]

    dqkv = jnp.concatenate([dq_ref[...], dk_ref[...], dv_ref[...]], axis=1)
    dx_ref[...] = qkv_back(
        mod_reader(rows_ref, 0), x_ref[...].astype(F32), dmid_ref[...], dqkv, wa_ref,
        gqkv_ref, narrow_ref, bias_ref,
    )

    @pl.when(pl.program_id(0) == pl.num_programs(0) - 1)
    def _():
        share = rows_ref[ROW_SHARE : ROW_SHARE + 1, :]
        for d in range(8):
            rows = slice(SLAB * d, SLAB * (d + 1))
            for g in range(3):
                qkv_blocks[d, g] = (gqkv_ref[rows, PART * g : PART * (g + 1)] * share).astype(BF)
            qkv_blocks[d, 3] = (gproj_in[rows, :] * share).astype(BF)

        def put(first, value):
            for j in range(value.shape[1] // 128):
                vec_ref[first + j : first + j + 1, :] = value[:, 128 * j : 128 * j + 128] * share[:, 0:128]

        qkv_bias = bias_ref[0:1, :] + bias1[0:1, :]
        put(0, qkv_bias[:, :D])
        put(3, qkv_bias[:, 2 * D :])
        put(6, narrow0[6:7, :] + narrow1[6:7, :])
        put(9, wide0[0:1, :] + wide1[0:1, :])
        put(21, narrow0[7:8, :] + narrow1[7:8, :])
        for r in range(6):
            put(24 + 3 * r, narrow0[r : r + 1, :] + narrow_ref[r : r + 1, :])
            put(42 + 3 * r, narrow1[r : r + 1, :] + narrow1b[r : r + 1, :])
        vec_ref[60:64, :] = jnp.zeros((4, 128), F32)


def rows_call(kernel, name, row_args, whole_args, row_outs, whole_outs, far_args=(), scratch=()):
    length = row_args[0].shape[0]
    row_spec = lambda width: pl.BlockSpec((ROWS, width), lambda i: (i, 0))
    fixed = lambda shape: (lambda i: (0,) * len(shape))
    whole_in = lambda shape: pl.BlockSpec(shape, fixed(shape), pipeline_mode=pl.Buffered(1))
    whole_out = lambda shape: pl.BlockSpec(shape, fixed(shape))
    return pl.pallas_call(
        kernel,
        grid=(length // ROWS,),
        in_specs=[row_spec(a.shape[1]) for a in row_args]
        + [whole_in(a.shape) for a in whole_args]
        + [pl.BlockSpec(memory_space=pl.ANY) for _ in far_args],
        out_specs=[row_spec(w) for w, _ in row_outs] + [whole_out(s) for s, _ in whole_outs],
        out_shape=[jax.ShapeDtypeStruct((length, w), t) for w, t in row_outs]
        + [jax.ShapeDtypeStruct(s, t) for s, t in whole_outs],
        scratch_shapes=list(scratch),
        name=name,
    )(*row_args, *whole_args, *far_args)


def head_lanes(rows):
    lane = lax.broadcasted_iota(jnp.int32, (rows, 2 * HEAD_DIM), 1)
    return (lane < HEAD_DIM, lane >= HEAD_DIM)


def turned_heads(rows_f32, out_ref):
    turned = jnp.transpose(rows_f32)
    row = lax.broadcasted_iota(jnp.int32, turned.shape, 0)
    out_ref[0] = jnp.where(row < HEAD_DIM, turned, 0.0).astype(BF)
    out_ref[1] = jnp.where(row >= HEAD_DIM, turned, 0.0).astype(BF)


score_scale = HEAD_DIM**-0.5


def attend_kernel(q_ref, k_ref, v_ref, o_ref, p_ref, vt_ref):
    @pl.when(pl.program_id(1) == 0)
    def _():
        turned_heads(v_ref[...].astype(F32), vt_ref)

    queries = q_ref[...] * BF(score_scale)
    mixed = None
    for half, lanes in enumerate(head_lanes(queries.shape[0])):
        scores = dot(k_ref[...], jnp.where(lanes, queries, BF(0)), NT)
        top = jnp.max(scores, axis=0, keepdims=True)
        weights = jnp.exp(scores - top)
        total = jnp.sum(weights, axis=0, keepdims=True)
        low = (weights * (1.0 / total)).astype(BF)
        p_ref[half] = low
        part = dot(vt_ref[half], low)
        mixed = part if mixed is None else mixed + part
    o_ref[...] = jnp.transpose(mixed).astype(BF)


def attend(qkv, block):
    length = qkv.shape[0]
    pairs = HEADS // 2
    return pl.pallas_call(
        attend_kernel,
        grid=(pairs, length // block),
        in_specs=[
            pl.BlockSpec((block, 128), lambda h, i: (i, h)),
            pl.BlockSpec((length, 128), lambda h, i: (0, pairs + h)),
            pl.BlockSpec((length, 128), lambda h, i: (0, 2 * pairs + h)),
        ],
        out_specs=[
            pl.BlockSpec((block, 128), lambda h, i: (i, h)),
            pl.BlockSpec((2, length, block), lambda h, i: (h, 0, i)),
        ],
        out_shape=[
            jax.ShapeDtypeStruct((length, D), BF),
            jax.ShapeDtypeStruct((HEADS, length, length), BF),
        ],
        scratch_shapes=[pltpu.VMEM((2, 128, length), BF)],
        name="attend",
    )(qkv, qkv, qkv)


def attend_back_kernel(
    q_ref, k_ref, v_ref, do_ref, p_ref, dq_ref, dk_ref, dv_ref, kt_ref, dk_sum, dv_sum
):
    block_id = pl.program_id(1)

    @pl.when(block_id == 0)
    def _():
        turned_heads(k_ref[...].astype(F32) * score_scale, kt_ref)
        dk_sum[...] = jnp.zeros_like(dk_sum)
        dv_sum[...] = jnp.zeros_like(dv_sum)

    queries = q_ref[...] * BF(score_scale)
    grads = do_ref[...]
    dq_turned = None
    for half, lanes in enumerate(head_lanes(queries.shape[0])):
        grad = jnp.where(lanes, grads, BF(0))
        query = jnp.where(lanes, queries, BF(0))
        low = p_ref[half]
        weight_grad = dot(v_ref[...], grad, NT)
        weights = low.astype(F32)
        delta = jnp.sum(weights * weight_grad, axis=0, keepdims=True)
        score_grad = (weights * (weight_grad - delta)).astype(BF)
        dk_sum[...] += dot(score_grad, query)
        dv_sum[...] += dot(low, grad)
        part = dot(kt_ref[half], score_grad)
        dq_turned = part if dq_turned is None else dq_turned + part
    dq_ref[...] = jnp.transpose(dq_turned).astype(BF)

    @pl.when(block_id == pl.num_programs(1) - 1)
    def _():
        dk_ref[...] = dk_sum[...].astype(BF)
        dv_ref[...] = dv_sum[...].astype(BF)


def attend_back(qkv, grads, weights, block):
    length = qkv.shape[0]
    pairs = HEADS // 2
    return pl.pallas_call(
        attend_back_kernel,
        grid=(pairs, length // block),
        in_specs=[
            pl.BlockSpec((block, 128), lambda h, i: (i, h)),
            pl.BlockSpec((length, 128), lambda h, i: (0, pairs + h)),
            pl.BlockSpec((length, 128), lambda h, i: (0, 2 * pairs + h)),
            pl.BlockSpec((block, 128), lambda h, i: (i, h)),
            pl.BlockSpec((2, length, block), lambda h, i: (h, 0, i)),
        ],
        out_specs=[
            pl.BlockSpec((block, 128), lambda h, i: (i, h)),
            pl.BlockSpec((length, 128), lambda h, i: (0, h)),
            pl.BlockSpec((length, 128), lambda h, i: (0, h)),
        ],
        out_shape=[jax.ShapeDtypeStruct((length, D), BF)] * 3,
        scratch_shapes=[
            pltpu.VMEM((2, 128, length), BF),
            pltpu.VMEM((length, 128), F32),
            pltpu.VMEM((length, 128), F32),
        ],
        name="attend_back",
    )(qkv, qkv, qkv, grads, weights)


MESH_ID = pl.DeviceIdType.MESH
GROUPS = 4
LAYERS = 4
UNITS = 3


class Place:
    def __init__(self):
        self.grp = lax.axis_index("grp")
        self.dp = lax.axis_index("dp")
        self.z = self.dp // 2
        self.core = self.dp % 2

    def sibling(self):
        return (self.grp, 2 * self.z + 1 - self.core)

    def along_grp(self, step):
        return (lax.rem(self.grp + step, GROUPS), self.dp)

    def along_z(self, step):
        return (self.grp, 2 * lax.rem(self.z + step, LAYERS) + self.core)

    def across(self, step):
        return (self.grp, 2 * lax.rem(self.z + step, LAYERS) + 1 - self.core)


def greet(peers):
    barrier = pltpu.get_barrier_semaphore()
    for peer in peers:
        pl.semaphore_signal(barrier, inc=1, device_id=peer, device_id_type=MESH_ID)
    return lambda: pl.semaphore_wait(barrier, len(peers))


def send(src, dst, send_sem, recv_sem, peer):
    copy = pltpu.make_async_remote_copy(
        src_ref=src, dst_ref=dst, send_sem=send_sem, recv_sem=recv_sem,
        device_id=peer, device_id_type=MESH_ID,
    )
    copy.start()
    return copy


def condition_rows(moments, intervals, lead_ref):
    shape = (8, D)
    row = lax.broadcasted_iota(jnp.int32, shape, 0)
    lane = lax.broadcasted_iota(jnp.int32, shape, 1)
    moment = jnp.zeros(shape, F32)
    chosen = jnp.zeros(shape, jnp.int32)
    for index, (value, interval) in enumerate(zip(moments, intervals)):
        moment = jnp.where(row == index, value.astype(F32), moment)
        chosen = jnp.where(row == index, interval, chosen)
    lead = jnp.zeros(shape, F32)
    for choice in range(INTERVALS):
        picked = jnp.broadcast_to(lead_ref[choice : choice + 1, :], shape)
        lead = jnp.where(chosen == choice, picked, lead)
    half_width = D // 2
    place = jnp.where(lane < half_width, lane, lane - half_width).astype(F32)
    angles = moment * jnp.exp(place * (-math.log(10000.0) / half_width))
    wave = jnp.where(lane < half_width, jnp.sin(angles), jnp.cos(angles))
    condition = lead + wave
    return (condition / (1.0 + jnp.exp(-condition))).astype(BF).astype(F32)


def part_of(unit, ref, grp, *owner):
    if unit == 2:
        return ref.at[(*owner, grp)]
    return ref.at[(*owner, slice(None), pl.ds(pl.multiple_of(PART * grp, 128), PART))]


def gather_kernel(
    start_ref, interval_ref, counts_ref, lead_ref, qkv_ref, proj_ref, up_ref, down_ref, ada_ref,
    bias_ref,
    wa_ref, wu_ref, wd_ref, rows_ref,
    slab_a, slab_u, slab_d, cond_t, part_own, part_sib, part_z, bias_slot, bias_full,
    z_send, z_recv, x_send, x_recv, s_send, s_recv, own_sem, m_send, m_recv,
):
    at = Place()
    steps = range(1, 4)
    ready = greet(
        [at.sibling()] + [at.along_grp(k) for k in steps] + [at.along_z(k) for k in steps]
    )
    slabs = (slab_a, slab_u, slab_d)
    wholes = (wa_ref, wu_ref, wd_ref)
    sends = []
    from_z = {}
    from_sib = {}

    def launch(unit):
        slab, whole = (slabs[unit], wholes[unit])
        for k in steps:
            copy = send(
                part_of(unit, slab, at.grp), part_of(unit, whole, at.grp, at.dp),
                z_send.at[unit, k - 1], z_recv.at[unit, k - 1], at.along_z(k),
            )
            from_z[unit, k] = copy
            sends.append(copy)
        copy = send(slab, whole.at[at.dp], s_send.at[unit, 0], s_recv.at[unit, 0], at.sibling())
        from_sib[unit, 0] = copy
        sends.append(copy)
        own = pltpu.make_async_copy(slab, whole.at[at.dp], own_sem.at[unit])
        own.start()
        return own

    for j in range(9):
        slab_a[:, 128 * j : 128 * j + 128] = qkv_ref[pl.ds(j, SLAB, stride=9), :].astype(BF)
    for j in range(3):
        slab_a[:, 128 * (9 + j) : 128 * (10 + j)] = proj_ref[pl.ds(j, SLAB, stride=3), :].astype(BF)
    ready()
    owns = [launch(0)]

    start = start_ref[at.grp]
    interval = interval_ref[at.grp]
    cond_t[...] = jnp.transpose(
        condition_rows([start + s for s in range(ROLLOUT)], [interval] * ROLLOUT, lead_ref)
    )
    own_cond = cond_t[pl.ds(pl.multiple_of(SLAB * at.dp, 8), SLAB), :]
    columns = [jnp.broadcast_to(own_cond[:, s : s + 1], (SLAB, 128)) for s in range(ROLLOUT)]
    for j in range(18):
        rows = ada_ref[pl.ds(j, SLAB, stride=18), :].astype(BF).astype(F32)
        for s in range(ROLLOUT):
            part_own[18 * s + j : 18 * s + j + 1, :] = col_sum(rows * columns[s])
    part_own[36:40, :] = jnp.zeros((4, 128), F32)
    lane = lax.broadcasted_iota(jnp.int32, (8, 128), 1)
    shift = lax.rem(32 * at.dp, 128)
    turned = pltpu.roll(bias_ref[...].astype(BF).astype(F32), shift, axis=1)
    above = pltpu.roll(turned, 1, axis=0)
    bias_slot[at.z, at.core] = jnp.where(lane >= shift, turned, above)
    part_copy = send(part_own, part_sib, m_send.at[0], m_recv.at[0], at.sibling())
    bias_copy = send(
        bias_slot.at[at.z, at.core], bias_slot.at[at.z, at.core], m_send.at[1], m_recv.at[1],
        at.sibling(),
    )
    sends += [part_copy, bias_copy]

    for j in range(12):
        slab_u[:, 128 * j : 128 * j + 128] = up_ref[pl.ds(j, SLAB, stride=12), :].astype(BF)
    owns.append(launch(1))
    for g in range(GROUPS):
        for j in range(3):
            slab_d[g, :, 128 * j : 128 * j + 128] = down_ref[
                pl.ds(3 * SLAB * g + j, SLAB, stride=3), :
            ].astype(BF)
    owns.append(launch(2))

    part_copy.wait_recv()
    bias_copy.wait_recv()
    part_z[at.z] = part_own[...] + part_sib[...]
    small = []
    for k in steps:
        small.append(
            send(part_z.at[at.z], part_z.at[at.z], m_send.at[1 + k], m_recv.at[1 + k], at.along_z(k))
        )
        small.append(
            send(
                bias_slot.at[at.z], bias_slot.at[at.z], m_send.at[4 + k], m_recv.at[4 + k],
                at.along_z(k),
            )
        )
    sends += small

    from_grp = {}
    for unit in range(UNITS):
        whole = wholes[unit]
        for k in steps:
            from_z[unit, k].wait_recv()
            owner = 2 * lax.rem(at.z + LAYERS - k, LAYERS) + at.core
            for m in steps:
                part = part_of(unit, whole, at.grp, owner)
                copy = send(
                    part, part, x_send.at[unit, k - 1, m - 1], x_recv.at[unit, k - 1, m - 1],
                    at.along_grp(m),
                )
                from_grp[unit, k, m] = copy
                sends.append(copy)

    for copy in small:
        copy.wait_recv()
    total = part_z[0] + part_z[1] + part_z[2] + part_z[3]
    bias_full[...] = jnp.zeros_like(bias_full)
    for d in range(2 * LAYERS):
        first = 672 * d // 128
        bias_full[first : first + 7, :] += bias_slot[d // 2, d % 2, 0:7, :]
    counts = [counts_ref[g].astype(F32) for g in range(GROUPS)]
    own_count = counts_ref[at.grp].astype(F32)
    share = jnp.full((1, D), GROUPS * own_count) / jnp.full((1, D), sum(counts[1:], counts[0]))

    def put(row, value):
        rows_ref[row : row + 1, :] = value

    def joined(first):
        return jnp.concatenate([bias_full[first + j : first + j + 1, :] for j in range(3)], axis=1)

    for s in range(ROLLOUT):
        for r in range(6):
            mod = jnp.concatenate(
                [total[18 * s + 3 * r + j : 18 * s + 3 * r + j + 1, :] for j in range(3)], axis=1
            )
            put(8 * s + r, mod + joined(24 + 3 * r))
        put(8 * s + 6, share)
        put(8 * s + 7, share)
    put(ROW_BQKV, joined(0))
    put(ROW_BQKV + 1, jnp.zeros((1, D), F32))
    put(ROW_BQKV + 2, joined(3))
    put(ROW_BPROJ, joined(6))
    for j in range(4):
        put(ROW_BUP + j, joined(9 + 3 * j))
    put(ROW_BDOWN, joined(21))
    rows_ref[25:32, :] = jnp.zeros((7, D), F32)

    for unit in range(UNITS):
        whole = wholes[unit]
        for k in steps:
            for m in steps:
                from_grp[unit, k, m].wait_recv()
            owner = 2 * lax.rem(at.z + LAYERS - k, LAYERS) + at.core
            copy = send(
                whole.at[owner], whole.at[owner], s_send.at[unit, k], s_recv.at[unit, k],
                at.sibling(),
            )
            from_sib[unit, k] = copy
            sends.append(copy)
    for copy in from_sib.values():
        copy.wait_recv()
    for own in owns:
        own.wait()
    for copy in sends:
        copy.wait_send()


def gather(start, interval, counts, lead, masters):
    qkv, proj, up, down, ada, bias = masters
    smem = pl.BlockSpec(memory_space=pltpu.SMEM)
    vmem = pl.BlockSpec(memory_space=pltpu.VMEM)
    hbm = pl.BlockSpec(memory_space=pl.ANY)
    dma = pltpu.SemaphoreType.DMA
    wa, wu, wd, rows = pl.pallas_call(
        gather_kernel,
        in_specs=[smem] * 3 + [vmem] * 7,
        out_specs=[hbm, hbm, hbm, vmem],
        out_shape=[
            jax.ShapeDtypeStruct((8, SLAB, FF), BF),
            jax.ShapeDtypeStruct((8, SLAB, FF), BF),
            jax.ShapeDtypeStruct((8, GROUPS, SLAB, PART), BF),
            jax.ShapeDtypeStruct((32, D), F32),
        ],
        scratch_shapes=[
            pltpu.VMEM((SLAB, FF), BF),
            pltpu.VMEM((SLAB, FF), BF),
            pltpu.VMEM((GROUPS, SLAB, PART), BF),
            pltpu.VMEM((D, 8), F32),
            pltpu.VMEM((40, 128), F32),
            pltpu.VMEM((40, 128), F32),
            pltpu.VMEM((LAYERS, 40, 128), F32),
            pltpu.VMEM((LAYERS, 2, 8, 128), F32),
            pltpu.VMEM((48, 128), F32),
            dma((UNITS, 3)), dma((UNITS, 3)), dma((UNITS, 3, 3)), dma((UNITS, 3, 3)),
            dma((UNITS, 4)), dma((UNITS, 4)), dma((UNITS,)), dma((8,)), dma((8,)),
        ],
        compiler_params=pltpu.CompilerParams(collective_id=0, has_side_effects=True),
        name="gather",
    )(
        start, interval, counts, lead, *(m.reshape(-1, 128) for m in (qkv, proj, up, down, ada)),
        jnp.pad(bias, (0, 1024 - bias.shape[0])).reshape(8, 128),
    )
    return (wa.reshape(D, FF), wu.reshape(D, FF), wd.reshape(FF, D), rows)


def reduce_kernel(
    start_ref, interval_ref, lead_ref, vec_ref, ga_ref, gu_ref, gd_ref,
    piece_ref, ada_ref, bias_ref, square_ref,
    own, got_s, sum_s, got_x, sum_x, got_z, pieces, cond_t,
    vec_s, vec_z, vec_g, square_own, square_d, square_g,
    own_sem, s_send, s_recv, x_send, x_recv, z_send, z_recv, a_send, a_recv,
    v_send, v_recv, q_send, q_recv,
):
    at = Place()
    steps = range(1, 4)
    ready = greet(
        [at.sibling()]
        + [at.along_grp(k) for k in steps]
        + [at.along_z(k) for k in steps]
        + [at.across(k) for k in steps]
    )
    grads = (ga_ref, gu_ref, gd_ref)
    sends = []
    owns = []
    for unit in range(UNITS):
        copy = pltpu.make_async_copy(grads[unit].at[:, at.core], own.at[unit], own_sem.at[unit])
        copy.start()
        owns.append(copy)
    ready()
    vec_copy = send(vec_ref, vec_s, v_send.at[0], v_recv.at[0], at.sibling())
    from_sib = [
        send(
            grads[unit].at[:, 1 - at.core], got_s.at[unit], s_send.at[unit], s_recv.at[unit],
            at.sibling(),
        )
        for unit in range(UNITS)
    ]
    sends += [vec_copy] + from_sib
    moments = [start_ref[g] + s for g in range(GROUPS) for s in range(ROLLOUT)]
    intervals = [interval_ref[g] for g in range(GROUPS) for s in range(ROLLOUT)]
    cond_t[...] = jnp.transpose(condition_rows(moments, intervals, lead_ref))

    vec_copy.wait_recv()
    vec_z[at.z] = vec_ref[...] + vec_s[...]
    vec_from_z = [
        send(vec_z.at[at.z], vec_z.at[at.z], v_send.at[k], v_recv.at[k], at.along_z(k))
        for k in steps
    ]
    sends += vec_from_z

    from_grp = {}
    for unit in range(UNITS):
        owns[unit].wait()
        from_sib[unit].wait_recv()

        def add_pair(z, carry):
            for g in range(GROUPS):
                sum_s[unit, z, g] = (
                    own[unit, z, g].astype(F32) + got_s[unit, z, g].astype(F32)
                ).astype(BF)
            return carry

        lax.fori_loop(0, LAYERS, add_pair, 0)
        for k in steps:
            peer = at.along_grp(k)
            copy = send(
                sum_s.at[unit, :, peer[0]], got_x.at[unit, k - 1], x_send.at[unit, k - 1],
                x_recv.at[unit, k - 1], peer,
            )
            from_grp[unit, k] = copy
            sends.append(copy)

    for copy in vec_from_z:
        copy.wait_recv()
    vec_g[at.grp] = vec_z[0] + vec_z[1] + vec_z[2] + vec_z[3]
    vec_from_grp = [
        send(vec_g.at[at.grp], vec_g.at[at.grp], v_send.at[3 + k], v_recv.at[3 + k], at.along_grp(k))
        for k in steps
    ]
    sends += vec_from_grp

    from_z = {}
    for unit in range(UNITS):
        for k in steps:
            from_grp[unit, k].wait_recv()

        def add_four(z, carry):
            value = sum_s[unit, z, at.grp].astype(F32)
            for k in range(3):
                value = value + got_x[unit, k, z].astype(F32)
            sum_x[unit, z] = value.astype(BF)
            return carry

        lax.fori_loop(0, LAYERS, add_four, 0)
        for k in steps:
            peer = at.along_z(k)
            copy = send(
                sum_x.at[unit, lax.rem(at.z + k, LAYERS)], got_z.at[unit, k - 1],
                z_send.at[unit, k - 1], z_recv.at[unit, k - 1], peer,
            )
            from_z[unit, k] = copy
            sends.append(copy)

    for copy in vec_from_grp:
        copy.wait_recv()
    own_cond = cond_t[pl.ds(pl.multiple_of(SLAB * at.dp, 8), SLAB), :]
    columns = [jnp.broadcast_to(own_cond[:, k : k + 1], (SLAB, 128)) for k in range(8)]

    def ada_tile(j, square):
        tile = jnp.zeros((SLAB, 128), F32)
        for g in range(GROUPS):
            for s in range(ROLLOUT):
                tile = tile + columns[ROLLOUT * g + s] * vec_g[g, pl.ds(24 + 18 * s + j, 1), :]
        ada_ref[pl.ds(j, SLAB, stride=18), :] = tile
        return square + col_sum(tile * tile)

    ada_square = lax.fori_loop(0, 18, ada_tile, jnp.zeros((1, 128), F32))
    vec_sum = vec_g[0] + vec_g[1] + vec_g[2] + vec_g[3]
    bias_ref[0:24, :] = vec_sum[0:24]
    bias_ref[24:42, :] = vec_sum[24:42] + vec_sum[42:60]
    bias_ref[42:48, :] = jnp.zeros((6, 128), F32)

    square = 0.25 * ada_square
    from_gather = []
    for unit in range(UNITS):
        for k in steps:
            from_z[unit, k].wait_recv()
        value = sum_x[unit, at.z].astype(F32)
        for k in range(3):
            value = value + got_z[unit, k].astype(F32)
        value = value.astype(BF)
        pieces[unit, at.grp] = value
        for k in steps:
            copy = send(
                pieces.at[unit, at.grp], pieces.at[unit, at.grp], a_send.at[unit, k - 1],
                a_recv.at[unit, k - 1], at.along_grp(k),
            )
            from_gather.append(copy)
            sends.append(copy)
        wide = value.astype(F32)
        wide = col_sum(wide * wide)
        square = square + wide[:, 0:128] + wide[:, 128:256] + wide[:, 256:384]

    square_d[at.dp] = jnp.broadcast_to(square, (8, 128))
    squares = [send(
        square_d.at[at.dp], square_d.at[at.dp], q_send.at[0], q_recv.at[0], at.sibling()
    )]
    for k in steps:
        for index, peer in ((k, at.along_z(k)), (3 + k, at.across(k))):
            squares.append(send(
                square_d.at[at.dp], square_d.at[at.dp], q_send.at[index], q_recv.at[index], peer
            ))
    for copy in squares:
        copy.wait_recv()
    total = square_d[0]
    for d in range(1, 2 * LAYERS):
        total = total + square_d[d]
    square_g[at.grp] = total
    final = [
        send(square_g.at[at.grp], square_g.at[at.grp], q_send.at[6 + k], q_recv.at[6 + k],
             at.along_grp(k))
        for k in steps
    ]
    sends += squares + final
    for copy in final:
        copy.wait_recv()
    bias_sum = bias_ref[...]
    bias_square = col_sum(bias_sum * bias_sum)
    total = square_g[0] + square_g[1] + square_g[2] + square_g[3] + bias_square
    square_ref[...] = jnp.broadcast_to(jnp.sum(total, axis=1, keepdims=True), (8, 128))

    for copy in from_gather:
        copy.wait_recv()
    piece_ref[...] = pieces[...]
    for copy in sends:
        copy.wait_send()


def reduce(start, interval, lead, vec, grads):
    smem = pl.BlockSpec(memory_space=pltpu.SMEM)
    vmem = pl.BlockSpec(memory_space=pltpu.VMEM)
    hbm = pl.BlockSpec(memory_space=pl.ANY)
    dma = pltpu.SemaphoreType.DMA
    slab = (LAYERS, GROUPS, SLAB, PART)
    piece = (SLAB, PART)
    return pl.pallas_call(
        reduce_kernel,
        in_specs=[smem, smem, vmem, vmem, hbm, hbm, hbm],
        out_specs=[vmem] * 4,
        out_shape=[
            jax.ShapeDtypeStruct((UNITS, GROUPS, *piece), BF),
            jax.ShapeDtypeStruct((18 * SLAB, 128), F32),
            jax.ShapeDtypeStruct((48, 128), F32),
            jax.ShapeDtypeStruct((8, 128), F32),
        ],
        scratch_shapes=[
            pltpu.VMEM((UNITS, *slab), BF),
            pltpu.VMEM((UNITS, *slab), BF),
            pltpu.VMEM((UNITS, *slab), BF),
            pltpu.VMEM((UNITS, 3, LAYERS, *piece), BF),
            pltpu.VMEM((UNITS, LAYERS, *piece), BF),
            pltpu.VMEM((UNITS, 3, *piece), BF),
            pltpu.VMEM((UNITS, GROUPS, *piece), BF),
            pltpu.VMEM((D, 8), F32),
            pltpu.VMEM((64, 128), F32),
            pltpu.VMEM((LAYERS, 64, 128), F32),
            pltpu.VMEM((GROUPS, 64, 128), F32),
            pltpu.VMEM((8, 128), F32),
            pltpu.VMEM((8, 8, 128), F32),
            pltpu.VMEM((GROUPS, 8, 128), F32),
            dma((UNITS,)), dma((UNITS,)), dma((UNITS,)),
            dma((UNITS, 3)), dma((UNITS, 3)), dma((UNITS, 3)), dma((UNITS, 3)),
            dma((UNITS, 3)), dma((UNITS, 3)), dma((7,)), dma((7,)), dma((10,)), dma((10,)),
        ],
        compiler_params=pltpu.CompilerParams(collective_id=1, has_side_effects=True),
        name="reduce",
    )(start, interval, lead, vec, *grads)


correction = 1.0 - 0.5**ADAM_STEP
grad_limit = math.sqrt(NPARAM)


def adam(master, first, second, clipped, decay):
    first_new = 0.5 * first + 0.5 * clipped
    second_new = 0.5 * second + 0.5 * clipped * clipped
    update = first_new / correction / (jnp.sqrt(second_new / correction) + adam_eps)
    return (master - learn_rate * (update + decay * master), first_new, second_new)


def adam_kernel(*refs):
    piece_ref, ada_ref, square_ref = refs[:3]
    masters, firsts, seconds = (refs[3:8], refs[8:13], refs[13:18])
    news, first_news, second_news, copies = (refs[18:23], refs[23:28], refs[28:33], refs[33:38])
    flats = refs[38:42]
    norm = jnp.sqrt(square_ref[0:1, :])
    clip = grad_limit / jnp.maximum(norm, grad_limit)
    qkv, proj, up, down = flats
    for g in range(3):
        for j in range(3):
            qkv[pl.ds(3 * g + j, SLAB, stride=9), :] = piece_ref[0, g, :, 128 * j : 128 * j + 128].astype(F32)
    for j in range(3):
        proj[pl.ds(j, SLAB, stride=3), :] = piece_ref[0, 3, :, 128 * j : 128 * j + 128].astype(F32)
    for g in range(GROUPS):
        for j in range(3):
            up[pl.ds(3 * g + j, SLAB, stride=12), :] = piece_ref[1, g, :, 128 * j : 128 * j + 128].astype(F32)
            down[pl.ds(3 * SLAB * g + j, SLAB, stride=3), :] = piece_ref[2, g, :, 128 * j : 128 * j + 128].astype(F32)
    for index, grad in enumerate((qkv, proj, up, down, ada_ref)):
        def chunk(i, carry):
            rows = pl.ds(pl.multiple_of(16 * i, 16), 16)
            new, first, second = adam(
                masters[index][rows, :], firsts[index][rows, :], seconds[index][rows, :],
                grad[rows, :] * clip, 0.1,
            )
            news[index][rows, :] = new
            first_news[index][rows, :] = first
            second_news[index][rows, :] = second
            copies[index][rows, :] = new.astype(BF)
            return carry

        lax.fori_loop(0, grad.shape[0] // 16, chunk, 0, unroll=3)


def update(pieces, ada, square, masters, firsts, seconds):
    flat = lambda arrays: [a.reshape(-1, 128) for a in arrays[:5]]
    masters, firsts, seconds = (flat(masters), flat(firsts), flat(seconds))
    vmem = pl.BlockSpec(memory_space=pltpu.VMEM)
    shapes = [m.shape for m in masters]
    outs = [jax.ShapeDtypeStruct(s, F32) for s in shapes] * 3
    outs += [jax.ShapeDtypeStruct(s, BF) for s in shapes]
    results = pl.pallas_call(
        adam_kernel,
        in_specs=[vmem] * 18,
        out_specs=[vmem] * 20,
        out_shape=outs,
        scratch_shapes=[pltpu.VMEM(s, F32) for s in shapes[:4]],
        name="adam",
    )(pieces, ada, square, *masters, *firsts, *seconds)
    results = [r.reshape(-1) for r in results]
    return (results[0:5], results[5:10], results[10:15], results[15:20])


def step_embedding(moment):
    half_width = D // 2
    freqs = jnp.exp(-math.log(10000.0) * jnp.arange(half_width, dtype=F32) / half_width)
    angles = moment[:, None] * freqs[None, :]
    return jnp.concatenate([jnp.sin(angles), jnp.cos(angles)], axis=1)


def all_conditions(group_interval, rollout_start, lead_table):
    chosen = group_interval[:, None] == jnp.arange(INTERVALS)[None, :]
    lead_rows = jnp.sum(jnp.where(chosen[:, :, None], lead_table[None], 0.0), axis=1)
    start = rollout_start.astype(F32)
    rows = [lead_rows + step_embedding(start + offset) for offset in range(ROLLOUT)]
    return jax.nn.silu(jnp.stack(rows, axis=1)).astype(BF)


def block_pass(inputs, cotangent, rows, wa, wup, wdown):
    block = inputs.shape[0]
    blocks = (8, 4, SLAB, PART)
    (qkv0,) = rows_call(first_kernel, "first", [inputs], [rows, wa], [(3 * D, BF)], [])
    att0, p0 = attend(qkv0, block)
    a0, gp0, act0, f0, x1, qkv1 = rows_call(
        middle_kernel, "middle", [inputs, att0], [rows, wa, wup, wdown],
        [(D, F32), (FF, F32), (FF, BF), (D, F32), (D, F32), (3 * D, BF)], [],
    )
    att1, p1 = attend(qkv1, block)
    result, dmid1, datt1, gdown, gup, gproj, wide1, narrow1 = rows_call(
        turn_kernel, "turn", [x1, att1, cotangent], [rows, wa, wup, wdown],
        [(D, F32), (D, F32), (D, BF)],
        [((FF, D), F32), ((D, FF), F32), ((D, D), F32), ((8, FF), F32), ((8, D), F32)],
    )
    dq, dk, dv = attend_back(qkv1, datt1, p1, block)
    dmid0, datt0, gqkv, gproj, wide0, narrow1b, narrow0, bias1, gup_blocks, gdown_blocks = rows_call(
        join_kernel, "join",
        [dq, dk, dv, x1, dmid1, inputs, a0, gp0, act0, f0, att0],
        [rows, wa, wup, wdown, gproj],
        [(D, F32), (D, BF)],
        [((D, 3 * D), F32), ((D, D), F32), ((8, FF), F32), ((8, D), F32), ((8, D), F32),
         ((8, 3 * D), F32), (blocks, BF), (blocks, BF)],
        [gdown, gup],
        [pltpu.VMEM((FF, D), F32), pltpu.VMEM((D, FF), F32), pltpu.VMEM((FF, D), F32),
         pltpu.VMEM((D, FF), F32), pltpu.SemaphoreType.DMA((2,))],
    )
    dq, dk, dv = attend_back(qkv0, datt0, p0, block)
    input_grad, vec, gqkv_blocks = rows_call(
        last_kernel, "last", [dq, dk, dv, inputs, dmid0],
        [rows, wa, gqkv, gproj, wide1, narrow1, wide0, narrow1b, narrow0, bias1],
        [(D, F32)], [((64, 128), F32), (blocks, BF)], (),
        [pltpu.VMEM((D, 3 * D), F32), pltpu.VMEM((8, D), F32), pltpu.VMEM((8, 3 * D), F32)],
    )
    return (result, input_grad, gqkv_blocks, gup_blocks, gdown_blocks, vec)


def plain_gather(group_interval, counts, rollout_start, lead_table, masters):
    low = [master.astype(BF) for master in masters]
    owner = lax.axis_index("dp")
    group_index = lax.axis_index("grp")
    own_rows = D // lax.axis_size("dp")
    counts = counts.astype(F32)
    share = lax.axis_size("grp") * counts / jnp.sum(counts)
    share = lax.dynamic_index_in_dim(share, group_index, keepdims=False)
    conditions = all_conditions(group_interval, rollout_start, lead_table)
    owner_columns = lax.dynamic_slice_in_dim(conditions, owner * own_rows, own_rows, axis=2)
    own_condition = lax.dynamic_index_in_dim(owner_columns, group_index, keepdims=False)
    modulation = lax.psum(dot(own_condition, low[4].reshape(own_rows, 6 * D)), "dp")
    qkv, proj, up, down, bias = [
        lax.all_gather(low[index], "dp", axis=0, tiled=True) for index in (0, 1, 2, 3, 5)
    ]
    bias = bias.astype(F32)
    modulation = modulation + bias[4 * D + FF :][None]
    share_rows = jnp.broadcast_to(share, (ROLLOUT, 2, D))
    mods = jnp.concatenate([modulation.reshape(ROLLOUT, 6, D), share_rows], axis=1).reshape(-1, D)
    rows = jnp.concatenate(
        [mods, bias[:D][None], jnp.zeros((1, D), F32), bias[D : 4 * D + FF].reshape(-1, D),
         jnp.zeros((7, D), F32)]
    )
    wa = jnp.concatenate([qkv.reshape(D, 3 * D), proj.reshape(D, D)], axis=1)
    return (wa, up.reshape(D, FF), down.reshape(FF, D), rows, owner_columns)


def plain_update(owner_columns, vec, blocks, masters, firsts, seconds):
    owner = lax.axis_index("dp")
    vec = vec.reshape(-1)
    split = 4 * D + FF
    dmod = vec[split : split + ROLLOUT * 6 * D].reshape(ROLLOUT, 6 * D)
    dmod_all = lax.all_gather(lax.psum(dmod, "dp"), "grp")
    bias_sum = lax.psum(vec[:split], ("grp", "dp"))
    bias_sum = jnp.concatenate([bias_sum, jnp.sum(dmod_all, axis=(0, 1))])
    bias_rows = masters[5].shape[0]
    bias_grad = lax.dynamic_slice_in_dim(bias_sum, owner * bias_rows, bias_rows)
    ada_grad = jnp.einsum(
        "gsr,gsc->rc", owner_columns.astype(F32), dmod_all, precision=lax.Precision.HIGHEST
    )
    flat_a, flat_up = [
        block.transpose(0, 2, 1, 3).reshape(D, FF) for block in blocks[:2]
    ]
    flat = [flat_a[:, : 3 * D], flat_a[:, 3 * D :], flat_up, blocks[2]]
    shares = []
    for grad in flat:
        summed = lax.psum(grad.reshape(-1), "grp").astype(F32)
        shares.append(lax.psum_scatter(summed, "dp", scatter_dimension=0, tiled=True))
    shares = shares + [ada_grad.reshape(-1), bias_grad]
    local_square = sum((jnp.sum(piece * piece) for piece in shares))
    grad_norm = jnp.sqrt(lax.psum(local_square, "dp"))
    clip = grad_limit / jnp.maximum(grad_norm, grad_limit)
    decays = [0.1, 0.1, 0.1, 0.1, 0.1, 0.0]
    results = [
        adam(master, first, second, grad * clip, decay)
        for master, first, second, grad, decay in zip(masters, firsts, seconds, shares, decays)
    ]
    news, first_news, second_news = zip(*results)
    return (grad_norm, *news, *first_news, *second_news, *(new.astype(BF) for new in news))


def per_device(
    inputs,
    cotangent,
    group_interval,
    sample_counts,
    rollout_start,
    lead_table,
    *state,
):
    masters, firsts, seconds = (state[0:6], state[6:12], state[12:18])
    owners = lax.axis_size("dp")
    fits = owners == 2 * LAYERS and lax.axis_size("grp") == GROUPS
    if fits:
        wa, wup, wdown, rows = gather(
            rollout_start, group_interval, sample_counts, lead_table, masters
        )
    else:
        wa, wup, wdown, rows, owner_columns = plain_gather(
            group_interval, sample_counts, rollout_start, lead_table, masters
        )
    result, input_grad, ga, gu, gd, vec = block_pass(inputs, cotangent, rows, wa, wup, wdown)
    if not fits:
        rest = plain_update(owner_columns, vec, (ga, gu, gd), masters, firsts, seconds)
        return (result, input_grad, *rest)
    pieces, ada_grad, bias_sum, square = reduce(
        rollout_start, group_interval, lead_table, vec,
        [grad.reshape(LAYERS, 2, GROUPS, SLAB, PART) for grad in (ga, gu, gd)],
    )
    news, first_news, second_news, copies = update(
        pieces, ada_grad, square, masters, firsts, seconds
    )
    grad_norm = jnp.sqrt(square[0, 0])
    clip = grad_limit / jnp.maximum(grad_norm, grad_limit)
    bias_rows = masters[5].shape[0]
    bias_grad = lax.dynamic_slice_in_dim(
        bias_sum.reshape(-1), lax.axis_index("dp") * bias_rows, bias_rows
    )
    new, first, second = adam(masters[5], firsts[5], seconds[5], bias_grad * clip, 0.0)
    return (
        result, input_grad, grad_norm, *news, new, *first_news, first, *second_news, second,
        *copies, new.astype(BF),
    )


def solution(mesh):
    rows = P(("grp", "dp"), None)
    return jax.shard_map(
        per_device,
        mesh=mesh,
        in_specs=(rows, rows, P(), P(), P(), P(), *[P("dp")] * 18),
        out_specs=(rows, rows, P(), *[P("dp")] * 24),
        check_vma=False,
    )
```

time: 562 us -> 217 us (0.39); the launches traced: 555 us -> 217 us
  blocking collectives: 294 us -> 0 us
  Pallas kernels: 134 us -> 210 us
  waiting for transfers between devices: 50.1 us -> 0 us
  other arithmetic: 30.3 us -> 1.4 us
  between operations: 23.2 us -> 2.62 us
  local copies, waits for them, and re-layouts: 21 us -> 2.5 us
    unnamed x2 -> x0, blocking collectives: 176 us -> none
    psum x3 -> x0, blocking collectives: 79.5 us -> none  [the longest x1 39.3 us: per_device(): bias_sum = lax.psum(vectors, ('grp', 'dp'))]
    pallas_call x0 -> x3, Pallas kernels: none -> 76.3 us  [the longest x1 41.2 us: reduce(): pl.pallas_call(reduce_kernel, in_specs=[smem, smem, vmem, vmem, hbm, hbm,...]
    psum x1 -> x0, waiting for transfers between devices: 50.1 us -> none  [per_device(): summed = lax.psum((grad * share).astype(BF).reshape(-1), 'grp').astype(F32)]
    all_gather x3 -> x0, blocking collectives: 38.8 us -> none  [the longest x2 30.3 us: per_device(): lax.all_gather(low[index], 'dp', axis=0, tiled=True)]
    convert_element_type x18 -> x1, other arithmetic: 19.7 us -> 1.4 us  [per_device(): new.astype(BF)]
    reshape x11 -> x1, local copies, waits for them, and re-layouts: 16.9 us -> 1.28 us  [gather(): jnp.pad(bias, (0, 1024 - bias.shape[0])).reshape(8, 128)]
  transfers between devices with their start and end apart: 3 -> 0, of which waited for: 1 -> 0; matrix products, arithmetic and copies ran while one was open for 4% -> 0% of each run, Pallas kernels for 3% -> 0%
where the time goes in v2:
time: 217 us
  Pallas kernels  210 us (97%)
  between operations  2.62 us (1%)
  local copies, waits for them, and re-layouts  2.5 us (1%)
    pallas_call x5, Pallas kernels, rows_call(): pl.pallas_call(kernel, grid=(length // ROWS,), in_specs=[row_spec(a.shape...  67.6 us
    pallas_call x1, Pallas kernels, reduce(): pl.pallas_call(reduce_kernel, in_specs=[smem, smem, vmem, vmem, hbm, hbm,...  41.2 us
    pallas_call x2, Pallas kernels, attend_back(): pl.pallas_call(attend_back_kernel, grid=(pairs, length // block), in_spec...  38.7 us
    pallas_call x1, Pallas kernels, gather(): pl.pallas_call(gather_kernel, in_specs=[smem] * 3 + [vmem] * 7, out_specs...  28.8 us
    pallas_call x2, Pallas kernels, attend(): pl.pallas_call(attend_kernel, grid=(pairs, length // block), in_specs=[pl...  27.6 us
    pallas_call x1, Pallas kernels, update(): pl.pallas_call(adam_kernel, in_specs=[vmem] * 18, out_specs=[vmem] * 20,...  6.33 us

profile of v2, /device:TPU:0, one launch (start us, length us, event | category | flops | bytes accessed | tf_op | source)
XLA Modules:
  0.0 216.6 jit_solution(144920894504374214)
XLA Ops:
  0.7 1.3 pad_bitcast_fusion.bias_ref
  2.0 28.8 %gather.1 = (bf16[8,48,1536]{2,1,0:T(8,128)(2,1)}, bf16[8,48,1536]{2,1,0:T(8,128)(2,1)}, bf16[8,4,48,384]{3,2,1,0:T(8,128)(2,1)}, f32[32,384]{1,0:T(8,128)}) custom-call(s32[4]{0:T(128)} %start_ref.3, s32[4]{0:T(128)} %interval_ref.3, s32[4]{0:T(128)} %counts_ref.1, f32[3,384]{1,0:T(4,128)} %lead_ref.3, f32[432,128]{1,0:T(8,128)} %bitcast.65, ...), custom_call_target="tpu_custom_call" | custom-call | tf_op jit(solution)/shard_map/gather/pallas_call | solution.py:641
  30.7 5.5 %first.1.q_ref.k_ref.v_ref = bf16[1024,1152]{1,0:T(8,128)(2,1)} custom-call(bf16[1024,384]{1,0:T(8,128)(2,1)} %x_ref.5, f32[32,384]{1,0:T(8,128)} %get-tuple-element.92.rows_ref, bf16[384,1536]{1,0:T(8,128)(2,1)} %bitcast.45), custom_call_target="tpu_custom_call" | custom-call | tf_op jit(solution)/shard_map/first/pallas_call | solution.py:272
  36.2 13.8 %attend.2 = (bf16[1024,384]{1,0:T(8,128)(2,1)}, bf16[6,1024,1024]{2,1,0:T(8,128)(2,1)}) custom-call(bf16[1024,1152]{1,0:T(8,128)(2,1)} %first.1.q_ref.k_ref.v_ref, bf16[1024,1152]{1,0:T(8,128)(2,1)} %first.1.q_ref.k_ref.v_ref, bf16[1024,1152]{1,0:T(8,128)(2,1)} %first.1.q_ref.k_ref.v_ref), custom_call_target="tpu_custom_call" | custom-call | tf_op jit(solution)/shard_map/attend/pallas_call | solution.py:323
  50.0 12.3 %middle.1 = (f32[1024,384]{1,0:T(8,128)}, f32[1024,1536]{1,0:T(8,128)}, bf16[1024,1536]{1,0:T(8,128)(2,1)}, f32[1024,384]{1,0:T(8,128)}, f32[1024,384]{1,0:T(8,128)}, /*index=5*/bf16[1024,1152]{1,0:T(8,128)(2,1)}) custom-call(bf16[1024,384]{1,0:T(8,128)(2,1)} %x_ref.5, bf16[1024,384]{1,0:T(8,128)(2,1)} %get-tuple-element.94.att_ref, ...), custom_call_target="tpu_custom_call" | custom-call | tf_op jit(solution)/shard_map/middle/pallas_call | solution.py:272
  62.3 13.8 %attend.3 = (bf16[1024,384]{1,0:T(8,128)(2,1)}, bf16[6,1024,1024]{2,1,0:T(8,128)(2,1)}) custom-call(bf16[1024,1152]{1,0:T(8,128)(2,1)} %get-tuple-element.98.q_ref.k_ref.v_ref, bf16[1024,1152]{1,0:T(8,128)(2,1)} %get-tuple-element.98.q_ref.k_ref.v_ref, bf16[1024,1152]{1,0:T(8,128)(2,1)} %get-tuple-element.98.q_ref.k_ref.v_ref), custom_call_target="tpu_custom_call" | custom-call | tf_op jit(solution)/shard_map/attend/pallas_call | solution.py:323
  76.1 18.8 %turn.1 = (f32[1024,384]{1,0:T(8,128)}, f32[1024,384]{1,0:T(8,128)}, bf16[1024,384]{1,0:T(8,128)(2,1)}, f32[1536,384]{1,0:T(8,128)}, f32[384,1536]{1,0:T(8,128)}...) custom-call(f32[1024,384]{1,0:T(8,128)} %get-tuple-element.97.x_ref.x1_ref, ...), custom_call_target="tpu_custom_call" | custom-call | tf_op jit(solution)/shard_map/turn/pallas_call | solution.py:272
  94.9 19.3 %attend_back.2 = (bf16[1024,384]{1,0:T(8,128)(2,1)}, bf16[1024,384]{1,0:T(8,128)(2,1)}, bf16[1024,384]{1,0:T(8,128)(2,1)}) custom-call(bf16[1024,1152]{1,0:T(8,128)(2,1)} %get-tuple-element.98.q_ref.k_ref.v_ref, bf16[1024,1152]{1,0:T(8,128)(2,1)} %get-tuple-element.98.q_ref.k_ref.v_ref, bf16[1024,1152]{1,0:T(8,128)(2,1)} %get-tuple-element.98.q_ref.k_ref.v_ref, ...), custom_call_target="tpu_custom_call" | custom-call | tf_op jit(solution)/shard_map/attend_back/pallas_call | solution.py:381
  114.3 21.9 %join.1 = (f32[1024,384]{1,0:T(8,128)}, bf16[1024,384]{1,0:T(8,128)(2,1)}, f32[384,1152]{1,0:T(8,128)}, f32[384,384]{1,0:T(8,128)}, f32[8,1536]{1,0:T(8,128)}, /...) custom-call(bf16[1024,384]{1,0:T(8,128)(2,1)} %get-tuple-element.103, ...), custom_call_target="tpu_custom_call" | custom-call | tf_op jit(solution)/shard_map/join/pallas_call | solution.py:272
  136.2 19.4 %attend_back.3 = (bf16[1024,384]{1,0:T(8,128)(2,1)}, bf16[1024,384]{1,0:T(8,128)(2,1)}, bf16[1024,384]{1,0:T(8,128)(2,1)}) custom-call(bf16[1024,1152]{1,0:T(8,128)(2,1)} %first.1.q_ref.k_ref.v_ref, bf16[1024,1152]{1,0:T(8,128)(2,1)} %first.1.q_ref.k_ref.v_ref, bf16[1024,1152]{1,0:T(8,128)(2,1)} %first.1.q_ref.k_ref.v_ref, ...), custom_call_target="tpu_custom_call" | custom-call | tf_op jit(solution)/shard_map/attend_back/pallas_call | solution.py:381
  155.6 9.0 %last.1 = (f32[1024,384]{1,0:T(8,128)}, f32[64,128]{1,0:T(8,128)}, bf16[8,4,48,384]{3,2,1,0:T(8,128)(2,1)}) custom-call(bf16[1024,384]{1,0:T(8,128)(2,1)} %get-tuple-element.116.dq_ref, bf16[1024,384]{1,0:T(8,128)(2,1)} %get-tuple-element.117.dk_ref, bf16[1024,384]{1,0:T(8,128)(2,1)} %get-tuple-element.118.dv_ref, bf16[1024,384]{1,0:T(8,128)(2,1)} %x_ref.5, ...), custom_call_target="tpu_custom_call" | custom-call | tf_op jit(solution)/shard_map/last/pallas_call | solution.py:272
  164.6 0.0 copy-start
  164.6 0.0 copy-start.1
  164.6 0.0 copy-start.2
  164.6 41.2 %reduce.1 = (bf16[3,4,48,384]{3,2,1,0:T(8,128)(2,1)}, f32[864,128]{1,0:T(8,128)}, f32[48,128]{1,0:T(8,128)}, f32[8,128]{1,0:T(8,128)}) custom-call(s32[4]{0:T(128)} %start_ref.3, s32[4]{0:T(128)} %interval_ref.3, f32[3,384]{1,0:T(4,128)} %lead_ref.3, f32[64,128]{1,0:T(8,128)} %get-tuple-element.129.vec_ref, bf16[4,2,4,48,384]{4,3,2,1,0:T(8,128)(2,1)} %bitcast.64, ...), custom_call_target="tpu_custom_call" | custom-call | tf_op jit(solution)/shard_map/reduce/pallas_call | solution.py:853
  205.8 1.2 slice.3
  207.7 0.0 copy-done
  207.8 0.0 copy-done.1
  207.8 0.0 copy-done.2
  207.8 1.4 fusion.1
  209.2 6.3 %adam.1 = (f32[432,128]{1,0:T(8,128)}, f32[144,128]{1,0:T(8,128)}, f32[576,128]{1,0:T(8,128)}, f32[576,128]{1,0:T(8,128)}, f32[864,128]{1,0:T(8,128)}, /*index=5...) custom-call(bf16[3,4,48,384]{3,2,1,0:T(8,128)(2,1)} %get-tuple-eleme, ...), custom_call_target="tpu_custom_call" | custom-call | tf_op jit(solution)/shard_map/adam/pallas_call | solution.py:938
Async XLA Ops:
  164.6 43.1 %copy-start = (f32[672]{0:T(1024)S(1)}, f32[672]{0:T(1024)}, u32[]{:S(2)}) copy-start(f32[672]{0:T(1024)} %param.35) | copy-start | bytes 8068
  164.6 43.1 %copy-start.1 = (f32[672]{0:T(1024)S(1)}, f32[672]{0:T(1024)}, u32[]{:S(2)}) copy-start(f32[672]{0:T(1024)} %param.41) | copy-start | bytes 8068
  164.6 43.1 %copy-start.2 = (f32[672]{0:T(1024)S(1)}, f32[672]{0:T(1024)}, u32[]{:S(2)}) copy-start(f32[672]{0:T(1024)} %param.47) | copy-start | bytes 8068

commit v3 on v2

--- a/solution.py
+++ b/solution.py
@@ -73,15 +73,14 @@
     return jnp.concatenate([ref[row : row + 1, :] for row in range(first, first + count)], axis=1)
 
 
-def first_kernel(x_ref, rows_ref, wa_ref, qkv_ref):
-    mods = mod_reader(rows_ref, 0)
-    normed, _ = layer_norm(x_ref[...].astype(F32))
-    hidden = modulated(normed, mods, SCALE1, SHIFT1)
+def first_rows(x, rows_ref, wa_ref):
+    normed, _ = layer_norm(x.astype(F32))
+    hidden = modulated(normed, mod_reader(rows_ref, 0), SCALE1, SHIFT1)
     qkv = dot(hidden, wa_ref[:, : 3 * D]) + side_by_side(rows_ref, ROW_BQKV, 3)
-    qkv_ref[...] = qkv.astype(BF)
-
-
-def middle_kernel(
+    return qkv.astype(BF)
+
+
+def middle_rows(
     x_ref, att_ref, rows_ref, wa_ref, wup_ref, wdown_ref,
     a_ref, gp_ref, act_ref, f_ref, next_ref, qkv_ref,
 ):
@@ -132,15 +131,10 @@
     datt_ref[...] = dot(da, wa_ref[:, 3 * D :], NT).astype(BF)
 
 
-def turn_kernel(
+def turn_rows(
     x_ref, att_ref, cot_ref, rows_ref, wa_ref, wup_ref, wdown_ref,
     out_ref, dmid_ref, datt_ref, gdown_ref, gup_ref, gproj_ref, wide_ref, narrow_ref,
 ):
-    @pl.when(pl.program_id(0) == 0)
-    def _():
-        for ref in (gdown_ref, gup_ref, gproj_ref, wide_ref, narrow_ref):
-            ref[...] = jnp.zeros_like(ref)
-
     mods = mod_reader(rows_ref, 1)
     shared = mod_reader(rows_ref, 0)
     att = att_ref[...]
@@ -171,29 +165,14 @@
     return dmid + norm_back(normed, inverse, dh * (1.0 + mods(SCALE1)))
 
 
-def join_kernel(
-    dq_ref, dk_ref, dv_ref, x1_ref, dmid1_ref, x0_ref, a_ref, gp_ref, act_ref, f_ref, att_ref,
-    rows_ref, wa_ref, wup_ref, wdown_ref, gproj_in, gdown_in, gup_in,
-    dmid_ref, datt_ref, gqkv_ref, gproj_ref, wide_ref, narrow1_ref, narrow_ref, bias_ref,
-    up_blocks, down_blocks,
-    gdown_sum, gup_sum, gdown_before, gup_before, sems,
+def join_rows(
+    dqkv_ref, x1_ref, x0_ref, a_ref, gp_ref, act_ref, f_ref, att_ref,
+    rows_ref, wa_ref, wup_ref, wdown_ref,
+    dmid_ref, datt_ref, gqkv_ref, gdown_ref, gup_ref, gproj_ref, wide_ref, narrow1_ref,
+    narrow_ref, bias_ref,
 ):
-    before = [
-        pltpu.make_async_copy(gdown_in, gdown_before, sems.at[0]),
-        pltpu.make_async_copy(gup_in, gup_before, sems.at[1]),
-    ]
-
-    @pl.when(pl.program_id(0) == 0)
-    def _():
-        for copy in before:
-            copy.start()
-        for ref in (gqkv_ref, wide_ref, narrow1_ref, narrow_ref, bias_ref, gdown_sum, gup_sum):
-            ref[...] = jnp.zeros_like(ref)
-        gproj_ref[...] = gproj_in[...]
-
-    dqkv = jnp.concatenate([dq_ref[...], dk_ref[...], dv_ref[...]], axis=1)
     grad = qkv_back(
-        mod_reader(rows_ref, 1), x1_ref[...], dmid1_ref[...], dqkv, wa_ref, gqkv_ref,
+        mod_reader(rows_ref, 1), x1_ref[...], dmid_ref[...], dqkv_ref[...], wa_ref, gqkv_ref,
         narrow1_ref, bias_ref,
     )
     mods = mod_reader(rows_ref, 0)
@@ -203,84 +182,9 @@
     hidden = modulated(normed, mods, SCALE2, SHIFT2)
     ffn_back(
         mods, grad, f_ref[...], act_ref[...], gp_ref[...], normed, inverse, hidden,
-        branch_one, att_ref[...], wa_ref, wup_ref, wdown_ref, gdown_sum, gup_sum, gproj_ref,
+        branch_one, att_ref[...], wa_ref, wup_ref, wdown_ref, gdown_ref, gup_ref, gproj_ref,
         wide_ref, narrow_ref, dmid_ref, datt_ref,
     )
-
-    @pl.when(pl.program_id(0) == pl.num_programs(0) - 1)
-    def _():
-        for copy in before:
-            copy.wait()
-        share = rows_ref[ROW_SHARE : ROW_SHARE + 1, :]
-        for d in range(8):
-            for g in range(4):
-                rows, columns = (slice(SLAB * d, SLAB * (d + 1)), slice(PART * g, PART * (g + 1)))
-                up_blocks[d, g] = ((gup_sum[rows, columns] + gup_before[rows, columns]) * share).astype(BF)
-                first = SLAB * (4 * d + g)
-                rows = slice(first, first + SLAB)
-                down_blocks[d, g] = ((gdown_sum[rows, :] + gdown_before[rows, :]) * share).astype(BF)
-
-
-def last_kernel(
-    dq_ref, dk_ref, dv_ref, x_ref, dmid_ref, rows_ref, wa_ref, gqkv_in, gproj_in,
-    wide1, narrow1, wide0, narrow1b, narrow0, bias1,
-    dx_ref, vec_ref, qkv_blocks, gqkv_ref, narrow_ref, bias_ref,
-):
-    @pl.when(pl.program_id(0) == 0)
-    def _():
-        narrow_ref[...] = jnp.zeros_like(narrow_ref)
-        bias_ref[...] = jnp.zeros_like(bias_ref)
-        gqkv_ref[...] = gqkv_in[...]
-
-    dqkv = jnp.concatenate([dq_ref[...], dk_ref[...], dv_ref[...]], axis=1)
-    dx_ref[...] = qkv_back(
-        mod_reader(rows_ref, 0), x_ref[...].astype(F32), dmid_ref[...], dqkv, wa_ref,
-        gqkv_ref, narrow_ref, bias_ref,
-    )
-
-    @pl.when(pl.program_id(0) == pl.num_programs(0) - 1)
-    def _():
-        share = rows_ref[ROW_SHARE : ROW_SHARE + 1, :]
-        for d in range(8):
-            rows = slice(SLAB * d, SLAB * (d + 1))
-            for g in range(3):
-                qkv_blocks[d, g] = (gqkv_ref[rows, PART * g : PART * (g + 1)] * share).astype(BF)
-            qkv_blocks[d, 3] = (gproj_in[rows, :] * share).astype(BF)
-
-        def put(first, value):
-            for j in range(value.shape[1] // 128):
-                vec_ref[first + j : first + j + 1, :] = value[:, 128 * j : 128 * j + 128] * share[:, 0:128]
-
-        qkv_bias = bias_ref[0:1, :] + bias1[0:1, :]
-        put(0, qkv_bias[:, :D])
-        put(3, qkv_bias[:, 2 * D :])
-        put(6, narrow0[6:7, :] + narrow1[6:7, :])
-        put(9, wide0[0:1, :] + wide1[0:1, :])
-        put(21, narrow0[7:8, :] + narrow1[7:8, :])
-        for r in range(6):
-            put(24 + 3 * r, narrow0[r : r + 1, :] + narrow_ref[r : r + 1, :])
-            put(42 + 3 * r, narrow1[r : r + 1, :] + narrow1b[r : r + 1, :])
-        vec_ref[60:64, :] = jnp.zeros((4, 128), F32)
-
-
-def rows_call(kernel, name, row_args, whole_args, row_outs, whole_outs, far_args=(), scratch=()):
-    length = row_args[0].shape[0]
-    row_spec = lambda width: pl.BlockSpec((ROWS, width), lambda i: (i, 0))
-    fixed = lambda shape: (lambda i: (0,) * len(shape))
-    whole_in = lambda shape: pl.BlockSpec(shape, fixed(shape), pipeline_mode=pl.Buffered(1))
-    whole_out = lambda shape: pl.BlockSpec(shape, fixed(shape))
-    return pl.pallas_call(
-        kernel,
-        grid=(length // ROWS,),
-        in_specs=[row_spec(a.shape[1]) for a in row_args]
-        + [whole_in(a.shape) for a in whole_args]
-        + [pl.BlockSpec(memory_space=pl.ANY) for _ in far_args],
-        out_specs=[row_spec(w) for w, _ in row_outs] + [whole_out(s) for s, _ in whole_outs],
-        out_shape=[jax.ShapeDtypeStruct((length, w), t) for w, t in row_outs]
-        + [jax.ShapeDtypeStruct(s, t) for s, t in whole_outs],
-        scratch_shapes=list(scratch),
-        name=name,
-    )(*row_args, *whole_args, *far_args)
 
 
 def head_lanes(rows):
@@ -298,12 +202,9 @@
 score_scale = HEAD_DIM**-0.5
 
 
-def attend_kernel(q_ref, k_ref, v_ref, o_ref, p_ref, vt_ref):
-    @pl.when(pl.program_id(1) == 0)
-    def _():
-        turned_heads(v_ref[...].astype(F32), vt_ref)
-
-    queries = q_ref[...] * BF(score_scale)
+def attend_pair(q, k_ref, v, o_ref, p_ref, vt_ref):
+    turned_heads(v.astype(F32), vt_ref)
+    queries = q * BF(score_scale)
     mixed = None
     for half, lanes in enumerate(head_lanes(queries.shape[0])):
         scores = dot(k_ref[...], jnp.where(lanes, queries, BF(0)), NT)
@@ -317,44 +218,10 @@
     o_ref[...] = jnp.transpose(mixed).astype(BF)
 
 
-def attend(qkv, block):
-    length = qkv.shape[0]
-    pairs = HEADS // 2
-    return pl.pallas_call(
-        attend_kernel,
-        grid=(pairs, length // block),
-        in_specs=[
-            pl.BlockSpec((block, 128), lambda h, i: (i, h)),
-            pl.BlockSpec((length, 128), lambda h, i: (0, pairs + h)),
-            pl.BlockSpec((length, 128), lambda h, i: (0, 2 * pairs + h)),
-        ],
-        out_specs=[
-            pl.BlockSpec((block, 128), lambda h, i: (i, h)),
-            pl.BlockSpec((2, length, block), lambda h, i: (h, 0, i)),
-        ],
-        out_shape=[
-            jax.ShapeDtypeStruct((length, D), BF),
-            jax.ShapeDtypeStruct((HEADS, length, length), BF),
-        ],
-        scratch_shapes=[pltpu.VMEM((2, 128, length), BF)],
-        name="attend",
-    )(qkv, qkv, qkv)
-
-
-def attend_back_kernel(
-    q_ref, k_ref, v_ref, do_ref, p_ref, dq_ref, dk_ref, dv_ref, kt_ref, dk_sum, dv_sum
-):
-    block_id = pl.program_id(1)
-
-    @pl.when(block_id == 0)
-    def _():
-        turned_heads(k_ref[...].astype(F32) * score_scale, kt_ref)
-        dk_sum[...] = jnp.zeros_like(dk_sum)
-        dv_sum[...] = jnp.zeros_like(dv_sum)
-
-    queries = q_ref[...] * BF(score_scale)
-    grads = do_ref[...]
-    dq_turned = None
+def attend_back_pair(q, k, v_ref, grads, p_ref, dq_ref, dk_ref, dv_ref, kt_ref):
+    turned_heads(k.astype(F32) * score_scale, kt_ref)
+    queries = q * BF(score_scale)
+    dq_turned, dk, dv = (None, None, None)
     for half, lanes in enumerate(head_lanes(queries.shape[0])):
         grad = jnp.where(lanes, grads, BF(0))
         query = jnp.where(lanes, queries, BF(0))
@@ -363,44 +230,14 @@
         weights = low.astype(F32)
         delta = jnp.sum(weights * weight_grad, axis=0, keepdims=True)
         score_grad = (weights * (weight_grad - delta)).astype(BF)
-        dk_sum[...] += dot(score_grad, query)
-        dv_sum[...] += dot(low, grad)
-        part = dot(kt_ref[half], score_grad)
-        dq_turned = part if dq_turned is None else dq_turned + part
+        parts = (dot(kt_ref[half], score_grad), dot(score_grad, query), dot(low, grad))
+        if half == 0:
+            dq_turned, dk, dv = parts
+        else:
+            dq_turned, dk, dv = (dq_turned + parts[0], dk + parts[1], dv + parts[2])
     dq_ref[...] = jnp.transpose(dq_turned).astype(BF)
-
-    @pl.when(block_id == pl.num_programs(1) - 1)
-    def _():
-        dk_ref[...] = dk_sum[...].astype(BF)
-        dv_ref[...] = dv_sum[...].astype(BF)
-
-
-def attend_back(qkv, grads, weights, block):
-    length = qkv.shape[0]
-    pairs = HEADS // 2
-    return pl.pallas_call(
-        attend_back_kernel,
-        grid=(pairs, length // block),
-        in_specs=[
-            pl.BlockSpec((block, 128), lambda h, i: (i, h)),
-            pl.BlockSpec((length, 128), lambda h, i: (0, pairs + h)),
-            pl.BlockSpec((length, 128), lambda h, i: (0, 2 * pairs + h)),
-            pl.BlockSpec((block, 128), lambda h, i: (i, h)),
-            pl.BlockSpec((2, length, block), lambda h, i: (h, 0, i)),
-        ],
-        out_specs=[
-            pl.BlockSpec((block, 128), lambda h, i: (i, h)),
-            pl.BlockSpec((length, 128), lambda h, i: (0, h)),
-            pl.BlockSpec((length, 128), lambda h, i: (0, h)),
-        ],
-        out_shape=[jax.ShapeDtypeStruct((length, D), BF)] * 3,
-        scratch_shapes=[
-            pltpu.VMEM((2, 128, length), BF),
-            pltpu.VMEM((length, 128), F32),
-            pltpu.VMEM((length, 128), F32),
-        ],
-        name="attend_back",
-    )(qkv, qkv, qkv, grads, weights)
+    dk_ref[...] = dk.astype(BF)
+    dv_ref[...] = dv.astype(BF)
 
 
 MESH_ID = pl.DeviceIdType.MESH
@@ -947,6 +784,239 @@
     return (results[0:5], results[5:10], results[10:15], results[15:20])
 
 
+def block_kernel(
+    x_ref, rows_ref, wa_far, wup_far, wdown_far, cot_far,
+    y_far, dx_far, ga_far, gu_far, gd_far, vec_ref, p_far,
+    wa_ref, wup_ref, wdown_ref, cot_ref, qkv0, qkv1, p_ref, att0, att1, a_ref, f_ref, x1_ref,
+    dmid_ref, y_ref, gp_ref, act_ref, datt_ref, dqkv_ref, gqkv, gproj, gup, gdown, turned_ref,
+    wide, narrow0, narrow1, bias, blocks, in_sems, p_sems, out_sems,
+):
+    def copy(src, dst, sem):
+        made = pltpu.make_async_copy(src, dst, sem)
+        made.start()
+        return made
+
+    length = x_ref.shape[0]
+    get_wa = copy(wa_far, wa_ref, in_sems.at[0])
+    later = [
+        copy(wup_far, wup_ref, in_sems.at[1]),
+        copy(wdown_far, wdown_ref, in_sems.at[2]),
+        copy(cot_far, cot_ref, in_sems.at[3]),
+    ]
+
+    def over_rows(body):
+        def step(i, carry):
+            body(pl.ds(pl.multiple_of(i * ROWS, ROWS), ROWS))
+            return carry
+
+        lax.fori_loop(0, length // ROWS, step, 0)
+
+    def columns(h, offset=0):
+        return pl.ds(pl.multiple_of(offset + 128 * h, 128), 128)
+
+    def over_pairs(body):
+        def step(h, carry):
+            body(h)
+            return carry
+
+        lax.fori_loop(0, HEADS // 2, step, 0)
+
+    pairs = HEADS // 2
+
+    def save(step, h):
+        slot = lax.rem(h, 2)
+        return pltpu.make_async_copy(
+            p_ref.at[slot], p_far.at[step, pl.ds(2 * h, 2)], p_sems.at[slot]
+        )
+
+    def fetch(step, h):
+        slot = lax.rem(h, 2)
+        return pltpu.make_async_copy(
+            p_far.at[step, pl.ds(2 * h, 2)], p_ref.at[slot], p_sems.at[slot]
+        )
+
+    def attend(step, qkv, att):
+        def body(h):
+            @pl.when(h >= 2)
+            def _():
+                save(step, h - 2).wait()
+
+            attend_pair(
+                qkv[:, columns(h)], qkv.at[:, columns(h, D)], qkv[:, columns(h, 2 * D)],
+                att.at[:, columns(h)], p_ref.at[lax.rem(h, 2)], turned_ref,
+            )
+            save(step, h).start()
+
+        over_pairs(body)
+
+    def finish_saves(step):
+        for h in range(pairs - 2, pairs):
+            save(step, h).wait()
+
+    def attend_back(step, qkv):
+        def body(h):
+            fetch(step, h).wait()
+            attend_back_pair(
+                qkv[:, columns(h)], qkv[:, columns(h, D)], qkv.at[:, columns(h, 2 * D)],
+                datt_ref[:, columns(h)], p_ref.at[lax.rem(h, 2)],
+                dqkv_ref.at[:, columns(h)], dqkv_ref.at[:, columns(h, D)],
+                dqkv_ref.at[:, columns(h, 2 * D)], turned_ref,
+            )
+
+            @pl.when(h + 2 < pairs)
+            def _():
+                fetch(step, h + 2).start()
+
+        over_pairs(body)
+
+    get_wa.wait()
+
+    def first(rows):
+        qkv0[rows, :] = first_rows(x_ref[rows, :], rows_ref, wa_ref)
+
+    over_rows(first)
+
+    attend(0, qkv0, att0)
+    for made in later:
+        made.wait()
+
+    def middle(rows):
+        middle_rows(
+            x_ref.at[rows], att0.at[rows], rows_ref, wa_ref, wup_ref, wdown_ref,
+            a_ref.at[rows], gp_ref.at[rows], act_ref.at[rows], f_ref.at[rows], x1_ref.at[rows],
+            qkv1.at[rows],
+        )
+
+    over_rows(middle)
+    finish_saves(0)
+    attend(1, qkv1, att1)
+
+    for ref in (gqkv, gproj, gup, gdown, wide, narrow0, narrow1, bias):
+        ref[...] = jnp.zeros_like(ref)
+
+    def turn(rows):
+        turn_rows(
+            x1_ref.at[rows], att1.at[rows], cot_ref.at[rows], rows_ref, wa_ref, wup_ref,
+            wdown_ref, y_ref.at[rows], dmid_ref.at[rows], datt_ref.at[rows], gdown, gup, gproj,
+            wide, narrow1,
+        )
+
+    finish_saves(1)
+    for h in range(2):
+        fetch(1, h).start()
+    over_rows(turn)
+    put_y = copy(y_ref, y_far, out_sems.at[0])
+    attend_back(1, qkv1)
+    for h in range(2):
+        fetch(0, h).start()
+
+    def join(rows):
+        join_rows(
+            dqkv_ref.at[rows], x1_ref.at[rows], x_ref.at[rows], a_ref.at[rows], gp_ref.at[rows],
+            act_ref.at[rows], f_ref.at[rows], att0.at[rows], rows_ref, wa_ref, wup_ref, wdown_ref,
+            dmid_ref.at[rows], datt_ref.at[rows], gqkv, gdown, gup, gproj, wide, narrow1, narrow0,
+            bias,
+        )
+
+    over_rows(join)
+    share = rows_ref[ROW_SHARE : ROW_SHARE + 1, :]
+    for d in range(8):
+        rows = slice(SLAB * d, SLAB * (d + 1))
+        blocks[0, d, 3] = (gproj[rows, :] * share).astype(BF)
+        for g in range(4):
+            blocks[1, d, g] = (gup[rows, PART * g : PART * (g + 1)] * share).astype(BF)
+            first_row = SLAB * (4 * d + g)
+            blocks[2, d, g] = (gdown[first_row : first_row + SLAB, :] * share).astype(BF)
+    puts = [copy(blocks.at[1], gu_far, out_sems.at[1]), copy(blocks.at[2], gd_far, out_sems.at[2])]
+    attend_back(0, qkv0)
+
+    def last(rows):
+        dmid_ref[rows, :] = qkv_back(
+            mod_reader(rows_ref, 0), x_ref[rows, :].astype(F32), dmid_ref[rows, :],
+            dqkv_ref[rows, :], wa_ref, gqkv, narrow0, bias,
+        )
+
+    over_rows(last)
+    put_dx = copy(dmid_ref, dx_far, out_sems.at[3])
+    for d in range(8):
+        rows = slice(SLAB * d, SLAB * (d + 1))
+        for g in range(3):
+            blocks[0, d, g] = (gqkv[rows, PART * g : PART * (g + 1)] * share).astype(BF)
+    puts.append(copy(blocks.at[0], ga_far, out_sems.at[4]))
+
+    def put(first_row, value):
+        for j in range(value.shape[1] // 128):
+            vec_ref[first_row + j : first_row + j + 1, :] = (
+                value[:, 128 * j : 128 * j + 128] * share[:, 0:128]
+            )
+
+    put(0, bias[0:1, :D])
+    put(3, bias[0:1, 2 * D :])
+    put(6, narrow0[6:7, :] + narrow1[6:7, :])
+    put(9, wide[0:1, :])
+    put(21, narrow0[7:8, :] + narrow1[7:8, :])
+    for r in range(6):
+        put(24 + 3 * r, narrow0[r : r + 1, :])
+        put(42 + 3 * r, narrow1[r : r + 1, :])
+    vec_ref[60:64, :] = jnp.zeros((4, 128), F32)
+    for made in puts + [put_y, put_dx]:
+        made.wait()
+
+
+def block_pass(inputs, cotangent, rows, wa, wup, wdown):
+    length = inputs.shape[0]
+    vmem = pl.BlockSpec(memory_space=pltpu.VMEM)
+    hbm = pl.BlockSpec(memory_space=pl.ANY)
+    blocks = (8, 4, SLAB, PART)
+    weights = (ROLLOUT, HEADS, length, length)
+    y, dx, ga, gu, gd, vec, _ = pl.pallas_call(
+        block_kernel,
+        in_specs=[vmem, vmem, hbm, hbm, hbm, hbm],
+        out_specs=[hbm, hbm, hbm, hbm, hbm, vmem, hbm],
+        out_shape=[
+            jax.ShapeDtypeStruct((length, D), F32),
+            jax.ShapeDtypeStruct((length, D), F32),
+            jax.ShapeDtypeStruct(blocks, BF),
+            jax.ShapeDtypeStruct(blocks, BF),
+            jax.ShapeDtypeStruct(blocks, BF),
+            jax.ShapeDtypeStruct((64, 128), F32),
+            jax.ShapeDtypeStruct(weights, BF),
+        ],
+        scratch_shapes=[
+            pltpu.VMEM((D, FF), BF),
+            pltpu.VMEM((D, FF), BF),
+            pltpu.VMEM((FF, D), BF),
+            pltpu.VMEM((length, D), BF),
+            pltpu.VMEM((length, 3 * D), BF),
+            pltpu.VMEM((length, 3 * D), BF),
+            pltpu.VMEM((2, 2, length, length), BF),
+            pltpu.VMEM((length, D), BF),
+            pltpu.VMEM((length, D), BF),
+            *[pltpu.VMEM((length, D), F32)] * 5,
+            pltpu.VMEM((length, FF), F32),
+            pltpu.VMEM((length, FF), BF),
+            pltpu.VMEM((length, D), BF),
+            pltpu.VMEM((length, 3 * D), BF),
+            pltpu.VMEM((D, 3 * D), F32),
+            pltpu.VMEM((D, D), F32),
+            pltpu.VMEM((D, FF), F32),
+            pltpu.VMEM((FF, D), F32),
+            pltpu.VMEM((2, 128, length), BF),
+            pltpu.VMEM((8, FF), F32),
+            pltpu.VMEM((8, D), F32),
+            pltpu.VMEM((8, D), F32),
+            pltpu.VMEM((8, 3 * D), F32),
+            pltpu.VMEM((UNITS, *blocks), BF),
+            pltpu.SemaphoreType.DMA((4,)),
+            pltpu.SemaphoreType.DMA((2,)),
+            pltpu.SemaphoreType.DMA((5,)),
+        ],
+        compiler_params=pltpu.CompilerParams(vmem_limit_bytes=67043328),
+        name="block",
+    )(inputs, rows, wa, wup, wdown, cotangent)
+    return (y, dx, ga, gu, gd, vec)
+
+
 def step_embedding(moment):
     half_width = D // 2
     freqs = jnp.exp(-math.log(10000.0) * jnp.arange(half_width, dtype=F32) / half_width)
@@ -960,43 +1030,6 @@
     start = rollout_start.astype(F32)
     rows = [lead_rows + step_embedding(start + offset) for offset in range(ROLLOUT)]
     return jax.nn.silu(jnp.stack(rows, axis=1)).astype(BF)
-
-
-def block_pass(inputs, cotangent, rows, wa, wup, wdown):
-    block = inputs.shape[0]
-    blocks = (8, 4, SLAB, PART)
-    (qkv0,) = rows_call(first_kernel, "first", [inputs], [rows, wa], [(3 * D, BF)], [])
-    att0, p0 = attend(qkv0, block)
-    a0, gp0, act0, f0, x1, qkv1 = rows_call(
-        middle_kernel, "middle", [inputs, att0], [rows, wa, wup, wdown],
-        [(D, F32), (FF, F32), (FF, BF), (D, F32), (D, F32), (3 * D, BF)], [],
-    )
-    att1, p1 = attend(qkv1, block)
-    result, dmid1, datt1, gdown, gup, gproj, wide1, narrow1 = rows_call(
-        turn_kernel, "turn", [x1, att1, cotangent], [rows, wa, wup, wdown],
-        [(D, F32), (D, F32), (D, BF)],
-        [((FF, D), F32), ((D, FF), F32), ((D, D), F32), ((8, FF), F32), ((8, D), F32)],
-    )
-    dq, dk, dv = attend_back(qkv1, datt1, p1, block)
-    dmid0, datt0, gqkv, gproj, wide0, narrow1b, narrow0, bias1, gup_blocks, gdown_blocks = rows_call(
-        join_kernel, "join",
-        [dq, dk, dv, x1, dmid1, inputs, a0, gp0, act0, f0, att0],
-        [rows, wa, wup, wdown, gproj],
-        [(D, F32), (D, BF)],
-        [((D, 3 * D), F32), ((D, D), F32), ((8, FF), F32), ((8, D), F32), ((8, D), F32),
-         ((8, 3 * D), F32), (blocks, BF), (blocks, BF)],
-        [gdown, gup],
-        [pltpu.VMEM((FF, D), F32), pltpu.VMEM((D, FF), F32), pltpu.VMEM((FF, D), F32),
-         pltpu.VMEM((D, FF), F32), pltpu.SemaphoreType.DMA((2,))],
-    )
-    dq, dk, dv = attend_back(qkv0, datt0, p0, block)
-    input_grad, vec, gqkv_blocks = rows_call(
-        last_kernel, "last", [dq, dk, dv, inputs, dmid0],
-        [rows, wa, gqkv, gproj, wide1, narrow1, wide0, narrow1b, narrow0, bias1],
-        [(D, F32)], [((64, 128), F32), (blocks, BF)], (),
-        [pltpu.VMEM((D, 3 * D), F32), pltpu.VMEM((8, D), F32), pltpu.VMEM((8, 3 * D), F32)],
-    )
-    return (result, input_grad, gqkv_blocks, gup_blocks, gdown_blocks, vec)
 
 
 def plain_gather(group_interval, counts, rollout_start, lead_table, masters):

time: 217 us -> 188 us (0.87)
  Pallas kernels: 210 us -> 181 us
    pallas_call x9 -> x1, Pallas kernels: 134 us -> 105 us  [block_pass(): pl.pallas_call(block_kernel, in_specs=[vmem, vmem, hbm, hbm, hbm, hbm], o...]
where the time goes in v3:
time: 188 us
  Pallas kernels  181 us (96%)
  between operations  2.61 us (1%)
  local copies, waits for them, and re-layouts  2.49 us (1%)
    pallas_call x1, Pallas kernels, block_pass(): pl.pallas_call(block_kernel, in_specs=[vmem, vmem, hbm, hbm, hbm, hbm], o...  105 us
    pallas_call x1, Pallas kernels, reduce(): pl.pallas_call(reduce_kernel, in_specs=[smem, smem, vmem, vmem, hbm, hbm,...  41.1 us
    pallas_call x1, Pallas kernels, gather(): pl.pallas_call(gather_kernel, in_specs=[smem] * 3 + [vmem] * 7, out_specs...  28.8 us
    pallas_call x1, Pallas kernels, update(): pl.pallas_call(adam_kernel, in_specs=[vmem] * 18, out_specs=[vmem] * 20,...  6.33 us

profile of v3, /device:TPU:0, one launch (start us, length us, event | category | flops | bytes accessed | tf_op | source)
XLA Modules:
  0.0 187.8 jit_solution(2498961389830591581)
XLA Ops:
  0.7 1.3 pad_bitcast_fusion.bias_ref
  2.0 28.8 %gather.1 = (bf16[8,48,1536]{2,1,0:T(8,128)(2,1)}, bf16[8,48,1536]{2,1,0:T(8,128)(2,1)}, bf16[8,4,48,384]{3,2,1,0:T(8,128)(2,1)}, f32[32,384]{1,0:T(8,128)}) custom-call(s32[4]{0:T(128)} %start_ref.3, s32[4]{0:T(128)} %interval_ref.3, s32[4]{0:T(128)} %counts_ref.1, f32[3,384]{1,0:T(4,128)} %lead_ref.3, f32[432,128]{1,0:T(8,128)} %bitcast.57, ...), custom_call_target="tpu_custom_call" | custom-call | tf_op jit(solution)/shard_map/gather/pallas_call | solution.py:478
  30.7 105.1 %block.1 = (f32[1024,384]{1,0:T(8,128)}, f32[1024,384]{1,0:T(8,128)}, bf16[8,4,48,384]{3,2,1,0:T(8,128)(2,1)}, bf16[8,4,48,384]{3,2,1,0:T(8,128)(2,1)}, bf16[8,4...) custom-call(bf16[1024,384]{1,0:T(8,128)(2,1)} %x_ref.1, ...), custom_call_target="tpu_custom_call" | custom-call | tf_op jit(solution)/shard_map/block/pallas_call | solution.py:972
  135.8 0.0 copy-start
  135.8 0.0 copy-start.1
  135.9 0.0 copy-start.2
  135.9 41.1 %reduce.1 = (bf16[3,4,48,384]{3,2,1,0:T(8,128)(2,1)}, f32[864,128]{1,0:T(8,128)}, f32[48,128]{1,0:T(8,128)}, f32[8,128]{1,0:T(8,128)}) custom-call(s32[4]{0:T(128)} %start_ref.3, s32[4]{0:T(128)} %interval_ref.3, f32[3,384]{1,0:T(4,128)} %lead_ref.3, f32[64,128]{1,0:T(8,128)} %get-tuple-element.67.vec_ref, bf16[4,2,4,48,384]{4,3,2,1,0:T(8,128)(2,1)} %bitcast.54, ...), custom_call_target="tpu_custom_call" | custom-call | tf_op jit(solution)/shard_map/reduce/pallas_call | solution.py:690
  177.0 1.2 slice.3
  178.9 0.0 copy-done
  178.9 0.0 copy-done.1
  178.9 0.0 copy-done.2
  179.0 1.4 fusion.1
  180.4 6.3 %adam.1 = (f32[432,128]{1,0:T(8,128)}, f32[144,128]{1,0:T(8,128)}, f32[576,128]{1,0:T(8,128)}, f32[576,128]{1,0:T(8,128)}, f32[864,128]{1,0:T(8,128)}, /*index=5...) custom-call(bf16[3,4,48,384]{3,2,1,0:T(8,128)(2,1)} %get-tuple-eleme, ...), custom_call_target="tpu_custom_call" | custom-call | tf_op jit(solution)/shard_map/adam/pallas_call | solution.py:775
Async XLA Ops:
  135.8 43.1 %copy-start = (f32[672]{0:T(1024)S(1)}, f32[672]{0:T(1024)}, u32[]{:S(2)}) copy-start(f32[672]{0:T(1024)} %param.35) | copy-start | bytes 8068
  135.8 43.1 %copy-start.1 = (f32[672]{0:T(1024)S(1)}, f32[672]{0:T(1024)}, u32[]{:S(2)}) copy-start(f32[672]{0:T(1024)} %param.41) | copy-start | bytes 8068
  135.9 43.1 %copy-start.2 = (f32[672]{0:T(1024)S(1)}, f32[672]{0:T(1024)}, u32[]{:S(2)}) copy-start(f32[672]{0:T(1024)} %param.47) | copy-start | bytes 8068

commit v4 on v1

v4 whole, which is shorter than its diff:
```python
import functools
import math

import jax
import jax.numpy as jnp
from jax import lax
from jax.experimental import pallas as pl
from jax.experimental.pallas import tpu as pltpu
from jax.sharding import PartitionSpec as P

D = 384
HEADS = 6
FF = 1536
ROLLOUT = 2
INTERVALS = 3
ADAM_STEP = 10
HEAD_DIM = 64
NPARAM = 2659584

norm_eps = 1e-06
learn_rate = 0.05
adam_eps = 1e-08

BF = jnp.bfloat16
F32 = jnp.float32
NN = (((1,), (0,)), ((), ()))
NT = (((1,), (1,)), ((), ()))
TN = (((0,), (0,)), ((), ()))

ROWS = 256
SLAB = 48
PART = 384
ROW_SHARE = 6
ROW_BQKV, ROW_BPROJ, ROW_BUP, ROW_BDOWN = 16, 19, 20, 24
SHIFT1, SCALE1, GATE1, SHIFT2, SCALE2, GATE2 = range(6)


def dot(left, right, dims=NN):
    return lax.dot_general(left, right, dims, preferred_element_type=F32)


def layer_norm(stream):
    centred = stream - jnp.mean(stream, axis=-1, keepdims=True)
    inverse = lax.rsqrt(jnp.mean(centred * centred, axis=-1, keepdims=True) + norm_eps)
    return (centred * inverse, inverse)


def norm_back(normed, inverse, grad_out):
    mean_grad = jnp.mean(grad_out, axis=-1, keepdims=True)
    mean_prod = jnp.mean(grad_out * normed, axis=-1, keepdims=True)
    return inverse * (grad_out - mean_grad - normed * mean_prod)


def col_sum(value):
    return jnp.sum(value, axis=0, keepdims=True)


def modulated(normed, mods, scale_row, shift_row):
    return (normed * (1.0 + mods(scale_row)) + mods(shift_row)).astype(BF)


def mod_reader(mod_ref, step):
    return lambda row: mod_ref[pl.ds(8 * step + row, 1), :]


def gelu_pair(value):
    cdf = 0.5 + 0.5 * lax.erf(value * (2.0**-0.5))
    density = jnp.exp(-0.5 * value * value) * (1.0 / math.sqrt(2.0 * math.pi))
    return (value * cdf, cdf + value * density)


def side_by_side(ref, first, count):
    return jnp.concatenate([ref[row : row + 1, :] for row in range(first, first + count)], axis=1)


def first_rows(x, rows_ref, wa_ref):
    normed, _ = layer_norm(x.astype(F32))
    hidden = modulated(normed, mod_reader(rows_ref, 0), SCALE1, SHIFT1)
    qkv = dot(hidden, wa_ref[:, : 3 * D]) + side_by_side(rows_ref, ROW_BQKV, 3)
    return qkv.astype(BF)


def middle_rows(
    x_ref, att_ref, rows_ref, wa_ref, wup_ref, wdown_ref,
    a_refs, gp_ref, act_refs, f_ref, next_ref, qkv_ref,
):
    mods = mod_reader(rows_ref, 0)
    later = mod_reader(rows_ref, 1)
    branch = dot(att_ref[...], wa_ref[:, 3 * D :]) + mods(ROW_BPROJ)
    for part, ref in enumerate(a_refs):
        ref[...] = branch[:, 128 * part : 128 * (part + 1)]
    middle = x_ref[...].astype(F32) + mods(GATE1) * branch
    normed, _ = layer_norm(middle)
    hidden = modulated(normed, mods, SCALE2, SHIFT2)
    upward = dot(hidden, wup_ref[...]) + side_by_side(rows_ref, ROW_BUP, 4)
    act, slope = gelu_pair(upward)
    gp_ref[...] = slope
    act = act.astype(BF)
    for part, ref in enumerate(act_refs):
        ref[...] = act[:, PART * part : PART * (part + 1)]
    branch = dot(act, wdown_ref[...]) + mods(ROW_BDOWN)
    f_ref[...] = branch
    stream = middle + mods(GATE2) * branch
    next_ref[...] = stream
    normed, _ = layer_norm(stream)
    hidden = modulated(normed, later, SCALE1, SHIFT1)
    qkv = dot(hidden, wa_ref[:, : 3 * D]) + side_by_side(rows_ref, ROW_BQKV, 3)
    qkv_ref[...] = qkv.astype(BF)


def ffn_back(
    mods, grad, branch_two, act, slope, normed, inverse, hidden, branch_one, att,
    wa_ref, wup_ref, wdown_ref, gdown_ref, gup_ref, gproj_ref, wide_ref, narrow_ref,
    dmid_ref, datt_ref,
):
    df = (mods(GATE2) * grad).astype(BF)
    narrow_ref[pl.ds(GATE2, 1), :] += col_sum(grad * branch_two)
    narrow_ref[pl.ds(7, 1), :] += col_sum(df.astype(F32))
    gdown_ref[...] += dot(act, df, TN)
    dact = dot(df, wdown_ref[...], NT)
    du = (dact * slope).astype(BF)
    wide_ref[pl.ds(0, 1), :] += col_sum(du.astype(F32))
    gup_ref[...] += dot(hidden, du, TN)
    dh = dot(du, wup_ref[...], NT)
    narrow_ref[pl.ds(SHIFT2, 1), :] += col_sum(dh)
    narrow_ref[pl.ds(SCALE2, 1), :] += col_sum(dh * normed)
    dmid = grad + norm_back(normed, inverse, dh * (1.0 + mods(SCALE2)))
    dmid_ref[...] = dmid
    da = (mods(GATE1) * dmid).astype(BF)
    narrow_ref[pl.ds(GATE1, 1), :] += col_sum(dmid * branch_one)
    narrow_ref[pl.ds(6, 1), :] += col_sum(da.astype(F32))
    gproj_ref[...] += dot(att, da, TN)
    datt_ref[...] = dot(da, wa_ref[:, 3 * D :], NT).astype(BF)


def turn_rows(
    x_ref, att_ref, cot_ref, rows_ref, wa_ref, wup_ref, wdown_ref,
    out_ref, dmid_ref, datt_ref, gdown_ref, gup_ref, gproj_ref, wide_ref, narrow_ref,
):
    mods = mod_reader(rows_ref, 1)
    shared = mod_reader(rows_ref, 0)
    att = att_ref[...]
    branch_one = dot(att, wa_ref[:, 3 * D :]) + shared(ROW_BPROJ)
    middle = x_ref[...] + mods(GATE1) * branch_one
    normed, inverse = layer_norm(middle)
    hidden = modulated(normed, mods, SCALE2, SHIFT2)
    upward = dot(hidden, wup_ref[...]) + side_by_side(rows_ref, ROW_BUP, 4)
    act, slope = gelu_pair(upward)
    act = act.astype(BF)
    branch_two = dot(act, wdown_ref[...]) + shared(ROW_BDOWN)
    out_ref[...] = middle + mods(GATE2) * branch_two
    ffn_back(
        mods, cot_ref[...].astype(F32), branch_two, act, slope, normed, inverse, hidden,
        branch_one, att, wa_ref, wup_ref, wdown_ref, gdown_ref, gup_ref, gproj_ref,
        wide_ref, narrow_ref, dmid_ref, datt_ref,
    )


def qkv_back(mods, stream, dmid, dqkv, wa_ref, gqkv_ref, narrow_ref, bias_ref):
    normed, inverse = layer_norm(stream)
    hidden = modulated(normed, mods, SCALE1, SHIFT1)
    bias_ref[pl.ds(0, 1), :] += col_sum(dqkv.astype(F32))
    gqkv_ref[...] += dot(hidden, dqkv, TN)
    dh = dot(dqkv, wa_ref[:, : 3 * D], NT)
    narrow_ref[pl.ds(SHIFT1, 1), :] += col_sum(dh)
    narrow_ref[pl.ds(SCALE1, 1), :] += col_sum(dh * normed)
    return dmid + norm_back(normed, inverse, dh * (1.0 + mods(SCALE1)))


def join_rows(
    dqkv_ref, x1_ref, x0_ref, a_refs, gp_ref, act_refs, f_ref, att_ref,
    rows_ref, wa_ref, wup_ref, wdown_ref,
    dmid_ref, datt_ref, gqkv_ref, gdown_ref, gup_ref, gproj_ref, wide_ref, narrow1_ref,
    narrow_ref, bias_ref,
):
    grad = qkv_back(
        mod_reader(rows_ref, 1), x1_ref[...], dmid_ref[...], dqkv_ref[...], wa_ref, gqkv_ref,
        narrow1_ref, bias_ref,
    )
    mods = mod_reader(rows_ref, 0)
    branch_one = jnp.concatenate([ref[...] for ref in a_refs], axis=1)
    middle = x0_ref[...].astype(F32) + mods(GATE1) * branch_one
    normed, inverse = layer_norm(middle)
    hidden = modulated(normed, mods, SCALE2, SHIFT2)
    ffn_back(
        mods, grad, f_ref[...], jnp.concatenate([ref[...] for ref in act_refs], axis=1), gp_ref[...], normed, inverse, hidden,
        branch_one, att_ref[...], wa_ref, wup_ref, wdown_ref, gdown_ref, gup_ref, gproj_ref,
        wide_ref, narrow_ref, dmid_ref, datt_ref,
    )


def head_lanes(rows):
    lane = lax.broadcasted_iota(jnp.int32, (rows, 2 * HEAD_DIM), 1)
    return (lane < HEAD_DIM, lane >= HEAD_DIM)


def turned_heads(rows_f32, out_ref):
    turned = jnp.transpose(rows_f32)
    row = lax.broadcasted_iota(jnp.int32, turned.shape, 0)
    out_ref[0] = jnp.where(row < HEAD_DIM, turned, 0.0).astype(BF)
    out_ref[1] = jnp.where(row >= HEAD_DIM, turned, 0.0).astype(BF)


score_scale = HEAD_DIM**-0.5


def attend_pair(q, k_ref, v, o_ref, p_ref, vt_ref):
    turned_heads(v.astype(F32), vt_ref)
    queries = q * BF(score_scale)
    mixed = None
    for half, lanes in enumerate(head_lanes(queries.shape[0])):
        scores = dot(k_ref[...], jnp.where(lanes, queries, BF(0)), NT)
        top = jnp.max(scores, axis=0, keepdims=True)
        weights = jnp.exp(scores - top)
        total = jnp.sum(weights, axis=0, keepdims=True)
        low = (weights * (1.0 / total)).astype(BF)
        p_ref[half] = low
        part = dot(vt_ref[half], low)
        mixed = part if mixed is None else mixed + part
    o_ref[...] = jnp.transpose(mixed).astype(BF)


def attend_back_pair(q, k, v_ref, grads, p_ref, dq_ref, dk_ref, dv_ref, kt_ref):
    turned_heads(k.astype(F32) * score_scale, kt_ref)
    queries = q * BF(score_scale)
    dq_turned, dk, dv = (None, None, None)
    for half, lanes in enumerate(head_lanes(queries.shape[0])):
        grad = jnp.where(lanes, grads, BF(0))
        query = jnp.where(lanes, queries, BF(0))
        low = p_ref[half]
        weight_grad = dot(v_ref[...], grad, NT)
        weights = low.astype(F32)
        delta = jnp.sum(weights * weight_grad, axis=0, keepdims=True)
        score_grad = (weights * (weight_grad - delta)).astype(BF)
        parts = (dot(kt_ref[half], score_grad), dot(score_grad, query), dot(low, grad))
        if half == 0:
            dq_turned, dk, dv = parts
        else:
            dq_turned, dk, dv = (dq_turned + parts[0], dk + parts[1], dv + parts[2])
    dq_ref[...] = jnp.transpose(dq_turned).astype(BF)
    dk_ref[...] = dk.astype(BF)
    dv_ref[...] = dv.astype(BF)


MESH_ID = pl.DeviceIdType.MESH
GROUPS = 4
LAYERS = 4
UNITS = 3
HALF = 768


class Place:
    def __init__(self):
        self.grp = lax.axis_index("grp")
        self.dp = lax.axis_index("dp")
        self.z = self.dp // 2
        self.core = self.dp % 2

    def sibling(self):
        return (self.grp, 2 * self.z + 1 - self.core)

    def along_grp(self, step):
        return (lax.rem(self.grp + step, GROUPS), self.dp)

    def along_z(self, step):
        return (self.grp, 2 * lax.rem(self.z + step, LAYERS) + self.core)

    def across(self, step):
        return (self.grp, 2 * lax.rem(self.z + step, LAYERS) + 1 - self.core)


def greet(peers):
    barrier = pltpu.get_barrier_semaphore()
    for peer in peers:
        pl.semaphore_signal(barrier, inc=1, device_id=peer, device_id_type=MESH_ID)
    return lambda: pl.semaphore_wait(barrier, len(peers))


def remote(src, dst, sems, index, peer):
    send_sem, recv_sem = sems
    return pltpu.make_async_remote_copy(
        src_ref=src, dst_ref=dst, send_sem=send_sem.at[index], recv_sem=recv_sem.at[index],
        device_id=peer, device_id_type=MESH_ID,
    )


def condition_rows(moments, intervals, lead_ref):
    shape = (8, D)
    row = lax.broadcasted_iota(jnp.int32, shape, 0)
    lane = lax.broadcasted_iota(jnp.int32, shape, 1)
    moment = jnp.zeros(shape, F32)
    chosen = jnp.zeros(shape, jnp.int32)
    for index, (value, interval) in enumerate(zip(moments, intervals)):
        moment = jnp.where(row == index, value.astype(F32), moment)
        chosen = jnp.where(row == index, interval, chosen)
    lead = jnp.zeros(shape, F32)
    for choice in range(INTERVALS):
        picked = jnp.broadcast_to(lead_ref[choice : choice + 1, :], shape)
        lead = jnp.where(chosen == choice, picked, lead)
    half_width = D // 2
    place = jnp.where(lane < half_width, lane, lane - half_width).astype(F32)
    angles = moment * jnp.exp(place * (-math.log(10000.0) / half_width))
    wave = jnp.where(lane < half_width, jnp.sin(angles), jnp.cos(angles))
    condition = lead + wave
    return (condition / (1.0 + jnp.exp(-condition))).astype(BF).astype(F32)


def span(start, size):
    return pl.ds(pl.multiple_of(start, SLAB), size)


def local(src, dst, sem):
    made = pltpu.make_async_copy(src, dst, sem)
    made.start()
    return made


class Alone:
    def __init__(self, refs):
        self.refs = refs

    def begin(self):
        r = self.refs
        sems = r.in_sems
        first = [local(r.wa_far, r.wa, sems.at[0]), local(r.rows_far, r.rows, sems.at[3])]
        self.later = [local(r.wup_far, r.wup, sems.at[1]), local(r.wdown_far, r.wdown, sems.at[2])]
        for made in first:
            made.wait()

    def after_first(self):
        pass

    def after_attend_pair(self, h):
        pass

    def before_middle(self):
        for made in self.later:
            made.wait()

    def after_join(self):
        fill_blocks(self.refs, (1, 2))

    def after_back_pair(self, h):
        pass

    def after_last(self):
        r = self.refs
        fill_blocks(r, (0,))
        fill_vec(r)
        puts = [local(r.blocks, r.blocks_far, r.in_sems.at[0]), local(r.vec, r.vec_far, r.in_sems.at[1])]
        for made in puts:
            made.wait()


def fill_blocks(refs, units):
    share = refs.rows[ROW_SHARE : ROW_SHARE + 1, :]
    for d in range(8):
        own = slice(SLAB * d, SLAB * (d + 1))
        for g in range(4):
            columns = slice(PART * g, PART * (g + 1))
            first = HALF * (d % 2) + 4 * SLAB * g + SLAB * (d // 2)
            there = slice(first, first + SLAB)
            for unit in units:
                if unit == 0:
                    value = refs.gqkv[own, columns] if g < 3 else refs.gproj[own, :]
                elif unit == 1:
                    value = refs.gup[own, columns]
                else:
                    value = refs.gdown[SLAB * (4 * d + g) : SLAB * (4 * d + g + 1), :]
                refs.blocks[unit, there, :] = (value * share).astype(BF)


def fill_vec(refs):
    share = refs.rows[ROW_SHARE : ROW_SHARE + 1, :]

    def put(first_row, value):
        for j in range(value.shape[1] // 128):
            refs.vec[first_row + j : first_row + j + 1, :] = (
                value[:, 128 * j : 128 * j + 128] * share[:, 0:128]
            )

    bias, wide, narrow0, narrow1 = (refs.bias, refs.wide, refs.narrow0, refs.narrow1)
    put(0, bias[0:1, :D])
    put(3, bias[0:1, 2 * D :])
    put(6, narrow0[6:7, :] + narrow1[6:7, :])
    put(9, wide[0:1, :])
    put(21, narrow0[7:8, :] + narrow1[7:8, :])
    for r in range(6):
        put(24 + 3 * r, narrow0[r : r + 1, :])
        put(42 + 3 * r, narrow1[r : r + 1, :])
    refs.vec[60:64, :] = jnp.zeros((4, 128), F32)


class Together:
    steps = range(1, 4)

    def __init__(self, refs):
        self.refs = refs
        self.at = Place()

    def start(self, copy):
        copy.start()


    def whole(self, unit):
        return (self.refs.wa, self.refs.wup, self.refs.wdown)[unit]

    def part(self, unit, owner, grp):
        if unit == 2:
            return self.whole(2).at[span(4 * SLAB * owner + SLAB * grp, SLAB), :]
        return self.whole(unit).at[
            span(SLAB * owner, SLAB), pl.ds(pl.multiple_of(PART * grp, 128), PART)
        ]

    def slab(self, unit, owner):
        if unit == 2:
            return self.whole(2).at[span(4 * SLAB * owner, 4 * SLAB), :]
        return self.whole(unit).at[span(SLAB * owner, SLAB), :]

    def owner(self, k):
        return 2 * lax.rem(self.at.z + LAYERS - k, LAYERS) + self.at.core

    def gather_z(self, unit, k):
        own = self.part(unit, self.at.dp, self.at.grp)
        return remote(own, own, self.refs.gz, (unit, k - 1), self.at.along_z(k))

    def gather_grp(self, unit, k, m):
        part = self.part(unit, self.owner(k), self.at.grp)
        return remote(part, part, self.refs.gx, (unit, k - 1, m - 1), self.at.along_grp(m))

    def gather_sibling(self, unit, k):
        slab = self.slab(unit, self.owner(k) if k else self.at.dp)
        return remote(slab, slab, self.refs.gs, (unit, k), self.at.sibling())

    def launch(self, unit):
        for k in self.steps:
            self.start(self.gather_z(unit, k))
        self.start(self.gather_sibling(unit, 0))

    def forward_grp(self, unit):
        for k in self.steps:
            self.gather_z(unit, k).wait_recv()
            for m in self.steps:
                self.start(self.gather_grp(unit, k, m))

    def forward_sibling(self, unit):
        for k in self.steps:
            for m in self.steps:
                self.gather_grp(unit, k, m).wait_recv()
            self.start(self.gather_sibling(unit, k))

    def finish_sibling(self, unit):
        for k in range(4):
            self.gather_sibling(unit, k).wait_recv()

    def small(self, index):
        r, at = (self.refs, self.at)
        if index == 0:
            return remote(r.part_own, r.part_sib, r.gm, 0, at.sibling())
        if index == 1:
            own = r.bias_slot.at[at.z, at.core]
            return remote(own, own, r.gm, 1, at.sibling())
        if index < 5:
            own = r.part_z.at[at.z]
            return remote(own, own, r.gm, index, at.along_z(index - 1))
        own = r.bias_slot.at[at.z]
        return remote(own, own, r.gm, index, at.along_z(index - 4))

    def begin(self):
        r, at, steps = (self.refs, self.at, self.steps)
        stage = {
            "qkv": r.a.at[0:432], "proj": r.a.at[432:576], "ada": r.a.at[1728:2592],
            "up": r.a.at[576:1152], "down": r.a.at[1152:1728],
        }
        loads = {
            name: local(r.masters[name], stage[name], r.in_sems.at[index])
            for index, name in enumerate(stage)
        }
        ready = greet(
            [at.sibling()]
            + [at.along_grp(k) for k in steps]
            + [at.along_z(k) for k in steps]
            + [at.across(k) for k in steps]
        )

        def fill(unit, source, count, offset, first=0):
            for j in range(count):
                value = source[pl.ds(first + j, SLAB, stride=count), :].astype(BF)
                where = offset + 128 * j
                if unit == 2:
                    rows = span(4 * SLAB * at.dp + offset, SLAB)
                    where = 128 * j
                else:
                    rows = span(SLAB * at.dp, SLAB)
                self.whole(unit)[rows, where : where + 128] = value

        loads["qkv"].wait()
        fill(0, stage["qkv"], 9, 0)
        loads["proj"].wait()
        fill(0, stage["proj"], 3, 3 * D)
        ready()
        self.launch(0)

        moment, interval = (r.start[at.grp], r.interval[at.grp])
        r.cond_t[...] = jnp.transpose(
            condition_rows([moment + s for s in range(ROLLOUT)], [interval] * ROLLOUT, r.lead)
        )
        own_cond = r.cond_t[span(SLAB * at.dp, SLAB), :]
        columns = [jnp.broadcast_to(own_cond[:, s : s + 1], (SLAB, 128)) for s in range(ROLLOUT)]
        loads["ada"].wait()
        for j in range(18):
            rows = stage["ada"][pl.ds(j, SLAB, stride=18), :].astype(BF).astype(F32)
            for s in range(ROLLOUT):
                r.part_own[18 * s + j : 18 * s + j + 1, :] = col_sum(rows * columns[s])
        r.part_own[36:40, :] = jnp.zeros((4, 128), F32)
        lane = lax.broadcasted_iota(jnp.int32, (8, 128), 1)
        shift = lax.rem(32 * at.dp, 128)
        turned = pltpu.roll(r.bias_own[...].astype(BF).astype(F32), shift, axis=1)
        above = pltpu.roll(turned, 1, axis=0)
        r.bias_slot[at.z, at.core] = jnp.where(lane >= shift, turned, above)
        self.start(self.small(0))
        self.start(self.small(1))

        loads["up"].wait()
        fill(1, stage["up"], 12, 0)
        loads["down"].wait()
        for g in range(GROUPS):
            fill(2, stage["down"], 3, SLAB * g, 3 * SLAB * g)

        self.small(0).wait_recv()
        self.small(1).wait_recv()
        r.part_z[at.z] = r.part_own[...] + r.part_sib[...]
        for index in range(2, 8):
            self.start(self.small(index))
        self.forward_grp(0)
        self.launch(1)
        self.launch(2)

        for index in range(2, 8):
            self.small(index).wait_recv()
        total = r.part_z[0] + r.part_z[1] + r.part_z[2] + r.part_z[3]
        r.bias_full[...] = jnp.zeros_like(r.bias_full)
        for d in range(2 * LAYERS):
            first = 672 * d // 128
            r.bias_full[first : first + 7, :] += r.bias_slot[d // 2, d % 2, 0:7, :]
        counts = [r.counts[g].astype(F32) for g in range(GROUPS)]
        own_count = r.counts[at.grp].astype(F32)
        share = jnp.full((1, D), GROUPS * own_count) / jnp.full((1, D), sum(counts[1:], counts[0]))

        def put(row, value):
            r.rows[row : row + 1, :] = value

        def joined(first):
            return jnp.concatenate(
                [r.bias_full[first + j : first + j + 1, :] for j in range(3)], axis=1
            )

        for s in range(ROLLOUT):
            for row in range(6):
                first = 18 * s + 3 * row
                mod = jnp.concatenate([total[first + j : first + j + 1, :] for j in range(3)], axis=1)
                put(8 * s + row, mod + joined(24 + 3 * row))
            put(8 * s + 6, share)
            put(8 * s + 7, share)
        put(ROW_BQKV, joined(0))
        put(ROW_BQKV + 1, jnp.zeros((1, D), F32))
        put(ROW_BQKV + 2, joined(3))
        put(ROW_BPROJ, joined(6))
        for j in range(4):
            put(ROW_BUP + j, joined(9 + 3 * j))
        put(ROW_BDOWN, joined(21))
        r.rows[25:32, :] = jnp.zeros((7, D), F32)
        self.forward_sibling(0)
        self.finish_sibling(0)

    def after_first(self):
        self.forward_grp(1)
        self.forward_grp(2)

    def after_attend_pair(self, h):
        @pl.when(h == 1)
        def _():
            self.forward_sibling(1)

    def before_middle(self):
        self.forward_sibling(2)
        self.finish_sibling(1)
        self.finish_sibling(2)


    def got(self, unit, name, k=1):
        first = {"sib": 0, "grp": HALF, "z": HALF + 12 * SLAB, "piece": HALF + 15 * SLAB}[name]
        first += {"sib": 0, "grp": 4 * SLAB, "z": SLAB, "piece": 0}[name] * (k - 1)
        size = {"sib": HALF, "grp": 4 * SLAB, "z": SLAB, "piece": 4 * SLAB}[name]
        if unit == 0:
            if name in ("sib", "piece"):
                first = 0 if name == "sib" else HALF
                return self.refs.att0.at[first : first + size]
            first += 2 * 35 * SLAB - HALF
        else:
            first += 35 * SLAB * (unit - 1)
        return self.refs.act.at[first : first + size]

    def mine(self, unit):
        return self.refs.blocks.at[unit, span(HALF * self.at.core, HALF), :]

    def sum_sibling(self, unit):
        src = self.refs.blocks.at[unit, span(HALF * (1 - self.at.core), HALF), :]
        return remote(src, self.got(unit, "sib"), self.refs.rs, unit, self.at.sibling())

    def sum_grp(self, unit, k):
        peer = self.at.along_grp(k)
        src = self.mine(unit).at[span(4 * SLAB * peer[0], 4 * SLAB), :]
        return remote(src, self.got(unit, "grp", k), self.refs.rx, (unit, k - 1), peer)

    def sum_z(self, unit, k):
        there = lax.rem(self.at.z + k, LAYERS)
        src = self.mine(unit).at[span(4 * SLAB * self.at.grp + SLAB * there, SLAB), :]
        return remote(src, self.got(unit, "z", k), self.refs.rz, (unit, k - 1), self.at.along_z(k))

    def share_piece(self, unit, k):
        own = self.got(unit, "piece").at[span(SLAB * self.at.grp, SLAB), :]
        return remote(own, own, self.refs.ra, (unit, k - 1), self.at.along_grp(k))

    def add_sibling(self, unit):
        self.sum_sibling(unit).wait_recv()
        mine, got = (self.mine(unit), self.got(unit, "sib"))

        def add(i, carry):
            rows = span(SLAB * i, SLAB)
            mine[rows, :] = (mine[rows, :].astype(F32) + got[rows, :].astype(F32)).astype(BF)
            return carry

        lax.fori_loop(0, 16, add, 0)
        for k in self.steps:
            self.start(self.sum_grp(unit, k))

    def add_grp(self, unit):
        for k in self.steps:
            self.sum_grp(unit, k).wait_recv()
        mine = self.mine(unit).at[span(4 * SLAB * self.at.grp, 4 * SLAB), :]

        def add(i, carry):
            rows = span(SLAB * i, SLAB)
            value = mine[rows, :].astype(F32)
            for k in self.steps:
                value = value + self.got(unit, "grp", k)[rows, :].astype(F32)
            mine[rows, :] = value.astype(BF)
            return carry

        lax.fori_loop(0, 4, add, 0)
        for k in self.steps:
            self.start(self.sum_z(unit, k))

    def add_z(self, unit):
        for k in self.steps:
            self.sum_z(unit, k).wait_recv()
        mine = self.mine(unit).at[span(4 * SLAB * self.at.grp + SLAB * self.at.z, SLAB), :]
        value = mine[...].astype(F32)
        for k in self.steps:
            value = value + self.got(unit, "z", k)[...].astype(F32)
        value = value.astype(BF)
        self.got(unit, "piece")[span(SLAB * self.at.grp, SLAB), :] = value
        for k in self.steps:
            self.start(self.share_piece(unit, k))
        value = value.astype(F32)
        squares = col_sum(value * value)
        return squares[:, 0:128] + squares[:, 128:256] + squares[:, 256:384]

    def after_join(self):
        r, at = (self.refs, self.at)
        for peer in (
            [at.sibling()]
            + [at.along_grp(k) for k in self.steps]
            + [at.along_z(k) for k in self.steps]
        ):
            pl.semaphore_signal(r.joined, inc=1, device_id=peer, device_id_type=MESH_ID)
        fill_blocks(r, (1, 2))
        pl.semaphore_wait(r.joined, 7)
        self.start(self.sum_sibling(1))
        self.start(self.sum_sibling(2))

    def after_back_pair(self, h):
        @pl.when(h == 0)
        def _():
            self.add_sibling(1)
            self.add_sibling(2)

    def small_sum(self, index):
        r, at = (self.refs, self.at)
        if index == 0:
            return remote(r.vec, r.vec_sib, r.rv, 0, at.sibling())
        if index < 4:
            own = r.vec_z.at[at.z]
            return remote(own, own, r.rv, index, at.along_z(index))
        own = r.vec_g.at[at.grp]
        return remote(own, own, r.rv, index, at.along_grp(index - 3))

    def square_sum(self, index):
        r, at = (self.refs, self.at)
        if index < 7:
            peer = at.sibling()
            if index > 0:
                peer = at.along_z(index) if index < 4 else at.across(index - 3)
            own = r.square_d.at[at.dp]
        else:
            peer = at.along_grp(index - 6)
            own = r.square_g.at[at.grp]
        return remote(own, own, r.rq, index, peer)

    def after_last(self):
        r, at, steps = (self.refs, self.at, self.steps)
        fill_blocks(r, (0,))
        self.start(self.sum_sibling(0))
        fill_vec(r)
        self.start(self.small_sum(0))
        self.add_grp(1)
        moments = [r.start[g] + s for g in range(GROUPS) for s in range(ROLLOUT)]
        intervals = [r.interval[g] for g in range(GROUPS) for s in range(ROLLOUT)]
        r.cond_t[...] = jnp.transpose(condition_rows(moments, intervals, r.lead))
        self.small_sum(0).wait_recv()
        r.vec_z[at.z] = r.vec[...] + r.vec_sib[...]
        for index in steps:
            self.start(self.small_sum(index))
        self.add_sibling(0)
        self.add_grp(2)
        square = self.add_z(1)
        for index in steps:
            self.small_sum(index).wait_recv()
        r.vec_g[at.grp] = r.vec_z[0] + r.vec_z[1] + r.vec_z[2] + r.vec_z[3]
        for index in steps:
            self.start(self.small_sum(3 + index))
        square = square + self.add_z(2)
        self.add_grp(0)

        for index in steps:
            self.small_sum(3 + index).wait_recv()
        own_cond = r.cond_t[span(SLAB * at.dp, SLAB), :]
        columns = [jnp.broadcast_to(own_cond[:, k : k + 1], (SLAB, 128)) for k in range(8)]
        ada = r.a.at[0:864]

        def ada_tile(j, total):
            tile = jnp.zeros((SLAB, 128), F32)
            for g in range(GROUPS):
                for s in range(ROLLOUT):
                    row = r.vec_g[g, pl.ds(24 + 18 * s + j, 1), :]
                    tile = tile + columns[ROLLOUT * g + s] * row
            ada[pl.ds(j, SLAB, stride=18), :] = tile
            return total + col_sum(tile * tile)

        ada_square = lax.fori_loop(0, 18, ada_tile, jnp.zeros((1, 128), F32))
        puts = [local(ada, r.ada_far, r.in_sems.at[0])]
        vec_sum = r.vec_g[0] + r.vec_g[1] + r.vec_g[2] + r.vec_g[3]
        r.bias_out[0:24, :] = vec_sum[0:24]
        r.bias_out[24:42, :] = vec_sum[24:42] + vec_sum[42:60]
        r.bias_out[42:48, :] = jnp.zeros((6, 128), F32)

        square = square + 0.25 * ada_square + self.add_z(0)
        r.square_d[at.dp] = jnp.broadcast_to(square, (8, 128))
        for index in range(7):
            self.start(self.square_sum(index))
        for index in range(7):
            self.square_sum(index).wait_recv()
        total = r.square_d[0]
        for d in range(1, 2 * LAYERS):
            total = total + r.square_d[d]
        r.square_g[at.grp] = total
        for index in range(7, 10):
            self.start(self.square_sum(index))
        for unit in (1, 2, 0):
            for k in steps:
                self.share_piece(unit, k).wait_recv()
            puts.append(local(self.got(unit, "piece"), r.pieces_far.at[unit], r.in_sems.at[1 + unit]))
        for index in range(7, 10):
            self.square_sum(index).wait_recv()
        bias_sum = r.bias_out[...]
        total = r.square_g[0] + r.square_g[1] + r.square_g[2] + r.square_g[3]
        total = total + col_sum(bias_sum * bias_sum)
        r.square_out[...] = jnp.broadcast_to(jnp.sum(total, axis=1, keepdims=True), (8, 128))
        for made in puts:
            made.wait()
        self.drain()

    def drain(self):
        for unit in range(UNITS):
            for k in self.steps:
                self.gather_z(unit, k).wait_send()
                for m in self.steps:
                    self.gather_grp(unit, k, m).wait_send()
                self.sum_grp(unit, k).wait_send()
                self.sum_z(unit, k).wait_send()
                self.share_piece(unit, k).wait_send()
            for k in range(4):
                self.gather_sibling(unit, k).wait_send()
            self.sum_sibling(unit).wait_send()
        for index in range(8):
            self.small(index).wait_send()
        for index in range(7):
            self.small_sum(index).wait_send()
        for index in range(10):
            self.square_sum(index).wait_send()


correction = 1.0 - 0.5**ADAM_STEP
grad_limit = math.sqrt(NPARAM)


def adam(master, first, second, clipped, decay):
    first_new = 0.5 * first + 0.5 * clipped
    second_new = 0.5 * second + 0.5 * clipped * clipped
    update = first_new / correction / (jnp.sqrt(second_new / correction) + adam_eps)
    return (master - learn_rate * (update + decay * master), first_new, second_new)


def adam_kernel(*refs):
    piece_ref, ada_ref, square_ref = refs[:3]
    masters, firsts, seconds = (refs[3:8], refs[8:13], refs[13:18])
    news, first_news, second_news, copies = (refs[18:23], refs[23:28], refs[28:33], refs[33:38])
    flats = refs[38:42]
    norm = jnp.sqrt(square_ref[0:1, :])
    clip = grad_limit / jnp.maximum(norm, grad_limit)
    qkv, proj, up, down = flats
    for g in range(3):
        for j in range(3):
            qkv[pl.ds(3 * g + j, SLAB, stride=9), :] = piece_ref[0, SLAB * g : SLAB * (g + 1), 128 * j : 128 * j + 128].astype(F32)
    for j in range(3):
        proj[pl.ds(j, SLAB, stride=3), :] = piece_ref[0, 3 * SLAB :, 128 * j : 128 * j + 128].astype(F32)
    for g in range(GROUPS):
        for j in range(3):
            up[pl.ds(3 * g + j, SLAB, stride=12), :] = piece_ref[1, SLAB * g : SLAB * (g + 1), 128 * j : 128 * j + 128].astype(F32)
            down[pl.ds(3 * SLAB * g + j, SLAB, stride=3), :] = piece_ref[2, SLAB * g : SLAB * (g + 1), 128 * j : 128 * j + 128].astype(F32)
    for index, grad in enumerate((qkv, proj, up, down, ada_ref)):
        def chunk(i, carry):
            rows = pl.ds(pl.multiple_of(16 * i, 16), 16)
            new, first, second = adam(
                masters[index][rows, :], firsts[index][rows, :], seconds[index][rows, :],
                grad[rows, :] * clip, 0.1,
            )
            news[index][rows, :] = new
            first_news[index][rows, :] = first
            second_news[index][rows, :] = second
            copies[index][rows, :] = new.astype(BF)
            return carry

        lax.fori_loop(0, grad.shape[0] // 16, chunk, 0, unroll=3)


def update(pieces, ada, square, masters, firsts, seconds):
    flat = lambda arrays: [a.reshape(-1, 128) for a in arrays[:5]]
    masters, firsts, seconds = (flat(masters), flat(firsts), flat(seconds))
    vmem = pl.BlockSpec(memory_space=pltpu.VMEM)
    shapes = [m.shape for m in masters]
    outs = [jax.ShapeDtypeStruct(s, F32) for s in shapes] * 3
    outs += [jax.ShapeDtypeStruct(s, BF) for s in shapes]
    results = pl.pallas_call(
        adam_kernel,
        in_specs=[vmem] * 18,
        out_specs=[vmem] * 20,
        out_shape=outs,
        scratch_shapes=[pltpu.VMEM(s, F32) for s in shapes[:4]],
        name="adam",
    )(pieces, ada, square, *masters, *firsts, *seconds)
    results = [r.reshape(-1) for r in results]
    return (results[0:5], results[5:10], results[10:15], results[15:20])


class Refs:
    def __init__(self, names, refs):
        for name, ref in zip(names, refs, strict=True):
            setattr(self, name, ref)


MASTERS = ("qkv", "proj", "up", "down", "ada")


def block_kernel(names, hooked, *refs):
    r = Refs(names, refs)
    if hooked is Together:
        r.masters = {name: getattr(r, "far_" + name) for name in MASTERS}
        for name in ("gz", "gx", "gs", "gm", "rs", "rx", "rz", "ra", "rv", "rq"):
            setattr(r, name, (getattr(r, name + "_out"), getattr(r, name + "_in")))
    hooks = hooked(r)
    length = r.x.shape[0]
    pairs = HEADS // 2
    get_cot = local(r.cot_far, r.cot, r.out_sems.at[2])

    def over_rows(body):
        def step(i, carry):
            body(pl.ds(pl.multiple_of(i * ROWS, ROWS), ROWS))
            return carry

        lax.fori_loop(0, length // ROWS, step, 0)

    def columns(h, offset=0):
        return pl.ds(pl.multiple_of(offset + 128 * h, 128), 128)

    def over_pairs(body):
        def step(h, carry):
            body(h)
            return carry

        lax.fori_loop(0, pairs, step, 0)

    def act_refs(rows):
        first = rows.start
        return [
            r.act.at[pl.ds(pl.multiple_of(length * part + first, ROWS), ROWS)] for part in range(4)
        ]

    def a_refs(rows):
        first = rows.start
        return [
            r.a.at[pl.ds(pl.multiple_of(length * part + first, ROWS), ROWS)] for part in range(3)
        ]

    def save(step, h):
        slot = lax.rem(h, 2)
        return pltpu.make_async_copy(
            r.p.at[slot], r.p_far.at[step, pl.ds(2 * h, 2)], r.p_sems.at[slot]
        )

    def fetch(step, h):
        slot = lax.rem(h, 2)
        return pltpu.make_async_copy(
            r.p_far.at[step, pl.ds(2 * h, 2)], r.p.at[slot], r.p_sems.at[slot]
        )

    def attend(step, qkv, att, after):
        def body(h):
            @pl.when(h >= 2)
            def _():
                save(step, h - 2).wait()

            attend_pair(
                qkv[:, columns(h)], qkv.at[:, columns(h, D)], qkv[:, columns(h, 2 * D)],
                att.at[:, columns(h)], r.p.at[lax.rem(h, 2)], r.turned,
            )
            save(step, h).start()
            after(h)

        over_pairs(body)

    def finish_saves(step):
        for h in range(pairs - 2, pairs):
            save(step, h).wait()

    def attend_back(step, qkv, after):
        def body(h):
            fetch(step, h).wait()
            attend_back_pair(
                qkv[:, columns(h)], qkv[:, columns(h, D)], qkv.at[:, columns(h, 2 * D)],
                r.datt[:, columns(h)], r.p.at[lax.rem(h, 2)],
                r.dqkv.at[:, columns(h)], r.dqkv.at[:, columns(h, D)],
                r.dqkv.at[:, columns(h, 2 * D)], r.turned,
            )

            @pl.when(h + 2 < pairs)
            def _():
                fetch(step, h + 2).start()

            after(h)

        over_pairs(body)

    nothing = lambda h: None
    hooks.begin()

    def first(rows):
        r.qkv0[rows, :] = first_rows(r.x[rows, :], r.rows, r.wa)

    over_rows(first)
    hooks.after_first()
    attend(0, r.qkv0, r.att0, hooks.after_attend_pair)
    hooks.before_middle()

    def middle(rows):
        middle_rows(
            r.x.at[rows], r.att0.at[rows], r.rows, r.wa, r.wup, r.wdown,
            a_refs(rows), r.gp.at[rows], act_refs(rows), r.f.at[rows], r.x1.at[rows],
            r.qkv1.at[rows],
        )

    over_rows(middle)
    finish_saves(0)
    attend(1, r.qkv1, r.att1, nothing)

    for ref in (r.gqkv, r.gproj, r.gup, r.gdown, r.wide, r.narrow0, r.narrow1, r.bias):
        ref[...] = jnp.zeros_like(ref)

    def turn(rows):
        turn_rows(
            r.x1.at[rows], r.att1.at[rows], r.cot.at[rows], r.rows, r.wa, r.wup,
            r.wdown, r.y.at[rows], r.dmid.at[rows], r.datt.at[rows], r.gdown, r.gup, r.gproj,
            r.wide, r.narrow1,
        )

    finish_saves(1)
    for h in range(2):
        fetch(1, h).start()
    get_cot.wait()
    over_rows(turn)
    put_y = local(r.y, r.y_far, r.out_sems.at[0])
    attend_back(1, r.qkv1, nothing)
    for h in range(2):
        fetch(0, h).start()

    def join(rows):
        join_rows(
            r.dqkv.at[rows], r.x1.at[rows], r.x.at[rows], a_refs(rows), r.gp.at[rows],
            act_refs(rows), r.f.at[rows], r.att0.at[rows], r.rows, r.wa, r.wup, r.wdown,
            r.dmid.at[rows], r.datt.at[rows], r.gqkv, r.gdown, r.gup, r.gproj, r.wide, r.narrow1,
            r.narrow0, r.bias,
        )

    over_rows(join)
    hooks.after_join()
    attend_back(0, r.qkv0, hooks.after_back_pair)

    def last(rows):
        r.dmid[rows, :] = qkv_back(
            mod_reader(r.rows, 0), r.x[rows, :].astype(F32), r.dmid[rows, :],
            r.dqkv[rows, :], r.wa, r.gqkv, r.narrow0, r.bias,
        )

    over_rows(last)
    put_dx = local(r.dmid, r.dx_far, r.out_sems.at[1])
    hooks.after_last()
    put_y.wait()
    put_dx.wait()


def block_call(hooked, inputs, cotangent, extra_in, extra_out, extra_scratch, params):
    length = inputs.shape[0]
    vmem, hbm, dma = (pltpu.VMEM, pl.ANY, pltpu.SemaphoreType.DMA)
    weights = (ROLLOUT, HEADS, length, length)
    ins = [("x", inputs, vmem), ("cot_far", cotangent, hbm), *extra_in]
    outs = [
        ("y_far", (length, D), F32, hbm), ("dx_far", (length, D), F32, hbm),
        ("p_far", weights, BF, hbm), *extra_out,
    ]
    scratch = [
        ("wa", vmem((D, FF), BF)), ("wup", vmem((D, FF), BF)), ("wdown", vmem((FF, D), BF)),
        ("cot", vmem((length, D), BF)), ("qkv0", vmem((length, 3 * D), BF)),
        ("qkv1", vmem((length, 3 * D), BF)), ("p", vmem((2, 2, length, length), BF)),
        ("att0", vmem((length, D), BF)), ("att1", vmem((length, D), BF)),
        *[(name, vmem((length, D), F32)) for name in ("f", "x1", "dmid", "y")], ("a", vmem((3 * length, 128), F32)),
        ("gp", vmem((length, FF), F32)), ("act", vmem((4 * length, D), BF)),
        ("datt", vmem((length, D), BF)), ("dqkv", vmem((length, 3 * D), BF)),
        ("gqkv", vmem((D, 3 * D), F32)), ("gproj", vmem((D, D), F32)),
        ("gup", vmem((D, FF), F32)), ("gdown", vmem((FF, D), F32)),
        ("turned", vmem((2, 128, length), BF)), ("wide", vmem((8, FF), F32)),
        ("narrow0", vmem((8, D), F32)), ("narrow1", vmem((8, D), F32)),
        ("bias", vmem((8, 3 * D), F32)), ("blocks", vmem((UNITS, 2 * HALF, PART), BF)),
        ("rows", vmem((32, D), F32)), ("vec", vmem((64, 128), F32)),
        ("in_sems", dma((5,))), ("p_sems", dma((2,))), ("out_sems", dma((3,))),
        *extra_scratch,
    ]
    names = [item[0] for item in (*ins, *outs, *scratch)]
    return pl.pallas_call(
        functools.partial(block_kernel, names, hooked),
        in_specs=[pl.BlockSpec(memory_space=space) for _, _, space in ins],
        out_specs=[pl.BlockSpec(memory_space=space) for *_, space in outs],
        out_shape=[jax.ShapeDtypeStruct(shape, kind) for _, shape, kind, _ in outs],
        scratch_shapes=[kind for _, kind in scratch],
        compiler_params=pltpu.CompilerParams(vmem_limit_bytes=67043328, **params),
        name="block",
    )(*(array for _, array, _ in ins))


def block_alone(inputs, cotangent, rows, wa, wup, wdown):
    hbm = pl.ANY
    y, dx, _, blocks, vec = block_call(
        Alone, inputs, cotangent,
        [("rows_far", rows, hbm), ("wa_far", wa, hbm), ("wup_far", wup, hbm), ("wdown_far", wdown, hbm)],
        [("blocks_far", (UNITS, 2 * HALF, PART), BF, hbm), ("vec_far", (64, 128), F32, hbm)],
        [], {},
    )
    return (y, dx, blocks, vec)


def block_together(inputs, cotangent, start, interval, counts, lead, masters):
    vmem, hbm, smem, dma = (pltpu.VMEM, pl.ANY, pltpu.SMEM, pltpu.SemaphoreType.DMA)
    qkv, proj, up, down, ada, bias = masters
    far = [
        ("far_" + name, array.reshape(-1, 128), hbm)
        for name, array in zip(MASTERS, (qkv, proj, up, down, ada))
    ]
    bias = jnp.pad(bias, (0, 1024 - bias.shape[0])).reshape(8, 128)
    pairs_of = [
        ("gz", (UNITS, 3)), ("gx", (UNITS, 3, 3)), ("gs", (UNITS, 4)), ("gm", (8,)),
        ("rs", (UNITS,)), ("rx", (UNITS, 3)), ("rz", (UNITS, 3)), ("ra", (UNITS, 3)),
        ("rv", (7,)), ("rq", (10,)),
    ]
    y, dx, _, pieces, ada_grad, bias_sum, square = block_call(
        Together, inputs, cotangent,
        [("start", start, smem), ("interval", interval, smem), ("counts", counts, smem),
         ("lead", lead, vmem), ("bias_own", bias, vmem), *far],
        [("pieces_far", (UNITS, 4 * SLAB, PART), BF, hbm), ("ada_far", (18 * SLAB, 128), F32, hbm),
         ("bias_out", (48, 128), F32, vmem), ("square_out", (8, 128), F32, vmem)],
        [("cond_t", vmem((D, 8), F32)), ("part_own", vmem((40, 128), F32)),
         ("part_sib", vmem((40, 128), F32)), ("part_z", vmem((LAYERS, 40, 128), F32)),
         ("bias_slot", vmem((LAYERS, 2, 8, 128), F32)), ("bias_full", vmem((48, 128), F32)),
         ("vec_sib", vmem((64, 128), F32)), ("vec_z", vmem((LAYERS, 64, 128), F32)),
         ("vec_g", vmem((GROUPS, 64, 128), F32)), ("square_d", vmem((8, 8, 128), F32)),
         ("square_g", vmem((GROUPS, 8, 128), F32)), ("joined", pltpu.SemaphoreType.REGULAR),
         *[(name + end, dma(shape)) for name, shape in pairs_of for end in ("_out", "_in")]],
        dict(collective_id=0, has_side_effects=True),
    )
    return (y, dx, pieces, ada_grad, bias_sum, square)


def step_embedding(moment):
    half_width = D // 2
    freqs = jnp.exp(-math.log(10000.0) * jnp.arange(half_width, dtype=F32) / half_width)
    angles = moment[:, None] * freqs[None, :]
    return jnp.concatenate([jnp.sin(angles), jnp.cos(angles)], axis=1)


def all_conditions(group_interval, rollout_start, lead_table):
    chosen = group_interval[:, None] == jnp.arange(INTERVALS)[None, :]
    lead_rows = jnp.sum(jnp.where(chosen[:, :, None], lead_table[None], 0.0), axis=1)
    start = rollout_start.astype(F32)
    rows = [lead_rows + step_embedding(start + offset) for offset in range(ROLLOUT)]
    return jax.nn.silu(jnp.stack(rows, axis=1)).astype(BF)


def plain_gather(group_interval, counts, rollout_start, lead_table, masters):
    low = [master.astype(BF) for master in masters]
    owner = lax.axis_index("dp")
    group_index = lax.axis_index("grp")
    own_rows = D // lax.axis_size("dp")
    counts = counts.astype(F32)
    share = lax.axis_size("grp") * counts / jnp.sum(counts)
    share = lax.dynamic_index_in_dim(share, group_index, keepdims=False)
    conditions = all_conditions(group_interval, rollout_start, lead_table)
    owner_columns = lax.dynamic_slice_in_dim(conditions, owner * own_rows, own_rows, axis=2)
    own_condition = lax.dynamic_index_in_dim(owner_columns, group_index, keepdims=False)
    modulation = lax.psum(dot(own_condition, low[4].reshape(own_rows, 6 * D)), "dp")
    qkv, proj, up, down, bias = [
        lax.all_gather(low[index], "dp", axis=0, tiled=True) for index in (0, 1, 2, 3, 5)
    ]
    bias = bias.astype(F32)
    modulation = modulation + bias[4 * D + FF :][None]
    share_rows = jnp.broadcast_to(share, (ROLLOUT, 2, D))
    mods = jnp.concatenate([modulation.reshape(ROLLOUT, 6, D), share_rows], axis=1).reshape(-1, D)
    rows = jnp.concatenate(
        [mods, bias[:D][None], jnp.zeros((1, D), F32), bias[D : 4 * D + FF].reshape(-1, D),
         jnp.zeros((7, D), F32)]
    )
    wa = jnp.concatenate([qkv.reshape(D, 3 * D), proj.reshape(D, D)], axis=1)
    return (wa, up.reshape(D, FF), down.reshape(FF, D), rows, owner_columns)


def plain_update(owner_columns, vec, blocks, masters, firsts, seconds):
    owner = lax.axis_index("dp")
    vec = vec.reshape(-1)
    split = 4 * D + FF
    dmod = vec[split : split + ROLLOUT * 6 * D].reshape(ROLLOUT, 6 * D)
    dmod_all = lax.all_gather(lax.psum(dmod, "dp"), "grp")
    bias_sum = lax.psum(vec[:split], ("grp", "dp"))
    bias_sum = jnp.concatenate([bias_sum, jnp.sum(dmod_all, axis=(0, 1))])
    bias_rows = masters[5].shape[0]
    bias_grad = lax.dynamic_slice_in_dim(bias_sum, owner * bias_rows, bias_rows)
    ada_grad = jnp.einsum(
        "gsr,gsc->rc", owner_columns.astype(F32), dmod_all, precision=lax.Precision.HIGHEST
    )
    blocks = blocks.reshape(UNITS, 2, 4, LAYERS, SLAB, PART)
    flat_a, flat_up = [blocks[u].transpose(2, 0, 3, 1, 4).reshape(D, FF) for u in (0, 1)]
    flat_down = blocks[2].transpose(2, 0, 1, 3, 4)
    flat = [flat_a[:, : 3 * D], flat_a[:, 3 * D :], flat_up, flat_down]
    shares = []
    for grad in flat:
        summed = lax.psum(grad.reshape(-1), "grp").astype(F32)
        shares.append(lax.psum_scatter(summed, "dp", scatter_dimension=0, tiled=True))
    shares = shares + [ada_grad.reshape(-1), bias_grad]
    local_square = sum((jnp.sum(piece * piece) for piece in shares))
    grad_norm = jnp.sqrt(lax.psum(local_square, "dp"))
    clip = grad_limit / jnp.maximum(grad_norm, grad_limit)
    decays = [0.1, 0.1, 0.1, 0.1, 0.1, 0.0]
    results = [
        adam(master, first, second, grad * clip, decay)
        for master, first, second, grad, decay in zip(masters, firsts, seconds, shares, decays)
    ]
    news, first_news, second_news = zip(*results)
    return (grad_norm, *news, *first_news, *second_news, *(new.astype(BF) for new in news))


def per_device(
    inputs,
    cotangent,
    group_interval,
    sample_counts,
    rollout_start,
    lead_table,
    *state,
):
    masters, firsts, seconds = (state[0:6], state[6:12], state[12:18])
    fits = (
        lax.axis_size("dp") == 2 * LAYERS
        and lax.axis_size("grp") == GROUPS
        and inputs.shape[0] == 1024
    )
    if not fits:
        wa, wup, wdown, rows, owner_columns = plain_gather(
            group_interval, sample_counts, rollout_start, lead_table, masters
        )
        result, input_grad, blocks, vec = block_alone(inputs, cotangent, rows, wa, wup, wdown)
        rest = plain_update(owner_columns, vec, blocks, masters, firsts, seconds)
        return (result, input_grad, *rest)
    result, input_grad, pieces, ada_grad, bias_sum, square = block_together(
        inputs, cotangent, rollout_start, group_interval, sample_counts, lead_table, masters
    )
    news, first_news, second_news, copies = update(
        pieces, ada_grad, square, masters, firsts, seconds
    )
    grad_norm = jnp.sqrt(square[0, 0])
    clip = grad_limit / jnp.maximum(grad_norm, grad_limit)
    bias_rows = masters[5].shape[0]
    bias_grad = lax.dynamic_slice_in_dim(
        bias_sum.reshape(-1), lax.axis_index("dp") * bias_rows, bias_rows
    )
    new, first, second = adam(masters[5], firsts[5], seconds[5], bias_grad * clip, 0.0)
    return (
        result, input_grad, grad_norm, *news, new, *first_news, first, *second_news, second,
        *copies, new.astype(BF),
    )


def solution(mesh):
    rows = P(("grp", "dp"), None)
    return jax.shard_map(
        per_device,
        mesh=mesh,
        in_specs=(rows, rows, P(), P(), P(), P(), *[P("dp")] * 18),
        out_specs=(rows, rows, P(), *[P("dp")] * 24),
        check_vma=False,
    )
```

time: 562 us -> 165 us (0.29); the launches traced: 555 us -> 165 us
  blocking collectives: 294 us -> 0 us
  waiting for transfers between devices: 50.1 us -> 0 us
  other arithmetic: 30.3 us -> 1.4 us
  Pallas kernels: 134 us -> 155 us
  between operations: 23.2 us -> 2.61 us
  local copies, waits for them, and re-layouts: 21 us -> 5.62 us
    unnamed x2 -> x0, blocking collectives: 176 us -> none
    psum x3 -> x0, blocking collectives: 79.5 us -> none  [the longest x1 39.3 us: per_device(): bias_sum = lax.psum(vectors, ('grp', 'dp'))]
    psum x1 -> x0, waiting for transfers between devices: 50.1 us -> none  [per_device(): summed = lax.psum((grad * share).astype(BF).reshape(-1), 'grp').astype(F32)]
    all_gather x3 -> x0, blocking collectives: 38.8 us -> none  [the longest x2 30.3 us: per_device(): lax.all_gather(low[index], 'dp', axis=0, tiled=True)]
    pallas_call x9 -> x2, Pallas kernels: 134 us -> 155 us  [the longest x1 149 us: block_call(): pl.pallas_call(functools.partial(block_kernel, names, hooked), in_specs=[...]
    convert_element_type x18 -> x1, other arithmetic: 19.7 us -> 1.4 us  [per_device(): new.astype(BF)]
    reshape x11 -> x1, local copies, waits for them, and re-layouts: 16.9 us -> 1.28 us  [block_together(): bias = jnp.pad(bias, (0, 1024 - bias.shape[0])).reshape(8, 128)]
  transfers between devices with their start and end apart: 3 -> 0, of which waited for: 1 -> 0; matrix products, arithmetic and copies ran while one was open for 4% -> 0% of each run, Pallas kernels for 3% -> 0%
where the time goes in v4:
time: 165 us
  Pallas kernels  155 us (94%)
  local copies, waits for them, and re-layouts  5.62 us (3%)
  between operations  2.61 us (2%)
    pallas_call x1, Pallas kernels, block_call(): pl.pallas_call(functools.partial(block_kernel, names, hooked), in_specs=[...  149 us
    pallas_call x1, Pallas kernels, update(): pl.pallas_call(adam_kernel, in_specs=[vmem] * 18, out_specs=[vmem] * 20,...  6.53 us

profile of v4, /device:TPU:0, one launch (start us, length us, event | category | flops | bytes accessed | tf_op | source)
XLA Modules:
  0.0 164.7 jit_solution(5055161515840506576)
XLA Ops:
  0.7 1.3 pad_bitcast_fusion.refs_6_
  2.0 148.6 %block.1 = (f32[1024,384]{1,0:T(8,128)}, f32[1024,384]{1,0:T(8,128)}, bf16[2,6,1024,1024]{3,2,1,0:T(8,128)(2,1)}, bf16[3,192,384]{2,1,0:T(8,128)(2,1)}, f32[864,...) custom-call(bf16[1024,384]{1,0:T(8,128)(2,1)} %refs_0_.1, bf16[1024,384]{1,0:T(8,128)(2,1)} %refs_1_.1, s32[4]{0:T(128)} %refs_2_.1, ...), custom_call_target="tpu_custom_call" | custom-call | tf_op jit(solution)/shard_map/block/pallas_call | solution.py:1059
  150.5 0.0 copy-start.2
  150.5 0.0 copy-start.3
  150.6 0.0 copy-start.4
  150.6 0.0 copy-start.1
  150.6 6.5 %adam.1 = (f32[432,128]{1,0:T(8,128)}, f32[144,128]{1,0:T(8,128)}, f32[576,128]{1,0:T(8,128)}, f32[576,128]{1,0:T(8,128)}, f32[864,128]{1,0:T(8,128)}, /*index=5...) custom-call(bf16[3,192,384]{2,1,0:T(8,128)(2,1)} %get-tuple-element., ...), custom_call_target="tpu_custom_call" | custom-call | tf_op jit(solution)/shard_map/adam/pallas_call | solution.py:855
  157.1 1.2 slice.3
  159.0 0.0 copy-done.2
  159.1 0.0 copy-done.3
  159.1 0.0 copy-done.4
  159.1 1.4 fusion.1
  160.5 0.0 copy-done.1
  160.5 0.0 copy-start
  160.5 1.1 copy.53
  161.6 0.8 copy-done
  162.5 1.1 copy.54
Async XLA Ops:
  150.5 8.5 %copy-start.2 = (f32[672]{0:T(1024)S(1)}, f32[672]{0:T(1024)}, u32[]{:S(2)}) copy-start(f32[672]{0:T(1024)} %param.35) | copy-start | bytes 8068
  150.5 8.5 %copy-start.3 = (f32[672]{0:T(1024)S(1)}, f32[672]{0:T(1024)}, u32[]{:S(2)}) copy-start(f32[672]{0:T(1024)} %param.41) | copy-start | bytes 8068
  150.6 8.5 %copy-start.4 = (f32[672]{0:T(1024)S(1)}, f32[672]{0:T(1024)}, u32[]{:S(2)}) copy-start(f32[672]{0:T(1024)} %param.47) | copy-start | bytes 8068
  150.6 9.9 %copy-start.1 = (f32[1024,384]{1,0:T(8,128)S(1)}, f32[1024,384]{1,0:T(8,128)}, u32[]{:S(2)}) copy-start(f32[1024,384]{1,0:T(8,128)} %get-tuple-element.110) | copy-start | bytes 4718596
  160.5 2.0 %copy-start = (f32[1024,384]{1,0:T(8,128)S(1)}, f32[1024,384]{1,0:T(8,128)}, u32[]{:S(2)}) copy-start(f32[1024,384]{1,0:T(8,128)} %get-tuple-element.111) | copy-start | bytes 4718596

commit v5 on v4

--- a/solution.py
+++ b/solution.py
@@ -242,6 +242,11 @@
     dv_ref[...] = dv.astype(BF)
 
 
+class Refs:
+    def __init__(self, names, refs):
+        for name, ref in zip(names, refs, strict=True):
+            setattr(self, name, ref)
+
 MESH_ID = pl.DeviceIdType.MESH
 GROUPS = 4
 LAYERS = 4
@@ -513,6 +518,10 @@
             for s in range(ROLLOUT):
                 r.part_own[18 * s + j : 18 * s + j + 1, :] = col_sum(rows * columns[s])
         r.part_own[36:40, :] = jnp.zeros((4, 128), F32)
+        r.bias_own[...] = jnp.zeros((8, 128), F32)
+        for i in range(6):
+            size = 128 if i < 5 else 32
+            r.bias_own[i : i + 1, 0:size] = r.bias_flat[pl.ds(128 * i, size)].reshape(1, size)
         lane = lax.broadcasted_iota(jnp.int32, (8, 128), 1)
         shift = lax.rem(32 * at.dp, 128)
         turned = pltpu.roll(r.bias_own[...].astype(BF).astype(F32), shift, axis=1)
@@ -812,62 +821,131 @@
     return (master - learn_rate * (update + decay * master), first_new, second_new)
 
 
-def adam_kernel(*refs):
-    piece_ref, ada_ref, square_ref = refs[:3]
-    masters, firsts, seconds = (refs[3:8], refs[8:13], refs[13:18])
-    news, first_news, second_news, copies = (refs[18:23], refs[23:28], refs[28:33], refs[33:38])
-    flats = refs[38:42]
-    norm = jnp.sqrt(square_ref[0:1, :])
+STATE = ("qkv", "proj", "up", "down", "ada")
+
+
+def finish_kernel(names, *refs):
+    r = Refs(names, refs)
+    loads = {
+        name: local(getattr(r, name + "_far"), getattr(r, name), r.in_sems.at[index])
+        for index, name in enumerate(("pieces", "grad_ada"))
+    }
+    for index, name in enumerate(STATE):
+        for kind in range(3):
+            loads[name, kind] = local(
+                getattr(r, f"{name}_in{kind}"), getattr(r, f"{name}_{kind}"),
+                r.in_sems.at[2 + 3 * index + kind],
+            )
+    streams = [
+        local(getattr(r, name + "_in"), getattr(r, name), r.stream_sems.at[index])
+        for index, name in enumerate(("y", "dx"))
+    ]
+    norm = jnp.sqrt(r.square[...])
+    r.norm[0, 0] = jnp.max(norm)
     clip = grad_limit / jnp.maximum(norm, grad_limit)
-    qkv, proj, up, down = flats
+    row_clip = clip[0:1, :]
+
+    owner = lax.axis_index("dp")
+    lane = lax.broadcasted_iota(jnp.int32, (1, 128), 1)
+    first = 672 * owner // 128
+    shift = lax.rem(32 * owner, 128)
+    back = lax.rem(128 - shift, 128)
+    for i in range(6):
+        size = 128 if i < 5 else 32
+        here = pltpu.roll(r.bias_sum[pl.ds(first + i, 1), :], back, axis=1)
+        there = pltpu.roll(r.bias_sum[pl.ds(first + i + 1, 1), :], back, axis=1)
+        grad = jnp.where(lane < 128 - shift, here, there) * row_clip
+        place = pl.ds(128 * i, size)
+        state = [getattr(r, f"bias_in{kind}")[place].reshape(1, size) for kind in range(3)]
+        new, first_new, second_new = adam(*state, grad[:, :size], 0.0)
+        r.bias_out0[place] = new.reshape(size)
+        r.bias_out1[place] = first_new.reshape(size)
+        r.bias_out2[place] = second_new.reshape(size)
+        r.bias_out3[place] = new.reshape(size).astype(BF)
+
+    loads["pieces"].wait()
+    piece = r.pieces
     for g in range(3):
         for j in range(3):
-            qkv[pl.ds(3 * g + j, SLAB, stride=9), :] = piece_ref[0, SLAB * g : SLAB * (g + 1), 128 * j : 128 * j + 128].astype(F32)
+            r.grad_qkv[pl.ds(3 * g + j, SLAB, stride=9), :] = piece[
+                0, SLAB * g : SLAB * (g + 1), 128 * j : 128 * j + 128
+            ].astype(F32)
     for j in range(3):
-        proj[pl.ds(j, SLAB, stride=3), :] = piece_ref[0, 3 * SLAB :, 128 * j : 128 * j + 128].astype(F32)
+        columns = slice(128 * j, 128 * j + 128)
+        r.grad_proj[pl.ds(j, SLAB, stride=3), :] = piece[0, 3 * SLAB :, columns].astype(F32)
     for g in range(GROUPS):
+        rows = slice(SLAB * g, SLAB * (g + 1))
         for j in range(3):
-            up[pl.ds(3 * g + j, SLAB, stride=12), :] = piece_ref[1, SLAB * g : SLAB * (g + 1), 128 * j : 128 * j + 128].astype(F32)
-            down[pl.ds(3 * SLAB * g + j, SLAB, stride=3), :] = piece_ref[2, SLAB * g : SLAB * (g + 1), 128 * j : 128 * j + 128].astype(F32)
-    for index, grad in enumerate((qkv, proj, up, down, ada_ref)):
+            columns = slice(128 * j, 128 * j + 128)
+            r.grad_up[pl.ds(3 * g + j, SLAB, stride=12), :] = piece[1, rows, columns].astype(F32)
+            r.grad_down[pl.ds(3 * SLAB * g + j, SLAB, stride=3), :] = piece[2, rows, columns].astype(F32)
+
+    stores = []
+    for index, name in enumerate(STATE):
+        for kind in range(3):
+            loads[name, kind].wait()
+        if name == "ada":
+            loads["grad_ada"].wait()
+        grad, low = (getattr(r, "grad_" + name), getattr(r, name + "_low"))
+        state = [getattr(r, f"{name}_{kind}") for kind in range(3)]
+
         def chunk(i, carry):
             rows = pl.ds(pl.multiple_of(16 * i, 16), 16)
-            new, first, second = adam(
-                masters[index][rows, :], firsts[index][rows, :], seconds[index][rows, :],
-                grad[rows, :] * clip, 0.1,
+            new, first_new, second_new = adam(
+                *(ref[rows, :] for ref in state), grad[rows, :] * row_clip, 0.1
             )
-            news[index][rows, :] = new
-            first_news[index][rows, :] = first
-            second_news[index][rows, :] = second
-            copies[index][rows, :] = new.astype(BF)
+            for ref, value in zip(state, (new, first_new, second_new)):
+                ref[rows, :] = value
+            low[rows, :] = new.astype(BF)
             return carry
 
         lax.fori_loop(0, grad.shape[0] // 16, chunk, 0, unroll=3)
-
-
-def update(pieces, ada, square, masters, firsts, seconds):
-    flat = lambda arrays: [a.reshape(-1, 128) for a in arrays[:5]]
-    masters, firsts, seconds = (flat(masters), flat(firsts), flat(seconds))
-    vmem = pl.BlockSpec(memory_space=pltpu.VMEM)
-    shapes = [m.shape for m in masters]
-    outs = [jax.ShapeDtypeStruct(s, F32) for s in shapes] * 3
-    outs += [jax.ShapeDtypeStruct(s, BF) for s in shapes]
-    results = pl.pallas_call(
-        adam_kernel,
-        in_specs=[vmem] * 18,
-        out_specs=[vmem] * 20,
-        out_shape=outs,
-        scratch_shapes=[pltpu.VMEM(s, F32) for s in shapes[:4]],
-        name="adam",
-    )(pieces, ada, square, *masters, *firsts, *seconds)
-    results = [r.reshape(-1) for r in results]
-    return (results[0:5], results[5:10], results[10:15], results[15:20])
-
-
-class Refs:
-    def __init__(self, names, refs):
-        for name, ref in zip(names, refs, strict=True):
-            setattr(self, name, ref)
+        for kind, ref in enumerate((*state, low)):
+            stores.append(local(ref, getattr(r, f"{name}_out{kind}"), r.out_sems.at[4 * index + kind]))
+        if index < 2:
+            name = ("y", "dx")[index]
+            streams[index].wait()
+            stores.append(local(getattr(r, name), getattr(r, name + "_out"), r.stream_sems.at[index]))
+    for made in stores:
+        made.wait()
+
+
+def finish(y, dx, pieces, ada, bias_sum, square, masters, firsts, seconds):
+    vmem, hbm, dma = (pltpu.VMEM, pl.ANY, pltpu.SemaphoreType.DMA)
+    state = list(zip(masters, firsts, seconds))
+    shapes = {name: (arrays[0].size // 128, 128) for name, arrays in zip(STATE, state)}
+    ins = [
+        ("square", square, vmem), ("bias_sum", bias_sum, vmem), ("pieces_far", pieces, hbm),
+        ("grad_ada_far", ada, hbm), ("y_in", y, hbm), ("dx_in", dx, hbm),
+        *[(f"bias_in{kind}", array, vmem) for kind, array in enumerate(state[5])],
+        *[
+            (f"{name}_in{kind}", array.reshape(-1, 128), hbm)
+            for name, arrays in zip(STATE, state)
+            for kind, array in enumerate(arrays)
+        ],
+    ]
+    outs = [("norm", (1, 1), F32, pltpu.SMEM), ("y_out", y.shape, F32, hbm), ("dx_out", dx.shape, F32, hbm)]
+    for kind in range(4):
+        dtype = F32 if kind < 3 else BF
+        outs += [(f"{name}_out{kind}", shapes[name], dtype, hbm) for name in STATE]
+        outs.append((f"bias_out{kind}", state[5][0].shape, dtype, vmem))
+    scratch = [
+        ("pieces", vmem(pieces.shape, BF)), ("y", vmem(y.shape, F32)), ("dx", vmem(dx.shape, F32)),
+        *[(f"{name}_{kind}", vmem(shapes[name], F32)) for name in STATE for kind in range(3)],
+        *[(f"{name}_low", vmem(shapes[name], BF)) for name in STATE],
+        *[(f"grad_{name}", vmem(shapes[name], F32)) for name in STATE],
+        ("in_sems", dma((17,))), ("stream_sems", dma((2,))), ("out_sems", dma((20,))),
+    ]
+    names = [item[0] for item in (*ins, *outs, *scratch)]
+    norm, y, dx, *rest = pl.pallas_call(
+        functools.partial(finish_kernel, names),
+        in_specs=[pl.BlockSpec(memory_space=space) for *_, space in ins],
+        out_specs=[pl.BlockSpec(memory_space=space) for *_, space in outs],
+        out_shape=[jax.ShapeDtypeStruct(shape, kind) for _, shape, kind, _ in outs],
+        scratch_shapes=[kind for _, kind in scratch],
+        name="finish",
+    )(*(array for _, array, _ in ins))
+    return (y, dx, norm.reshape(()), *(array.reshape(-1) for array in rest))
 
 
 MASTERS = ("qkv", "proj", "up", "down", "ada")
@@ -1085,7 +1163,6 @@
         ("far_" + name, array.reshape(-1, 128), hbm)
         for name, array in zip(MASTERS, (qkv, proj, up, down, ada))
     ]
-    bias = jnp.pad(bias, (0, 1024 - bias.shape[0])).reshape(8, 128)
     pairs_of = [
         ("gz", (UNITS, 3)), ("gx", (UNITS, 3, 3)), ("gs", (UNITS, 4)), ("gm", (8,)),
         ("rs", (UNITS,)), ("rx", (UNITS, 3)), ("rz", (UNITS, 3)), ("ra", (UNITS, 3)),
@@ -1094,12 +1171,12 @@
     y, dx, _, pieces, ada_grad, bias_sum, square = block_call(
         Together, inputs, cotangent,
         [("start", start, smem), ("interval", interval, smem), ("counts", counts, smem),
-         ("lead", lead, vmem), ("bias_own", bias, vmem), *far],
+         ("lead", lead, vmem), ("bias_flat", bias, vmem), *far],
         [("pieces_far", (UNITS, 4 * SLAB, PART), BF, hbm), ("ada_far", (18 * SLAB, 128), F32, hbm),
          ("bias_out", (48, 128), F32, vmem), ("square_out", (8, 128), F32, vmem)],
         [("cond_t", vmem((D, 8), F32)), ("part_own", vmem((40, 128), F32)),
          ("part_sib", vmem((40, 128), F32)), ("part_z", vmem((LAYERS, 40, 128), F32)),
-         ("bias_slot", vmem((LAYERS, 2, 8, 128), F32)), ("bias_full", vmem((48, 128), F32)),
+         ("bias_own", vmem((8, 128), F32)), ("bias_slot", vmem((LAYERS, 2, 8, 128), F32)), ("bias_full", vmem((48, 128), F32)),
          ("vec_sib", vmem((64, 128), F32)), ("vec_z", vmem((LAYERS, 64, 128), F32)),
          ("vec_g", vmem((GROUPS, 64, 128), F32)), ("square_d", vmem((8, 8, 128), F32)),
          ("square_g", vmem((GROUPS, 8, 128), F32)), ("joined", pltpu.SemaphoreType.REGULAR),
@@ -1210,19 +1287,8 @@
     result, input_grad, pieces, ada_grad, bias_sum, square = block_together(
         inputs, cotangent, rollout_start, group_interval, sample_counts, lead_table, masters
     )
-    news, first_news, second_news, copies = update(
-        pieces, ada_grad, square, masters, firsts, seconds
-    )
-    grad_norm = jnp.sqrt(square[0, 0])
-    clip = grad_limit / jnp.maximum(grad_norm, grad_limit)
-    bias_rows = masters[5].shape[0]
-    bias_grad = lax.dynamic_slice_in_dim(
-        bias_sum.reshape(-1), lax.axis_index("dp") * bias_rows, bias_rows
-    )
-    new, first, second = adam(masters[5], firsts[5], seconds[5], bias_grad * clip, 0.0)
-    return (
-        result, input_grad, grad_norm, *news, new, *first_news, first, *second_news, second,
-        *copies, new.astype(BF),
+    return finish(
+        result, input_grad, pieces, ada_grad, bias_sum, square, masters, firsts, seconds
     )
 
 

time: 165 us -> 158 us (0.958)
  local copies, waits for them, and re-layouts: 5.62 us -> 0 us
  Pallas kernels: 155 us -> 157 us
  between operations: 2.61 us -> 0.86 us
    unnamed x12 -> x0, local copies, waits for them, and re-layouts: 3.14 us -> none
where the time goes in v5:
time: 158 us
  Pallas kernels  157 us (99%)
    pallas_call x1, Pallas kernels, block_call(): pl.pallas_call(functools.partial(block_kernel, names, hooked), in_specs=[...  149 us
    pallas_call x1, Pallas kernels, finish(): pl.pallas_call(functools.partial(finish_kernel, names), in_specs=[pl.Bloc...  8.05 us

profile of v5, /device:TPU:0, one launch (start us, length us, event | category | flops | bytes accessed | tf_op | source)
XLA Modules:
  0.0 157.8 jit_solution(5345385741859087300)
XLA Ops:
  0.7 148.9 %block.1 = (f32[1024,384]{1,0:T(8,128)}, f32[1024,384]{1,0:T(8,128)}, bf16[2,6,1024,1024]{3,2,1,0:T(8,128)(2,1)}, bf16[3,192,384]{2,1,0:T(8,128)(2,1)}, f32[864,...) custom-call(bf16[1024,384]{1,0:T(8,128)(2,1)} %refs_0_.1, bf16[1024,384]{1,0:T(8,128)(2,1)} %refs_1_.1, s32[4]{0:T(128)} %refs_2_.1, ...), custom_call_target="tpu_custom_call" | custom-call | tf_op jit(solution)/shard_map/block/pallas_call | solution.py:1137
  149.6 8.1 %finish.1 = (f32[1,1]{1,0:T(1,128)}, f32[1024,384]{1,0:T(8,128)}, f32[1024,384]{1,0:T(8,128)}, f32[432,128]{1,0:T(8,128)}, f32[144,128]{1,0:T(8,128)}, /*index=5...) custom-call(f32[8,128]{1,0:T(8,128)} %get-tuple-element.60.refs_0_, ...), custom_call_target="tpu_custom_call" | custom-call | tf_op jit(solution)/shard_map/finish/pallas_call | solution.py:940

commit v6 on v5

--- a/solution.py
+++ b/solution.py
@@ -109,9 +109,7 @@
 
 
 def ffn_back(
-    mods, grad, branch_two, act, slope, normed, inverse, hidden, branch_one, att,
-    wa_ref, wup_ref, wdown_ref, gdown_ref, gup_ref, gproj_ref, wide_ref, narrow_ref,
-    dmid_ref, datt_ref,
+    mods, grad, branch_two, act, slope, hidden, wdown_ref, gdown_ref, gup_ref, wide_ref, narrow_ref
 ):
     df = (mods(GATE2) * grad).astype(BF)
     narrow_ref[pl.ds(GATE2, 1), :] += col_sum(grad * branch_two)
@@ -121,6 +119,13 @@
     du = (dact * slope).astype(BF)
     wide_ref[pl.ds(0, 1), :] += col_sum(du.astype(F32))
     gup_ref[...] += dot(hidden, du, TN)
+    return du
+
+
+def middle_back(
+    mods, grad, du, normed, inverse, branch_one, att, wa_ref, wup_ref, gproj_ref, narrow_ref,
+    dmid_ref, datt_ref,
+):
     dh = dot(du, wup_ref[...], NT)
     narrow_ref[pl.ds(SHIFT2, 1), :] += col_sum(dh)
     narrow_ref[pl.ds(SCALE2, 1), :] += col_sum(dh * normed)
@@ -149,43 +154,65 @@
     act = act.astype(BF)
     branch_two = dot(act, wdown_ref[...]) + shared(ROW_BDOWN)
     out_ref[...] = middle + mods(GATE2) * branch_two
-    ffn_back(
-        mods, cot_ref[...].astype(F32), branch_two, act, slope, normed, inverse, hidden,
-        branch_one, att, wa_ref, wup_ref, wdown_ref, gdown_ref, gup_ref, gproj_ref,
-        wide_ref, narrow_ref, dmid_ref, datt_ref,
+    grad = cot_ref[...].astype(F32)
+    du = ffn_back(
+        mods, grad, branch_two, act, slope, hidden, wdown_ref, gdown_ref, gup_ref, wide_ref, narrow_ref
     )
-
-
-def qkv_back(mods, stream, dmid, dqkv, wa_ref, gqkv_ref, narrow_ref, bias_ref):
+    middle_back(
+        mods, grad, du, normed, inverse, branch_one, att, wa_ref, wup_ref, gproj_ref, narrow_ref,
+        dmid_ref, datt_ref,
+    )
+
+
+def qkv_back(mods, stream, dmid, dqkv, wa_ref, narrow_ref, bias_ref, gqkv_ref=None):
     normed, inverse = layer_norm(stream)
-    hidden = modulated(normed, mods, SCALE1, SHIFT1)
     bias_ref[pl.ds(0, 1), :] += col_sum(dqkv.astype(F32))
-    gqkv_ref[...] += dot(hidden, dqkv, TN)
+    if gqkv_ref is not None:
+        gqkv_ref[...] += dot(modulated(normed, mods, SCALE1, SHIFT1), dqkv, TN)
     dh = dot(dqkv, wa_ref[:, : 3 * D], NT)
     narrow_ref[pl.ds(SHIFT1, 1), :] += col_sum(dh)
     narrow_ref[pl.ds(SCALE1, 1), :] += col_sum(dh * normed)
     return dmid + norm_back(normed, inverse, dh * (1.0 + mods(SCALE1)))
 
 
+def middle_again(mods, x_ref, a_refs):
+    branch_one = jnp.concatenate([ref[...] for ref in a_refs], axis=1)
+    normed, inverse = layer_norm(x_ref[...].astype(F32) + mods(GATE1) * branch_one)
+    return (branch_one, normed, inverse)
+
+
 def join_rows(
-    dqkv_ref, x1_ref, x0_ref, a_refs, gp_ref, act_refs, f_ref, att_ref,
-    rows_ref, wa_ref, wup_ref, wdown_ref,
-    dmid_ref, datt_ref, gqkv_ref, gdown_ref, gup_ref, gproj_ref, wide_ref, narrow1_ref,
-    narrow_ref, bias_ref,
+    dqkv_ref, x1_ref, x0_ref, a_refs, gp_ref, act_refs, f_ref, rows_ref, wa_ref, wdown_ref,
+    hidden_ref, dmid_ref, gqkv_ref, gdown_ref, gup_ref, wide_ref, narrow1_ref, narrow_ref, bias_ref,
 ):
     grad = qkv_back(
-        mod_reader(rows_ref, 1), x1_ref[...], dmid_ref[...], dqkv_ref[...], wa_ref, gqkv_ref,
-        narrow1_ref, bias_ref,
+        mod_reader(rows_ref, 1), x1_ref[...], dmid_ref[...], dqkv_ref[...], wa_ref,
+        narrow1_ref, bias_ref, gqkv_ref,
     )
+    dmid_ref[...] = grad
     mods = mod_reader(rows_ref, 0)
-    branch_one = jnp.concatenate([ref[...] for ref in a_refs], axis=1)
-    middle = x0_ref[...].astype(F32) + mods(GATE1) * branch_one
-    normed, inverse = layer_norm(middle)
-    hidden = modulated(normed, mods, SCALE2, SHIFT2)
-    ffn_back(
-        mods, grad, f_ref[...], jnp.concatenate([ref[...] for ref in act_refs], axis=1), gp_ref[...], normed, inverse, hidden,
-        branch_one, att_ref[...], wa_ref, wup_ref, wdown_ref, gdown_ref, gup_ref, gproj_ref,
-        wide_ref, narrow_ref, dmid_ref, datt_ref,
+    normed, _ = layer_norm(x0_ref[...].astype(F32))
+    hidden_ref[...] = modulated(normed, mods, SCALE1, SHIFT1)
+    _, normed, _ = middle_again(mods, x0_ref, a_refs)
+    act = jnp.concatenate([ref[...] for ref in act_refs], axis=1)
+    du = ffn_back(
+        mods, grad, f_ref[...], act, gp_ref[...], modulated(normed, mods, SCALE2, SHIFT2),
+        wdown_ref, gdown_ref, gup_ref, wide_ref, narrow_ref,
+    )
+    for part, ref in enumerate(act_refs):
+        ref[...] = du[:, PART * part : PART * (part + 1)]
+
+
+def join_middle_rows(
+    x0_ref, a_refs, du_refs, att_ref, rows_ref, wa_ref, wup_ref,
+    dmid_ref, datt_ref, gproj_ref, narrow_ref,
+):
+    mods = mod_reader(rows_ref, 0)
+    branch_one, normed, inverse = middle_again(mods, x0_ref, a_refs)
+    du = jnp.concatenate([ref[...] for ref in du_refs], axis=1)
+    middle_back(
+        mods, dmid_ref[...], du, normed, inverse, branch_one, att_ref[...], wa_ref, wup_ref,
+        gproj_ref, narrow_ref, dmid_ref, datt_ref,
     )
 
 
@@ -220,11 +247,11 @@
     o_ref[...] = jnp.transpose(mixed).astype(BF)
 
 
-def attend_back_pair(q, k, v_ref, grads, p_ref, dq_ref, dk_ref, dv_ref, kt_ref):
+def attend_back_pair(q, k, v_ref, grads, p_ref, dq_ref, dk_ref, dv_ref, kt_ref, between):
     turned_heads(k.astype(F32) * score_scale, kt_ref)
     queries = q * BF(score_scale)
-    dq_turned, dk, dv = (None, None, None)
-    for half, lanes in enumerate(head_lanes(queries.shape[0])):
+    own_lanes = head_lanes(queries.shape[0])
+    for half, lanes in enumerate(own_lanes):
         grad = jnp.where(lanes, grads, BF(0))
         query = jnp.where(lanes, queries, BF(0))
         low = p_ref[half]
@@ -232,14 +259,14 @@
         weights = low.astype(F32)
         delta = jnp.sum(weights * weight_grad, axis=0, keepdims=True)
         score_grad = (weights * (weight_grad - delta)).astype(BF)
-        parts = (dot(kt_ref[half], score_grad), dot(score_grad, query), dot(low, grad))
-        if half == 0:
-            dq_turned, dk, dv = parts
-        else:
-            dq_turned, dk, dv = (dq_turned + parts[0], dk + parts[1], dv + parts[2])
-    dq_ref[...] = jnp.transpose(dq_turned).astype(BF)
-    dk_ref[...] = dk.astype(BF)
-    dv_ref[...] = dv.astype(BF)
+        news = (
+            jnp.transpose(dot(kt_ref[half], score_grad)), dot(score_grad, query), dot(low, grad)
+        )
+        for ref, new in zip((dq_ref, dk_ref, dv_ref), news):
+            new = new.astype(BF)
+            ref[...] = new if half == 0 else jnp.where(lanes, new, ref[...])
+        if half == 0 and between is not None:
+            between()
 
 
 class Refs:
@@ -342,58 +369,95 @@
         for made in self.later:
             made.wait()
 
+    def before_join(self):
+        pass
+
+    def amid_join(self):
+        fill_blocks(self.refs)
+
     def after_join(self):
-        fill_blocks(self.refs, (1, 2))
+        pass
+
+    def amid_back_pair(self, h):
+        pass
 
     def after_back_pair(self, h):
+        fill_pair(self.refs, h)
+
+    def after_last_rows(self, i):
         pass
 
     def after_last(self):
         r = self.refs
-        fill_blocks(r, (0,))
         fill_vec(r)
+        fill_late(r, r.late)
+        r.vec[0:6, :] = r.late[0:6, :]
+        r.vec[VEC_STEP : VEC_STEP + 6, :] = r.late[6:12, :]
         puts = [local(r.blocks, r.blocks_far, r.in_sems.at[0]), local(r.vec, r.vec_far, r.in_sems.at[1])]
         for made in puts:
             made.wait()
 
 
-def fill_blocks(refs, units):
+def block_rows(owner, part):
+    first = HALF * (owner % 2) + 4 * SLAB * part + SLAB * (owner // 2)
+    return slice(first, first + SLAB)
+
+
+def fill_blocks(refs):
     share = refs.rows[ROW_SHARE : ROW_SHARE + 1, :]
     for d in range(8):
         own = slice(SLAB * d, SLAB * (d + 1))
         for g in range(4):
-            columns = slice(PART * g, PART * (g + 1))
-            first = HALF * (d % 2) + 4 * SLAB * g + SLAB * (d // 2)
-            there = slice(first, first + SLAB)
-            for unit in units:
-                if unit == 0:
-                    value = refs.gqkv[own, columns] if g < 3 else refs.gproj[own, :]
-                elif unit == 1:
-                    value = refs.gup[own, columns]
-                else:
-                    value = refs.gdown[SLAB * (4 * d + g) : SLAB * (4 * d + g + 1), :]
-                refs.blocks[unit, there, :] = (value * share).astype(BF)
+            up = refs.gup[own, PART * g : PART * (g + 1)]
+            down = refs.gdown[SLAB * (4 * d + g) : SLAB * (4 * d + g + 1), :]
+            refs.blocks[1, block_rows(d, g), :] = (up * share).astype(BF)
+            refs.blocks[2, block_rows(d, g), :] = (down * share).astype(BF)
+
+
+def fill_pair(refs, h):
+    share = refs.rows[ROW_SHARE : ROW_SHARE + 1, 0:128]
+    columns = [pl.ds(pl.multiple_of(D * g + 128 * h, 128), 128) for g in range(3)]
+    grads = jnp.concatenate([refs.dqkv[:, column] for column in columns], axis=1)
+    value = dot(refs.att1[...], grads, TN)
+    for d in range(8):
+        own = slice(SLAB * d, SLAB * (d + 1))
+        for g in range(3):
+            part = value[own, 128 * g : 128 * (g + 1)] + refs.gqkv[own, columns[g]]
+            refs.blocks[0, block_rows(d, g), columns[0]] = (part * share).astype(BF)
+        part = refs.gproj[own, columns[0]]
+        refs.blocks[0, block_rows(d, 3), columns[0]] = (part * share).astype(BF)
+
+
+VEC = 72
+VEC_STEP = 24
 
 
 def fill_vec(refs):
-    share = refs.rows[ROW_SHARE : ROW_SHARE + 1, :]
+    share = refs.rows[ROW_SHARE : ROW_SHARE + 1, 0:128]
 
     def put(first_row, value):
         for j in range(value.shape[1] // 128):
-            refs.vec[first_row + j : first_row + j + 1, :] = (
-                value[:, 128 * j : 128 * j + 128] * share[:, 0:128]
-            )
-
-    bias, wide, narrow0, narrow1 = (refs.bias, refs.wide, refs.narrow0, refs.narrow1)
-    put(0, bias[0:1, :D])
-    put(3, bias[0:1, 2 * D :])
+            refs.vec[first_row + j : first_row + j + 1, :] = value[:, 128 * j : 128 * j + 128] * share
+
+    refs.vec[...] = jnp.zeros_like(refs.vec)
+    wide, narrow0, narrow1 = (refs.wide, refs.narrow0, refs.narrow1)
     put(6, narrow0[6:7, :] + narrow1[6:7, :])
     put(9, wide[0:1, :])
     put(21, narrow0[7:8, :] + narrow1[7:8, :])
     for r in range(6):
-        put(24 + 3 * r, narrow0[r : r + 1, :])
-        put(42 + 3 * r, narrow1[r : r + 1, :])
-    refs.vec[60:64, :] = jnp.zeros((4, 128), F32)
+        if r > 1:
+            put(VEC_STEP + 3 * r, narrow0[r : r + 1, :])
+        put(2 * VEC_STEP + 3 * r, narrow1[r : r + 1, :])
+
+
+def fill_late(refs, late_ref):
+    share = refs.rows[ROW_SHARE : ROW_SHARE + 1, 0:128]
+    rest = (refs.bias[0:1, :D], refs.bias[0:1, 2 * D :], refs.narrow0[0:1, :], refs.narrow0[1:2, :])
+    for index, value in enumerate(rest):
+        for j in range(3):
+            row = 3 * index + j
+            late_ref[row : row + 1, :] = value[:, 128 * j : 128 * j + 128] * share
+    late_ref[12:16, :] = jnp.zeros((4, 128), F32)
 
 
 class Together:
@@ -481,12 +545,7 @@
             name: local(r.masters[name], stage[name], r.in_sems.at[index])
             for index, name in enumerate(stage)
         }
-        ready = greet(
-            [at.sibling()]
-            + [at.along_grp(k) for k in steps]
-            + [at.along_z(k) for k in steps]
-            + [at.across(k) for k in steps]
-        )
+        ready = greet([self.everywhere(step) for step in range(1, 8 * LAYERS)])
 
         def fill(unit, source, count, offset, first=0):
             for j in range(count):
@@ -584,9 +643,12 @@
 
     def after_first(self):
         self.forward_grp(1)
-        self.forward_grp(2)
 
     def after_attend_pair(self, h):
+        @pl.when(h == 0)
+        def _():
+            self.forward_grp(2)
+
         @pl.when(h == 1)
         def _():
             self.forward_sibling(1)
@@ -597,103 +659,215 @@
         self.finish_sibling(2)
 
 
-    def got(self, unit, name, k=1):
-        first = {"sib": 0, "grp": HALF, "z": HALF + 12 * SLAB, "piece": HALF + 15 * SLAB}[name]
-        first += {"sib": 0, "grp": 4 * SLAB, "z": SLAB, "piece": 0}[name] * (k - 1)
-        size = {"sib": HALF, "grp": 4 * SLAB, "z": SLAB, "piece": 4 * SLAB}[name]
-        if unit == 0:
-            if name in ("sib", "piece"):
-                first = 0 if name == "sib" else HALF
-                return self.refs.att0.at[first : first + size]
-            first += 2 * 35 * SLAB - HALF
-        else:
-            first += 35 * SLAB * (unit - 1)
-        return self.refs.act.at[first : first + size]
-
-    def mine(self, unit):
-        return self.refs.blocks.at[unit, span(HALF * self.at.core, HALF), :]
+    x_first = {3: True, 4: False}
+
+    def columns(self, unit):
+        return pl.ds(128 * unit, 128) if unit < 3 else slice(None)
+
+    def got(self, unit, name):
+        first = {"sib": 0, "piece": HALF, "grp": 0, "one": 0, "two": 8 * SLAB, "z": 12 * SLAB}[name]
+        size = {"sib": HALF, "piece": 4 * SLAB, "grp": 12 * SLAB, "one": 8 * SLAB, "two": 4 * SLAB, "z": 3 * SLAB}[name]
+        r, rows = (self.refs, slice(first, first + size))
+        if unit < 3:
+            return (r.att0 if name in ("sib", "piece") else r.act).at[rows, self.columns(unit)]
+        if name in ("sib", "piece"):
+            third = 0 if unit == 3 else 1
+            return r.qkv1.at[rows, D * third : D * (third + 1)]
+        return r.cot.at[rows] if unit == 3 else r.qkv1.at[rows, 2 * D : 3 * D]
+
+    def half(self, unit, core):
+        block = max(unit - 2, 0)
+        return self.refs.blocks.at[block, span(HALF * core, HALF), self.columns(unit)]
+
+    def parts(self, unit, part, count=1):
+        return self.half(unit, self.at.core).at[span(4 * SLAB * part, 4 * SLAB * count), :]
 
     def sum_sibling(self, unit):
-        src = self.refs.blocks.at[unit, span(HALF * (1 - self.at.core), HALF), :]
+        src = self.half(unit, 1 - self.at.core)
         return remote(src, self.got(unit, "sib"), self.refs.rs, unit, self.at.sibling())
+
+    def grp_peer(self, along_x):
+        x, y = (self.at.grp % 2, self.at.grp // 2)
+        grp = 2 * y + 1 - x if along_x else 2 * (1 - y) + x
+        return (grp, self.at.dp)
+
+    def stage_parts(self, unit, own):
+        x, y = (self.at.grp % 2, self.at.grp // 2)
+        if self.x_first[unit]:
+            return [2 * j + (x if own else 1 - x) for j in range(2)]
+        return [2 * (y if own else 1 - y) + j for j in range(2)]
+
+    def sum_one(self, unit, j):
+        src = self.parts(unit, self.stage_parts(unit, False)[j])
+        dst = self.got(unit, "one").at[4 * SLAB * j : 4 * SLAB * (j + 1)]
+        return remote(src, dst, self.refs.rx, (unit, j), self.grp_peer(self.x_first[unit]))
+
+    def sum_two(self, unit):
+        peer = self.grp_peer(not self.x_first[unit])
+        return remote(self.parts(unit, peer[0]), self.got(unit, "two"), self.refs.rx, (unit, 2), peer)
 
     def sum_grp(self, unit, k):
         peer = self.at.along_grp(k)
-        src = self.mine(unit).at[span(4 * SLAB * peer[0], 4 * SLAB), :]
-        return remote(src, self.got(unit, "grp", k), self.refs.rx, (unit, k - 1), peer)
+        first = 4 * SLAB * (k - 1)
+        dst = self.got(unit, "grp").at[first : first + 4 * SLAB]
+        return remote(self.parts(unit, peer[0]), dst, self.refs.rx, (unit, k - 1), peer)
+
+    def own_part(self, unit):
+        return self.parts(unit, self.at.grp)
 
     def sum_z(self, unit, k):
         there = lax.rem(self.at.z + k, LAYERS)
-        src = self.mine(unit).at[span(4 * SLAB * self.at.grp + SLAB * there, SLAB), :]
-        return remote(src, self.got(unit, "z", k), self.refs.rz, (unit, k - 1), self.at.along_z(k))
+        src = self.own_part(unit).at[span(SLAB * there, SLAB), :]
+        dst = self.got(unit, "z").at[SLAB * (k - 1) : SLAB * k]
+        return remote(src, dst, self.refs.rz, (unit, k - 1), self.at.along_z(k))
 
     def share_piece(self, unit, k):
         own = self.got(unit, "piece").at[span(SLAB * self.at.grp, SLAB), :]
         return remote(own, own, self.refs.ra, (unit, k - 1), self.at.along_grp(k))
 
-    def add_sibling(self, unit):
-        self.sum_sibling(unit).wait_recv()
-        mine, got = (self.mine(unit), self.got(unit, "sib"))
-
-        def add(i, carry):
+    def add(self, mine, got, count):
+        def step(i, carry):
             rows = span(SLAB * i, SLAB)
             mine[rows, :] = (mine[rows, :].astype(F32) + got[rows, :].astype(F32)).astype(BF)
             return carry
 
-        lax.fori_loop(0, 16, add, 0)
-        for k in self.steps:
-            self.start(self.sum_grp(unit, k))
+        lax.fori_loop(0, count, step, 0)
+
+    def add_sibling(self, unit):
+        self.sum_sibling(unit).wait_recv()
+        self.add(self.half(unit, self.at.core), self.got(unit, "sib"), 16)
+        if unit < 3:
+            for k in self.steps:
+                self.start(self.sum_grp(unit, k))
+        else:
+            for j in range(2):
+                self.start(self.sum_one(unit, j))
 
     def add_grp(self, unit):
         for k in self.steps:
             self.sum_grp(unit, k).wait_recv()
-        mine = self.mine(unit).at[span(4 * SLAB * self.at.grp, 4 * SLAB), :]
-
-        def add(i, carry):
+        mine, got = (self.own_part(unit), self.got(unit, "grp"))
+
+        def step(i, carry):
             rows = span(SLAB * i, SLAB)
             value = mine[rows, :].astype(F32)
             for k in self.steps:
-                value = value + self.got(unit, "grp", k)[rows, :].astype(F32)
+                value = value + got[span(SLAB * (i + 4 * (k - 1)), SLAB), :].astype(F32)
             mine[rows, :] = value.astype(BF)
             return carry
 
-        lax.fori_loop(0, 4, add, 0)
+        lax.fori_loop(0, 4, step, 0)
+        for k in self.steps:
+            self.start(self.sum_z(unit, k))
+
+    def add_one(self, unit):
+        for j in range(2):
+            self.sum_one(unit, j).wait_recv()
+            got = self.got(unit, "one").at[4 * SLAB * j : 4 * SLAB * (j + 1)]
+            self.add(self.parts(unit, self.stage_parts(unit, True)[j]), got, 4)
+        self.start(self.sum_two(unit))
+
+    def add_two(self, unit):
+        self.sum_two(unit).wait_recv()
+        self.add(self.own_part(unit), self.got(unit, "two"), 4)
         for k in self.steps:
             self.start(self.sum_z(unit, k))
 
     def add_z(self, unit):
         for k in self.steps:
             self.sum_z(unit, k).wait_recv()
-        mine = self.mine(unit).at[span(4 * SLAB * self.at.grp + SLAB * self.at.z, SLAB), :]
-        value = mine[...].astype(F32)
+        value = self.own_part(unit)[span(SLAB * self.at.z, SLAB), :].astype(F32)
         for k in self.steps:
-            value = value + self.got(unit, "z", k)[...].astype(F32)
+            value = value + self.got(unit, "z")[SLAB * (k - 1) : SLAB * k, :].astype(F32)
         value = value.astype(BF)
         self.got(unit, "piece")[span(SLAB * self.at.grp, SLAB), :] = value
         for k in self.steps:
             self.start(self.share_piece(unit, k))
         value = value.astype(F32)
         squares = col_sum(value * value)
+        if unit < 3:
+            return squares
         return squares[:, 0:128] + squares[:, 128:256] + squares[:, 256:384]
 
-    def after_join(self):
-        r, at = (self.refs, self.at)
+    def tell(self, sem):
+        at = self.at
         for peer in (
             [at.sibling()]
             + [at.along_grp(k) for k in self.steps]
             + [at.along_z(k) for k in self.steps]
         ):
-            pl.semaphore_signal(r.joined, inc=1, device_id=peer, device_id_type=MESH_ID)
-        fill_blocks(r, (1, 2))
-        pl.semaphore_wait(r.joined, 7)
-        self.start(self.sum_sibling(1))
-        self.start(self.sum_sibling(2))
-
-    def after_back_pair(self, h):
+            pl.semaphore_signal(sem, inc=1, device_id=peer, device_id_type=MESH_ID)
+
+    def before_join(self):
+        self.tell(self.refs.turned_back)
+
+    def amid_join(self):
+        fill_blocks(self.refs)
+        pl.semaphore_wait(self.refs.turned_back, 7)
+        self.start(self.sum_sibling(3))
+        self.start(self.sum_sibling(4))
+
+    def after_join(self):
+        r = self.refs
+        self.tell(r.joined)
+        self.add_sibling(3)
+        self.add_sibling(4)
+        fill_vec(r)
+        self.start(self.small_sum(0))
+
+    def amid_back_pair(self, h):
+        r, at = (self.refs, self.at)
+
         @pl.when(h == 0)
         def _():
+            self.small_sum(0).wait_recv()
+            r.vec_z[at.z] = r.vec[...] + r.vec_sib[...]
+            for index in self.steps:
+                self.start(self.small_sum(index))
+
+        @pl.when(h == 1)
+        def _():
+            self.add_one(3)
+            self.add_one(4)
+            self.add_sibling(0)
+            for index in self.steps:
+                self.small_sum(index).wait_recv()
+            r.vec_g[at.grp] = r.vec_z[0] + r.vec_z[1] + r.vec_z[2] + r.vec_z[3]
+            for index in self.steps:
+                self.start(self.small_sum(3 + index))
+
+        @pl.when(h == 2)
+        def _():
+            self.add_two(3)
+            self.add_two(4)
             self.add_sibling(1)
+            self.add_grp(0)
+
+    def after_back_pair(self, h):
+        r = self.refs
+        fill_pair(r, h)
+
+        @pl.when(h == 0)
+        def _():
+            pl.semaphore_wait(r.joined, 7)
+            self.start(self.sum_sibling(0))
+
+        @pl.when(h == 1)
+        def _():
+            self.start(self.sum_sibling(1))
+
+        @pl.when(h == 2)
+        def _():
+            self.start(self.sum_sibling(2))
+
+    def after_last_rows(self, i):
+        @pl.when(i == 0)
+        def _():
             self.add_sibling(2)
+
+        @pl.when(i == 2)
+        def _():
+            self.add_grp(1)
 
     def small_sum(self, index):
         r, at = (self.refs, self.at)
@@ -705,86 +879,94 @@
         own = r.vec_g.at[at.grp]
         return remote(own, own, r.rv, index, at.along_grp(index - 3))
 
-    def square_sum(self, index):
+    def across_dp(self, index):
+        at = self.at
+        if index == 0:
+            return at.sibling()
+        return at.along_z(index) if index < 4 else at.across(index - 3)
+
+    def everywhere(self, step):
+        device = lax.rem(2 * LAYERS * self.at.grp + self.at.dp + step, 8 * LAYERS)
+        return (device // (2 * LAYERS), lax.rem(device, 2 * LAYERS))
+
+    def square_sum(self, step):
+        own = self.refs.squares.at[2 * LAYERS * self.at.grp + self.at.dp]
+        return remote(own, own, self.refs.rq, step, self.everywhere(step))
+
+    def late_sum(self, index):
         r, at = (self.refs, self.at)
         if index < 7:
-            peer = at.sibling()
-            if index > 0:
-                peer = at.along_z(index) if index < 4 else at.across(index - 3)
-            own = r.square_d.at[at.dp]
-        else:
-            peer = at.along_grp(index - 6)
-            own = r.square_g.at[at.grp]
-        return remote(own, own, r.rq, index, peer)
+            own = r.late_d.at[at.dp]
+            return remote(own, own, r.rl, index, self.across_dp(index))
+        own = r.late_g.at[at.grp]
+        return remote(own, own, r.rl, index, at.along_grp(index - 6))
+
+    def ada_square(self):
+        r = self.refs
+        left = r.cond_out[...]
+        right = [
+            r.vec_out[g, VEC_STEP * (s + 1) : VEC_STEP * (s + 2), :]
+            for g in range(GROUPS)
+            for s in range(ROLLOUT)
+        ]
+        total = jnp.zeros((VEC_STEP, 128), F32)
+        for step, weight in ((0, 1.0), (1, 2.0), (2, 2.0), (3, 2.0), (4, 1.0)):
+            moved = left if step == 0 else pltpu.roll(left, step, axis=0)
+            products = jnp.sum(left * moved, axis=1, keepdims=True) * weight
+            for k in range(8):
+                total = total + products[k : k + 1, :] * (right[k] * right[(k - step) % 8])
+        return col_sum(total)
 
     def after_last(self):
         r, at, steps = (self.refs, self.at, self.steps)
-        fill_blocks(r, (0,))
-        self.start(self.sum_sibling(0))
-        fill_vec(r)
-        self.start(self.small_sum(0))
-        self.add_grp(1)
+        fill_late(r, r.late_d.at[at.dp])
+        for index in range(7):
+            self.start(self.late_sum(index))
         moments = [r.start[g] + s for g in range(GROUPS) for s in range(ROLLOUT)]
         intervals = [r.interval[g] for g in range(GROUPS) for s in range(ROLLOUT)]
-        r.cond_t[...] = jnp.transpose(condition_rows(moments, intervals, r.lead))
-        self.small_sum(0).wait_recv()
-        r.vec_z[at.z] = r.vec[...] + r.vec_sib[...]
-        for index in steps:
-            self.start(self.small_sum(index))
-        self.add_sibling(0)
+        r.cond_out[...] = condition_rows(moments, intervals, r.lead)
         self.add_grp(2)
-        square = self.add_z(1)
-        for index in steps:
-            self.small_sum(index).wait_recv()
-        r.vec_g[at.grp] = r.vec_z[0] + r.vec_z[1] + r.vec_z[2] + r.vec_z[3]
-        for index in steps:
-            self.start(self.small_sum(3 + index))
-        square = square + self.add_z(2)
-        self.add_grp(0)
-
+        for index in range(7):
+            self.late_sum(index).wait_recv()
+        total = r.late_d[0]
+        for d in range(1, 2 * LAYERS):
+            total = total + r.late_d[d]
+        r.late_g[at.grp] = total
+        for index in range(7, 10):
+            self.start(self.late_sum(index))
+        square = self.add_z(0) + self.add_z(3) + self.add_z(4) + self.add_z(1)
         for index in steps:
             self.small_sum(3 + index).wait_recv()
-        own_cond = r.cond_t[span(SLAB * at.dp, SLAB), :]
-        columns = [jnp.broadcast_to(own_cond[:, k : k + 1], (SLAB, 128)) for k in range(8)]
-        ada = r.a.at[0:864]
-
-        def ada_tile(j, total):
-            tile = jnp.zeros((SLAB, 128), F32)
-            for g in range(GROUPS):
-                for s in range(ROLLOUT):
-                    row = r.vec_g[g, pl.ds(24 + 18 * s + j, 1), :]
-                    tile = tile + columns[ROLLOUT * g + s] * row
-            ada[pl.ds(j, SLAB, stride=18), :] = tile
-            return total + col_sum(tile * tile)
-
-        ada_square = lax.fori_loop(0, 18, ada_tile, jnp.zeros((1, 128), F32))
-        puts = [local(ada, r.ada_far, r.in_sems.at[0])]
-        vec_sum = r.vec_g[0] + r.vec_g[1] + r.vec_g[2] + r.vec_g[3]
+        for index in range(7, 10):
+            self.late_sum(index).wait_recv()
+        vec = r.vec_out
+        vec[...] = r.vec_g[...]
+        for g in range(GROUPS):
+            vec[g, 0:6, :] = r.late_g[g, 0:6, :]
+            vec[g, VEC_STEP : VEC_STEP + 6, :] = r.late_g[g, 6:12, :]
+        vec_sum = vec[0] + vec[1] + vec[2] + vec[3]
         r.bias_out[0:24, :] = vec_sum[0:24]
-        r.bias_out[24:42, :] = vec_sum[24:42] + vec_sum[42:60]
-        r.bias_out[42:48, :] = jnp.zeros((6, 128), F32)
-
-        square = square + 0.25 * ada_square + self.add_z(0)
-        r.square_d[at.dp] = jnp.broadcast_to(square, (8, 128))
-        for index in range(7):
-            self.start(self.square_sum(index))
-        for index in range(7):
-            self.square_sum(index).wait_recv()
-        total = r.square_d[0]
-        for d in range(1, 2 * LAYERS):
-            total = total + r.square_d[d]
-        r.square_g[at.grp] = total
-        for index in range(7, 10):
-            self.start(self.square_sum(index))
-        for unit in (1, 2, 0):
+        r.bias_out[24:48, :] = vec_sum[24:48] + vec_sum[48:72]
+        ada_square = self.ada_square()
+        square = square + self.add_z(2)
+        own = 2 * LAYERS * at.grp + at.dp
+        r.squares[own] = square
+        for k in range(1, 8 * LAYERS):
+            self.start(self.square_sum(k))
+        for unit in range(5):
             for k in steps:
                 self.share_piece(unit, k).wait_recv()
-            puts.append(local(self.got(unit, "piece"), r.pieces_far.at[unit], r.in_sems.at[1 + unit]))
-        for index in range(7, 10):
-            self.square_sum(index).wait_recv()
+        whole = [r.att0.at[HALF : HALF + 4 * SLAB], self.got(3, "piece"), self.got(4, "piece")]
+        puts = [
+            local(whole[unit], r.pieces_far.at[unit], r.in_sems.at[1 + unit])
+            for unit in range(UNITS)
+        ]
         bias_sum = r.bias_out[...]
-        total = r.square_g[0] + r.square_g[1] + r.square_g[2] + r.square_g[3]
-        total = total + col_sum(bias_sum * bias_sum)
+        total = col_sum(bias_sum * bias_sum) + ada_square
+        for k in range(1, 8 * LAYERS):
+            self.square_sum(k).wait_recv()
+        for device in range(8 * LAYERS):
+            total = total + r.squares[device]
         r.square_out[...] = jnp.broadcast_to(jnp.sum(total, axis=1, keepdims=True), (8, 128))
         for made in puts:
             made.wait()
@@ -796,18 +978,28 @@
                 self.gather_z(unit, k).wait_send()
                 for m in self.steps:
                     self.gather_grp(unit, k, m).wait_send()
-                self.sum_grp(unit, k).wait_send()
+            for k in range(4):
+                self.gather_sibling(unit, k).wait_send()
+        for unit in range(5):
+            self.sum_sibling(unit).wait_send()
+            if unit < 3:
+                for k in self.steps:
+                    self.sum_grp(unit, k).wait_send()
+            else:
+                self.sum_one(unit, 0).wait_send()
+                self.sum_one(unit, 1).wait_send()
+                self.sum_two(unit).wait_send()
+            for k in self.steps:
                 self.sum_z(unit, k).wait_send()
                 self.share_piece(unit, k).wait_send()
-            for k in range(4):
-                self.gather_sibling(unit, k).wait_send()
-            self.sum_sibling(unit).wait_send()
         for index in range(8):
             self.small(index).wait_send()
         for index in range(7):
             self.small_sum(index).wait_send()
         for index in range(10):
-            self.square_sum(index).wait_send()
+            self.late_sum(index).wait_send()
+        for step in range(1, 8 * LAYERS):
+            self.square_sum(step).wait_send()
 
 
 correction = 1.0 - 0.5**ADAM_STEP
@@ -826,15 +1018,12 @@
 
 def finish_kernel(names, *refs):
     r = Refs(names, refs)
-    loads = {
-        name: local(getattr(r, name + "_far"), getattr(r, name), r.in_sems.at[index])
-        for index, name in enumerate(("pieces", "grad_ada"))
-    }
+    loads = {"pieces": local(r.pieces_far, r.pieces, r.in_sems.at[0])}
     for index, name in enumerate(STATE):
         for kind in range(3):
             loads[name, kind] = local(
                 getattr(r, f"{name}_in{kind}"), getattr(r, f"{name}_{kind}"),
-                r.in_sems.at[2 + 3 * index + kind],
+                r.in_sems.at[1 + 3 * index + kind],
             )
     streams = [
         local(getattr(r, name + "_in"), getattr(r, name), r.stream_sems.at[index])
@@ -863,6 +1052,20 @@
         r.bias_out2[place] = second_new.reshape(size)
         r.bias_out3[place] = new.reshape(size).astype(BF)
 
+    r.cond_t[...] = jnp.transpose(r.cond[...])
+    own_cond = r.cond_t[pl.ds(pl.multiple_of(SLAB * owner, SLAB), SLAB), :]
+    columns = [jnp.broadcast_to(own_cond[:, k : k + 1], (SLAB, 128)) for k in range(8)]
+
+    def ada_tile(j, carry):
+        tile = jnp.zeros((SLAB, 128), F32)
+        for k in range(8):
+            row = r.vec[k // ROLLOUT, pl.ds(VEC_STEP * (k % ROLLOUT + 1) + j, 1), :]
+            tile = tile + columns[k] * row
+        r.grad_ada[pl.ds(j, SLAB, stride=18), :] = tile
+        return carry
+
+    lax.fori_loop(0, 18, ada_tile, 0)
+
     loads["pieces"].wait()
     piece = r.pieces
     for g in range(3):
@@ -884,8 +1087,6 @@
     for index, name in enumerate(STATE):
         for kind in range(3):
             loads[name, kind].wait()
-        if name == "ada":
-            loads["grad_ada"].wait()
         grad, low = (getattr(r, "grad_" + name), getattr(r, name + "_low"))
         state = [getattr(r, f"{name}_{kind}") for kind in range(3)]
 
@@ -910,13 +1111,13 @@
         made.wait()
 
 
-def finish(y, dx, pieces, ada, bias_sum, square, masters, firsts, seconds):
+def finish(y, dx, pieces, vec, cond, bias_sum, square, masters, firsts, seconds):
     vmem, hbm, dma = (pltpu.VMEM, pl.ANY, pltpu.SemaphoreType.DMA)
     state = list(zip(masters, firsts, seconds))
     shapes = {name: (arrays[0].size // 128, 128) for name, arrays in zip(STATE, state)}
     ins = [
         ("square", square, vmem), ("bias_sum", bias_sum, vmem), ("pieces_far", pieces, hbm),
-        ("grad_ada_far", ada, hbm), ("y_in", y, hbm), ("dx_in", dx, hbm),
+        ("vec", vec, vmem), ("cond", cond, vmem), ("y_in", y, hbm), ("dx_in", dx, hbm),
         *[(f"bias_in{kind}", array, vmem) for kind, array in enumerate(state[5])],
         *[
             (f"{name}_in{kind}", array.reshape(-1, 128), hbm)
@@ -934,7 +1135,7 @@
         *[(f"{name}_{kind}", vmem(shapes[name], F32)) for name in STATE for kind in range(3)],
         *[(f"{name}_low", vmem(shapes[name], BF)) for name in STATE],
         *[(f"grad_{name}", vmem(shapes[name], F32)) for name in STATE],
-        ("in_sems", dma((17,))), ("stream_sems", dma((2,))), ("out_sems", dma((20,))),
+        ("cond_t", vmem((D, 8), F32)), ("in_sems", dma((16,))), ("stream_sems", dma((2,))), ("out_sems", dma((20,))),
     ]
     names = [item[0] for item in (*ins, *outs, *scratch)]
     norm, y, dx, *rest = pl.pallas_call(
@@ -955,16 +1156,18 @@
     r = Refs(names, refs)
     if hooked is Together:
         r.masters = {name: getattr(r, "far_" + name) for name in MASTERS}
-        for name in ("gz", "gx", "gs", "gm", "rs", "rx", "rz", "ra", "rv", "rq"):
+        for name in ("gz", "gx", "gs", "gm", "rs", "rx", "rz", "ra", "rv", "rq", "rl"):
             setattr(r, name, (getattr(r, name + "_out"), getattr(r, name + "_in")))
     hooks = hooked(r)
     length = r.x.shape[0]
     pairs = HEADS // 2
     get_cot = local(r.cot_far, r.cot, r.out_sems.at[2])
 
-    def over_rows(body):
+    def over_rows(body, after=None):
         def step(i, carry):
             body(pl.ds(pl.multiple_of(i * ROWS, ROWS), ROWS))
+            if after is not None:
+                after(i)
             return carry
 
         lax.fori_loop(0, length // ROWS, step, 0)
@@ -1022,7 +1225,7 @@
         for h in range(pairs - 2, pairs):
             save(step, h).wait()
 
-    def attend_back(step, qkv, after):
+    def attend_back(step, qkv, between, after):
         def body(h):
             fetch(step, h).wait()
             attend_back_pair(
@@ -1030,6 +1233,7 @@
                 r.datt[:, columns(h)], r.p.at[lax.rem(h, 2)],
                 r.dqkv.at[:, columns(h)], r.dqkv.at[:, columns(h, D)],
                 r.dqkv.at[:, columns(h, 2 * D)], r.turned,
+                None if between is None else lambda: between(h),
             )
 
             @pl.when(h + 2 < pairs)
@@ -1078,29 +1282,37 @@
     get_cot.wait()
     over_rows(turn)
     put_y = local(r.y, r.y_far, r.out_sems.at[0])
-    attend_back(1, r.qkv1, nothing)
+    attend_back(1, r.qkv1, None, nothing)
     for h in range(2):
         fetch(0, h).start()
 
     def join(rows):
         join_rows(
             r.dqkv.at[rows], r.x1.at[rows], r.x.at[rows], a_refs(rows), r.gp.at[rows],
-            act_refs(rows), r.f.at[rows], r.att0.at[rows], r.rows, r.wa, r.wup, r.wdown,
-            r.dmid.at[rows], r.datt.at[rows], r.gqkv, r.gdown, r.gup, r.gproj, r.wide, r.narrow1,
-            r.narrow0, r.bias,
+            act_refs(rows), r.f.at[rows], r.rows, r.wa, r.wdown, r.att1.at[rows],
+            r.dmid.at[rows], r.gqkv, r.gdown, r.gup, r.wide, r.narrow1, r.narrow0, r.bias,
         )
 
+    def join_middle(rows):
+        join_middle_rows(
+            r.x.at[rows], a_refs(rows), act_refs(rows), r.att0.at[rows], r.rows, r.wa, r.wup,
+            r.dmid.at[rows], r.datt.at[rows], r.gproj, r.narrow0,
+        )
+
+    hooks.before_join()
     over_rows(join)
+    hooks.amid_join()
+    over_rows(join_middle)
     hooks.after_join()
-    attend_back(0, r.qkv0, hooks.after_back_pair)
+    attend_back(0, r.qkv0, hooks.amid_back_pair, hooks.after_back_pair)
 
     def last(rows):
         r.dmid[rows, :] = qkv_back(
             mod_reader(r.rows, 0), r.x[rows, :].astype(F32), r.dmid[rows, :],
-            r.dqkv[rows, :], r.wa, r.gqkv, r.narrow0, r.bias,
+            r.dqkv[rows, :], r.wa, r.narrow0, r.bias,
         )
 
-    over_rows(last)
+    over_rows(last, hooks.after_last_rows)
     put_dx = local(r.dmid, r.dx_far, r.out_sems.at[1])
     hooks.after_last()
     put_y.wait()
@@ -1129,7 +1341,7 @@
         ("turned", vmem((2, 128, length), BF)), ("wide", vmem((8, FF), F32)),
         ("narrow0", vmem((8, D), F32)), ("narrow1", vmem((8, D), F32)),
         ("bias", vmem((8, 3 * D), F32)), ("blocks", vmem((UNITS, 2 * HALF, PART), BF)),
-        ("rows", vmem((32, D), F32)), ("vec", vmem((64, 128), F32)),
+        ("rows", vmem((32, D), F32)), ("vec", vmem((VEC, 128), F32)), ("late", vmem((16, 128), F32)),
         ("in_sems", dma((5,))), ("p_sems", dma((2,))), ("out_sems", dma((3,))),
         *extra_scratch,
     ]
@@ -1150,7 +1362,7 @@
     y, dx, _, blocks, vec = block_call(
         Alone, inputs, cotangent,
         [("rows_far", rows, hbm), ("wa_far", wa, hbm), ("wup_far", wup, hbm), ("wdown_far", wdown, hbm)],
-        [("blocks_far", (UNITS, 2 * HALF, PART), BF, hbm), ("vec_far", (64, 128), F32, hbm)],
+        [("blocks_far", (UNITS, 2 * HALF, PART), BF, hbm), ("vec_far", (VEC, 128), F32, hbm)],
         [], {},
     )
     return (y, dx, blocks, vec)
@@ -1165,25 +1377,25 @@
     ]
     pairs_of = [
         ("gz", (UNITS, 3)), ("gx", (UNITS, 3, 3)), ("gs", (UNITS, 4)), ("gm", (8,)),
-        ("rs", (UNITS,)), ("rx", (UNITS, 3)), ("rz", (UNITS, 3)), ("ra", (UNITS, 3)),
-        ("rv", (7,)), ("rq", (10,)),
+        ("rs", (5,)), ("rx", (5, 3)), ("rz", (5, 3)), ("ra", (5, 3)),
+        ("rv", (7,)), ("rq", (8 * LAYERS,)), ("rl", (10,)),
     ]
-    y, dx, _, pieces, ada_grad, bias_sum, square = block_call(
+    y, dx, _, pieces, vec, cond, bias_sum, square = block_call(
         Together, inputs, cotangent,
         [("start", start, smem), ("interval", interval, smem), ("counts", counts, smem),
          ("lead", lead, vmem), ("bias_flat", bias, vmem), *far],
-        [("pieces_far", (UNITS, 4 * SLAB, PART), BF, hbm), ("ada_far", (18 * SLAB, 128), F32, hbm),
+        [("pieces_far", (UNITS, 4 * SLAB, PART), BF, hbm), ("vec_out", (GROUPS, VEC, 128), F32, vmem), ("cond_out", (8, D), F32, vmem),
          ("bias_out", (48, 128), F32, vmem), ("square_out", (8, 128), F32, vmem)],
         [("cond_t", vmem((D, 8), F32)), ("part_own", vmem((40, 128), F32)),
          ("part_sib", vmem((40, 128), F32)), ("part_z", vmem((LAYERS, 40, 128), F32)),
          ("bias_own", vmem((8, 128), F32)), ("bias_slot", vmem((LAYERS, 2, 8, 128), F32)), ("bias_full", vmem((48, 128), F32)),
-         ("vec_sib", vmem((64, 128), F32)), ("vec_z", vmem((LAYERS, 64, 128), F32)),
-         ("vec_g", vmem((GROUPS, 64, 128), F32)), ("square_d", vmem((8, 8, 128), F32)),
-         ("square_g", vmem((GROUPS, 8, 128), F32)), ("joined", pltpu.SemaphoreType.REGULAR),
+         ("vec_sib", vmem((VEC, 128), F32)), ("vec_z", vmem((LAYERS, VEC, 128), F32)),
+         ("vec_g", vmem((GROUPS, VEC, 128), F32)), ("late_d", vmem((8, 16, 128), F32)),
+         ("late_g", vmem((GROUPS, 16, 128), F32)), ("squares", vmem((8 * LAYERS, 1, 128), F32)), ("joined", pltpu.SemaphoreType.REGULAR), ("turned_back", pltpu.SemaphoreType.REGULAR),
          *[(name + end, dma(shape)) for name, shape in pairs_of for end in ("_out", "_in")]],
         dict(collective_id=0, has_side_effects=True),
     )
-    return (y, dx, pieces, ada_grad, bias_sum, square)
+    return (y, dx, pieces, vec, cond, bias_sum, square)
 
 
 def step_embedding(moment):
@@ -1232,7 +1444,7 @@
     owner = lax.axis_index("dp")
     vec = vec.reshape(-1)
     split = 4 * D + FF
-    dmod = vec[split : split + ROLLOUT * 6 * D].reshape(ROLLOUT, 6 * D)
+    dmod = vec[split:].reshape(ROLLOUT, VEC_STEP * 128)[:, : 6 * D]
     dmod_all = lax.all_gather(lax.psum(dmod, "dp"), "grp")
     bias_sum = lax.psum(vec[:split], ("grp", "dp"))
     bias_sum = jnp.concatenate([bias_sum, jnp.sum(dmod_all, axis=(0, 1))])
@@ -1284,11 +1496,11 @@
         result, input_grad, blocks, vec = block_alone(inputs, cotangent, rows, wa, wup, wdown)
         rest = plain_update(owner_columns, vec, blocks, masters, firsts, seconds)
         return (result, input_grad, *rest)
-    result, input_grad, pieces, ada_grad, bias_sum, square = block_together(
+    result, input_grad, pieces, vec, cond, bias_sum, square = block_together(
         inputs, cotangent, rollout_start, group_interval, sample_counts, lead_table, masters
     )
     return finish(
-        result, input_grad, pieces, ada_grad, bias_sum, square, masters, firsts, seconds
+        result, input_grad, pieces, vec, cond, bias_sum, square, masters, firsts, seconds
     )
 
 

time: 158 us -> 152 us (0.962)
  Pallas kernels: 157 us -> 151 us
    pallas_call x1, Pallas kernels: 149 us -> 142 us  [block_call(): pl.pallas_call(functools.partial(block_kernel, names, hooked), in_specs=[...]
where the time goes in v6:
time: 152 us
  Pallas kernels  151 us (99%)
    pallas_call x1, Pallas kernels, block_call(): pl.pallas_call(functools.partial(block_kernel, names, hooked), in_specs=[...  142 us
    pallas_call x1, Pallas kernels, finish(): pl.pallas_call(functools.partial(finish_kernel, names), in_specs=[pl.Bloc...  8.8 us

profile of v6, /device:TPU:0, one launch (start us, length us, event | category | flops | bytes accessed | tf_op | source)
XLA Modules:
  0.0 152.1 jit_solution(7813062103363896783)
XLA Ops:
  0.7 142.4 %block.1 = (f32[1024,384]{1,0:T(8,128)}, f32[1024,384]{1,0:T(8,128)}, bf16[2,6,1024,1024]{3,2,1,0:T(8,128)(2,1)}, bf16[3,192,384]{2,1,0:T(8,128)(2,1)}, f32[4,72...) custom-call(bf16[1024,384]{1,0:T(8,128)(2,1)} %refs_0_.1, bf16[1024,384]{1,0:T(8,128)(2,1)} %refs_1_.1, ...), custom_call_target="tpu_custom_call" | custom-call | tf_op jit(solution)/shard_map/block/pallas_call | solution.py:1349
  143.1 8.8 %finish.1 = (f32[1,1]{1,0:T(1,128)}, f32[1024,384]{1,0:T(8,128)}, f32[1024,384]{1,0:T(8,128)}, f32[432,128]{1,0:T(8,128)}, f32[144,128]{1,0:T(8,128)}, /*index=5...) custom-call(f32[8,128]{1,0:T(8,128)} %get-tuple-element.61.refs_0_, ...), custom_call_target="tpu_custom_call" | custom-call | tf_op jit(solution)/shard_map/finish/pallas_call | solution.py:1141

commit v7 on v6

--- a/solution.py
+++ b/solution.py
@@ -405,13 +405,17 @@
 
 def fill_blocks(refs):
     share = refs.rows[ROW_SHARE : ROW_SHARE + 1, :]
-    for d in range(8):
-        own = slice(SLAB * d, SLAB * (d + 1))
+
+    def owner(d, carry):
         for g in range(4):
-            up = refs.gup[own, PART * g : PART * (g + 1)]
-            down = refs.gdown[SLAB * (4 * d + g) : SLAB * (4 * d + g + 1), :]
-            refs.blocks[1, block_rows(d, g), :] = (up * share).astype(BF)
-            refs.blocks[2, block_rows(d, g), :] = (down * share).astype(BF)
+            there = span(HALF * (d % 2) + 4 * SLAB * g + SLAB * (d // 2), SLAB)
+            up = refs.gup[span(SLAB * d, SLAB), PART * g : PART * (g + 1)]
+            down = refs.gdown[span(SLAB * (4 * d + g), SLAB), :]
+            refs.blocks[1, there, :] = (up * share).astype(BF)
+            refs.blocks[2, there, :] = (down * share).astype(BF)
+        return carry
+
+    lax.fori_loop(0, 8, owner, 0)
 
 
 def fill_pair(refs, h):
@@ -903,9 +907,9 @@
 
     def ada_square(self):
         r = self.refs
-        left = r.cond_out[...]
+        left = r.cond[...]
         right = [
-            r.vec_out[g, VEC_STEP * (s + 1) : VEC_STEP * (s + 2), :]
+            r.vec_sum[g, VEC_STEP * (s + 1) : VEC_STEP * (s + 2), :]
             for g in range(GROUPS)
             for s in range(ROLLOUT)
         ]
@@ -924,7 +928,7 @@
             self.start(self.late_sum(index))
         moments = [r.start[g] + s for g in range(GROUPS) for s in range(ROLLOUT)]
         intervals = [r.interval[g] for g in range(GROUPS) for s in range(ROLLOUT)]
-        r.cond_out[...] = condition_rows(moments, intervals, r.lead)
+        r.cond[...] = condition_rows(moments, intervals, r.lead)
         self.add_grp(2)
         for index in range(7):
             self.late_sum(index).wait_recv()
@@ -939,7 +943,7 @@
             self.small_sum(3 + index).wait_recv()
         for index in range(7, 10):
             self.late_sum(index).wait_recv()
-        vec = r.vec_out
+        vec = r.vec_sum
         vec[...] = r.vec_g[...]
         for g in range(GROUPS):
             vec[g, 0:6, :] = r.late_g[g, 0:6, :]
@@ -953,11 +957,27 @@
         r.squares[own] = square
         for k in range(1, 8 * LAYERS):
             self.start(self.square_sum(k))
+
+        r.cond_t[...] = jnp.transpose(r.cond[...])
+        own_cond = r.cond_t[span(SLAB * at.dp, SLAB), :]
+        columns = [jnp.broadcast_to(own_cond[:, k : k + 1], (SLAB, 128)) for k in range(8)]
+        ada = r.a.at[0 : 18 * SLAB]
+
+        def ada_tile(j, carry):
+            tile = jnp.zeros((SLAB, 128), F32)
+            for k in range(8):
+                row = vec[k // ROLLOUT, pl.ds(VEC_STEP * (k % ROLLOUT + 1) + j, 1), :]
+                tile = tile + columns[k] * row
+            ada[pl.ds(j, SLAB, stride=18), :] = tile
+            return carry
+
+        lax.fori_loop(0, 18, ada_tile, 0)
         for unit in range(5):
             for k in steps:
                 self.share_piece(unit, k).wait_recv()
         whole = [r.att0.at[HALF : HALF + 4 * SLAB], self.got(3, "piece"), self.got(4, "piece")]
-        puts = [
+        puts = [local(ada, r.ada_far, r.in_sems.at[0])]
+        puts += [
             local(whole[unit], r.pieces_far.at[unit], r.in_sems.at[1 + unit])
             for unit in range(UNITS)
         ]
@@ -1013,12 +1033,16 @@
     return (master - learn_rate * (update + decay * master), first_new, second_new)
 
 
+CHUNK = 48
 STATE = ("qkv", "proj", "up", "down", "ada")
 
 
 def finish_kernel(names, *refs):
     r = Refs(names, refs)
-    loads = {"pieces": local(r.pieces_far, r.pieces, r.in_sems.at[0])}
+    loads = {
+        "pieces": local(r.pieces_far, r.pieces, r.in_sems.at[0]),
+        "grad": local(r.grad_ada_far, r.grad_ada, r.in_sems.at[16]),
+    }
     for index, name in enumerate(STATE):
         for kind in range(3):
             loads[name, kind] = local(
@@ -1034,6 +1058,50 @@
     clip = grad_limit / jnp.maximum(norm, grad_limit)
     row_clip = clip[0:1, :]
 
+    loads["pieces"].wait()
+    piece = r.pieces
+
+    def unpack(name):
+        for j in range(3):
+            columns = slice(128 * j, 128 * j + 128)
+            if name == "proj":
+                r.grad_proj[pl.ds(j, SLAB, stride=3), :] = piece[0, 3 * SLAB :, columns].astype(F32)
+            for g in range(GROUPS):
+                rows = slice(SLAB * g, SLAB * (g + 1))
+                if name == "qkv" and g < 3:
+                    r.grad_qkv[pl.ds(3 * g + j, SLAB, stride=9), :] = piece[0, rows, columns].astype(F32)
+                if name == "up":
+                    r.grad_up[pl.ds(3 * g + j, SLAB, stride=12), :] = piece[1, rows, columns].astype(F32)
+                if name == "down":
+                    r.grad_down[pl.ds(3 * SLAB * g + j, SLAB, stride=3), :] = piece[2, rows, columns].astype(F32)
+
+    stores = []
+    for index, name in enumerate(STATE):
+        for kind in range(3):
+            loads[name, kind].wait()
+        if name == "ada":
+            loads["grad"].wait()
+        unpack(name)
+        grad, low = (getattr(r, "grad_" + name), getattr(r, name + "_low"))
+        state = [getattr(r, f"{name}_{kind}") for kind in range(3)]
+
+        def chunk(i, carry):
+            rows = pl.ds(pl.multiple_of(CHUNK * i, 16), CHUNK)
+            new, first_new, second_new = adam(
+                *(ref[rows, :] for ref in state), grad[rows, :] * row_clip, 0.1
+            )
+            for ref, value in zip(state, (new, first_new, second_new)):
+                ref[rows, :] = value
+            low[rows, :] = new.astype(BF)
+            return carry
+
+        lax.fori_loop(0, grad.shape[0] // CHUNK, chunk, 0)
+        for kind, ref in enumerate((*state, low)):
+            stores.append(local(ref, getattr(r, f"{name}_out{kind}"), r.out_sems.at[4 * index + kind]))
+        if index < 2:
+            name = ("y", "dx")[index]
+            streams[index].wait()
+            stores.append(local(getattr(r, name), getattr(r, name + "_out"), r.stream_sems.at[index]))
     owner = lax.axis_index("dp")
     lane = lax.broadcasted_iota(jnp.int32, (1, 128), 1)
     first = 672 * owner // 128
@@ -1052,72 +1120,17 @@
         r.bias_out2[place] = second_new.reshape(size)
         r.bias_out3[place] = new.reshape(size).astype(BF)
 
-    r.cond_t[...] = jnp.transpose(r.cond[...])
-    own_cond = r.cond_t[pl.ds(pl.multiple_of(SLAB * owner, SLAB), SLAB), :]
-    columns = [jnp.broadcast_to(own_cond[:, k : k + 1], (SLAB, 128)) for k in range(8)]
-
-    def ada_tile(j, carry):
-        tile = jnp.zeros((SLAB, 128), F32)
-        for k in range(8):
-            row = r.vec[k // ROLLOUT, pl.ds(VEC_STEP * (k % ROLLOUT + 1) + j, 1), :]
-            tile = tile + columns[k] * row
-        r.grad_ada[pl.ds(j, SLAB, stride=18), :] = tile
-        return carry
-
-    lax.fori_loop(0, 18, ada_tile, 0)
-
-    loads["pieces"].wait()
-    piece = r.pieces
-    for g in range(3):
-        for j in range(3):
-            r.grad_qkv[pl.ds(3 * g + j, SLAB, stride=9), :] = piece[
-                0, SLAB * g : SLAB * (g + 1), 128 * j : 128 * j + 128
-            ].astype(F32)
-    for j in range(3):
-        columns = slice(128 * j, 128 * j + 128)
-        r.grad_proj[pl.ds(j, SLAB, stride=3), :] = piece[0, 3 * SLAB :, columns].astype(F32)
-    for g in range(GROUPS):
-        rows = slice(SLAB * g, SLAB * (g + 1))
-        for j in range(3):
-            columns = slice(128 * j, 128 * j + 128)
-            r.grad_up[pl.ds(3 * g + j, SLAB, stride=12), :] = piece[1, rows, columns].astype(F32)
-            r.grad_down[pl.ds(3 * SLAB * g + j, SLAB, stride=3), :] = piece[2, rows, columns].astype(F32)
-
-    stores = []
-    for index, name in enumerate(STATE):
-        for kind in range(3):
-            loads[name, kind].wait()
-        grad, low = (getattr(r, "grad_" + name), getattr(r, name + "_low"))
-        state = [getattr(r, f"{name}_{kind}") for kind in range(3)]
-
-        def chunk(i, carry):
-            rows = pl.ds(pl.multiple_of(16 * i, 16), 16)
-            new, first_new, second_new = adam(
-                *(ref[rows, :] for ref in state), grad[rows, :] * row_clip, 0.1
-            )
-            for ref, value in zip(state, (new, first_new, second_new)):
-                ref[rows, :] = value
-            low[rows, :] = new.astype(BF)
-            return carry
-
-        lax.fori_loop(0, grad.shape[0] // 16, chunk, 0, unroll=3)
-        for kind, ref in enumerate((*state, low)):
-            stores.append(local(ref, getattr(r, f"{name}_out{kind}"), r.out_sems.at[4 * index + kind]))
-        if index < 2:
-            name = ("y", "dx")[index]
-            streams[index].wait()
-            stores.append(local(getattr(r, name), getattr(r, name + "_out"), r.stream_sems.at[index]))
     for made in stores:
         made.wait()
 
 
-def finish(y, dx, pieces, vec, cond, bias_sum, square, masters, firsts, seconds):
+def finish(y, dx, pieces, ada, bias_sum, square, masters, firsts, seconds):
     vmem, hbm, dma = (pltpu.VMEM, pl.ANY, pltpu.SemaphoreType.DMA)
     state = list(zip(masters, firsts, seconds))
     shapes = {name: (arrays[0].size // 128, 128) for name, arrays in zip(STATE, state)}
     ins = [
         ("square", square, vmem), ("bias_sum", bias_sum, vmem), ("pieces_far", pieces, hbm),
-        ("vec", vec, vmem), ("cond", cond, vmem), ("y_in", y, hbm), ("dx_in", dx, hbm),
+        ("grad_ada_far", ada, hbm), ("y_in", y, hbm), ("dx_in", dx, hbm),
         *[(f"bias_in{kind}", array, vmem) for kind, array in enumerate(state[5])],
         *[
             (f"{name}_in{kind}", array.reshape(-1, 128), hbm)
@@ -1135,7 +1148,7 @@
         *[(f"{name}_{kind}", vmem(shapes[name], F32)) for name in STATE for kind in range(3)],
         *[(f"{name}_low", vmem(shapes[name], BF)) for name in STATE],
         *[(f"grad_{name}", vmem(shapes[name], F32)) for name in STATE],
-        ("cond_t", vmem((D, 8), F32)), ("in_sems", dma((16,))), ("stream_sems", dma((2,))), ("out_sems", dma((20,))),
+        ("in_sems", dma((17,))), ("stream_sems", dma((2,))), ("out_sems", dma((20,))),
     ]
     names = [item[0] for item in (*ins, *outs, *scratch)]
     norm, y, dx, *rest = pl.pallas_call(
@@ -1163,14 +1176,14 @@
     pairs = HEADS // 2
     get_cot = local(r.cot_far, r.cot, r.out_sems.at[2])
 
-    def over_rows(body, after=None):
+    def over_rows(body, after=None, size=ROWS):
         def step(i, carry):
-            body(pl.ds(pl.multiple_of(i * ROWS, ROWS), ROWS))
+            body(pl.ds(pl.multiple_of(i * size, size), size))
             if after is not None:
                 after(i)
             return carry
 
-        lax.fori_loop(0, length // ROWS, step, 0)
+        lax.fori_loop(0, length // size, step, 0)
 
     def columns(h, offset=0):
         return pl.ds(pl.multiple_of(offset + 128 * h, 128), 128)
@@ -1185,13 +1198,15 @@
     def act_refs(rows):
         first = rows.start
         return [
-            r.act.at[pl.ds(pl.multiple_of(length * part + first, ROWS), ROWS)] for part in range(4)
+            r.act.at[pl.ds(pl.multiple_of(length * part + first, ROWS), rows.size)]
+            for part in range(4)
         ]
 
     def a_refs(rows):
         first = rows.start
         return [
-            r.a.at[pl.ds(pl.multiple_of(length * part + first, ROWS), ROWS)] for part in range(3)
+            r.a.at[pl.ds(pl.multiple_of(length * part + first, ROWS), rows.size)]
+            for part in range(3)
         ]
 
     def save(step, h):
@@ -1262,11 +1277,18 @@
             r.qkv1.at[rows],
         )
 
-    over_rows(middle)
+    over_rows(middle, size=2 * ROWS)
     finish_saves(0)
     attend(1, r.qkv1, r.att1, nothing)
 
-    for ref in (r.gqkv, r.gproj, r.gup, r.gdown, r.wide, r.narrow0, r.narrow1, r.bias):
+    def clear(i, carry):
+        for ref in (r.gqkv, r.gproj, r.gup, r.gdown):
+            size = ref.shape[0] // 8
+            ref[span(i * size, size), :] = jnp.zeros((size, ref.shape[1]), F32)
+        return carry
+
+    lax.fori_loop(0, 8, clear, 0)
+    for ref in (r.wide, r.narrow0, r.narrow1, r.bias):
         ref[...] = jnp.zeros_like(ref)
 
     def turn(rows):
@@ -1280,7 +1302,7 @@
     for h in range(2):
         fetch(1, h).start()
     get_cot.wait()
-    over_rows(turn)
+    over_rows(turn, size=2 * ROWS)
     put_y = local(r.y, r.y_far, r.out_sems.at[0])
     attend_back(1, r.qkv1, None, nothing)
     for h in range(2):
@@ -1302,7 +1324,7 @@
     hooks.before_join()
     over_rows(join)
     hooks.amid_join()
-    over_rows(join_middle)
+    over_rows(join_middle, size=2 * ROWS)
     hooks.after_join()
     attend_back(0, r.qkv0, hooks.amid_back_pair, hooks.after_back_pair)
 
@@ -1380,22 +1402,23 @@
         ("rs", (5,)), ("rx", (5, 3)), ("rz", (5, 3)), ("ra", (5, 3)),
         ("rv", (7,)), ("rq", (8 * LAYERS,)), ("rl", (10,)),
     ]
-    y, dx, _, pieces, vec, cond, bias_sum, square = block_call(
+    y, dx, _, pieces, ada_grad, bias_sum, square = block_call(
         Together, inputs, cotangent,
         [("start", start, smem), ("interval", interval, smem), ("counts", counts, smem),
          ("lead", lead, vmem), ("bias_flat", bias, vmem), *far],
-        [("pieces_far", (UNITS, 4 * SLAB, PART), BF, hbm), ("vec_out", (GROUPS, VEC, 128), F32, vmem), ("cond_out", (8, D), F32, vmem),
+        [("pieces_far", (UNITS, 4 * SLAB, PART), BF, hbm), ("ada_far", (18 * SLAB, 128), F32, hbm),
          ("bias_out", (48, 128), F32, vmem), ("square_out", (8, 128), F32, vmem)],
         [("cond_t", vmem((D, 8), F32)), ("part_own", vmem((40, 128), F32)),
          ("part_sib", vmem((40, 128), F32)), ("part_z", vmem((LAYERS, 40, 128), F32)),
          ("bias_own", vmem((8, 128), F32)), ("bias_slot", vmem((LAYERS, 2, 8, 128), F32)), ("bias_full", vmem((48, 128), F32)),
          ("vec_sib", vmem((VEC, 128), F32)), ("vec_z", vmem((LAYERS, VEC, 128), F32)),
          ("vec_g", vmem((GROUPS, VEC, 128), F32)), ("late_d", vmem((8, 16, 128), F32)),
+         ("vec_sum", vmem((GROUPS, VEC, 128), F32)), ("cond", vmem((8, D), F32)),
          ("late_g", vmem((GROUPS, 16, 128), F32)), ("squares", vmem((8 * LAYERS, 1, 128), F32)), ("joined", pltpu.SemaphoreType.REGULAR), ("turned_back", pltpu.SemaphoreType.REGULAR),
          *[(name + end, dma(shape)) for name, shape in pairs_of for end in ("_out", "_in")]],
         dict(collective_id=0, has_side_effects=True),
     )
-    return (y, dx, pieces, vec, cond, bias_sum, square)
+    return (y, dx, pieces, ada_grad, bias_sum, square)
 
 
 def step_embedding(moment):
@@ -1496,11 +1519,11 @@
         result, input_grad, blocks, vec = block_alone(inputs, cotangent, rows, wa, wup, wdown)
         rest = plain_update(owner_columns, vec, blocks, masters, firsts, seconds)
         return (result, input_grad, *rest)
-    result, input_grad, pieces, vec, cond, bias_sum, square = block_together(
+    result, input_grad, pieces, ada_grad, bias_sum, square = block_together(
         inputs, cotangent, rollout_start, group_interval, sample_counts, lead_table, masters
     )
     return finish(
-        result, input_grad, pieces, vec, cond, bias_sum, square, masters, firsts, seconds
+        result, input_grad, pieces, ada_grad, bias_sum, square, masters, firsts, seconds
     )
 
 

time: 152 us -> 148 us (0.974)
  Pallas kernels: 151 us -> 147 us
    pallas_call x1, Pallas kernels: 142 us -> 139 us  [block_call(): pl.pallas_call(functools.partial(block_kernel, names, hooked), in_specs=[...]
where the time goes in v7:
time: 148 us
  Pallas kernels  147 us (99%)
    pallas_call x1, Pallas kernels, block_call(): pl.pallas_call(functools.partial(block_kernel, names, hooked), in_specs=[...  139 us
    pallas_call x1, Pallas kernels, finish(): pl.pallas_call(functools.partial(finish_kernel, names), in_specs=[pl.Bloc...  7.9 us

profile of v7, /device:TPU:0, one launch (start us, length us, event | category | flops | bytes accessed | tf_op | source)
XLA Modules:
  0.0 148.0 jit_solution(13370967201182841129)
XLA Ops:
  0.7 139.2 %block.1 = (f32[1024,384]{1,0:T(8,128)}, f32[1024,384]{1,0:T(8,128)}, bf16[2,6,1024,1024]{3,2,1,0:T(8,128)(2,1)}, bf16[3,192,384]{2,1,0:T(8,128)(2,1)}, f32[864,...) custom-call(bf16[1024,384]{1,0:T(8,128)(2,1)} %refs_0_.1, bf16[1024,384]{1,0:T(8,128)(2,1)} %refs_1_.1, s32[4]{0:T(128)} %refs_2_.1, ...), custom_call_target="tpu_custom_call" | custom-call | tf_op jit(solution)/shard_map/block/pallas_call | solution.py:1371
  139.9 7.9 %finish.1 = (f32[1,1]{1,0:T(1,128)}, f32[1024,384]{1,0:T(8,128)}, f32[1024,384]{1,0:T(8,128)}, f32[432,128]{1,0:T(8,128)}, f32[144,128]{1,0:T(8,128)}, /*index=5...) custom-call(f32[8,128]{1,0:T(8,128)} %get-tuple-element.60.refs_0_, ...), custom_call_target="tpu_custom_call" | custom-call | tf_op jit(solution)/shard_map/finish/pallas_call | solution.py:1154

commit v8 on v7

--- a/solution.py
+++ b/solution.py
@@ -347,6 +347,18 @@
     return made
 
 
+def clear_sums(r):
+    def clear(i, carry):
+        for ref in (r.gqkv, r.gproj, r.gup, r.gdown):
+            size = ref.shape[0] // 8
+            ref[span(i * size, size), :] = jnp.zeros((size, ref.shape[1]), F32)
+        return carry
+
+    lax.fori_loop(0, 8, clear, 0)
+    for ref in (r.wide, r.narrow0, r.narrow1, r.bias):
+        ref[...] = jnp.zeros_like(ref)
+
+
 class Alone:
     def __init__(self, refs):
         self.refs = refs
@@ -356,6 +368,7 @@
         sems = r.in_sems
         first = [local(r.wa_far, r.wa, sems.at[0]), local(r.rows_far, r.rows, sems.at[3])]
         self.later = [local(r.wup_far, r.wup, sems.at[1]), local(r.wdown_far, r.wdown, sems.at[2])]
+        clear_sums(r)
         for made in first:
             made.wait()
 
@@ -599,6 +612,7 @@
         for g in range(GROUPS):
             fill(2, stage["down"], 3, SLAB * g, 3 * SLAB * g)
 
+        clear_sums(r)
         self.small(0).wait_recv()
         self.small(1).wait_recv()
         r.part_z[at.z] = r.part_own[...] + r.part_sib[...]
@@ -939,6 +953,12 @@
         for index in range(7, 10):
             self.start(self.late_sum(index))
         square = self.add_z(0) + self.add_z(3) + self.add_z(4) + self.add_z(1)
+        square = square + self.add_z(2)
+        own = 2 * LAYERS * at.grp + at.dp
+        r.squares[own] = square
+        for k in range(1, 8 * LAYERS):
+            self.start(self.square_sum(k))
+
         for index in steps:
             self.small_sum(3 + index).wait_recv()
         for index in range(7, 10):
@@ -952,11 +972,6 @@
         r.bias_out[0:24, :] = vec_sum[0:24]
         r.bias_out[24:48, :] = vec_sum[24:48] + vec_sum[48:72]
         ada_square = self.ada_square()
-        square = square + self.add_z(2)
-        own = 2 * LAYERS * at.grp + at.dp
-        r.squares[own] = square
-        for k in range(1, 8 * LAYERS):
-            self.start(self.square_sum(k))
 
         r.cond_t[...] = jnp.transpose(r.cond[...])
         own_cond = r.cond_t[span(SLAB * at.dp, SLAB), :]
@@ -1076,7 +1091,8 @@
                     r.grad_down[pl.ds(3 * SLAB * g + j, SLAB, stride=3), :] = piece[2, rows, columns].astype(F32)
 
     stores = []
-    for index, name in enumerate(STATE):
+    for turn, name in enumerate(("qkv", "up", "down", "ada", "proj")):
+        index = STATE.index(name)
         for kind in range(3):
             loads[name, kind].wait()
         if name == "ada":
@@ -1098,10 +1114,10 @@
         lax.fori_loop(0, grad.shape[0] // CHUNK, chunk, 0)
         for kind, ref in enumerate((*state, low)):
             stores.append(local(ref, getattr(r, f"{name}_out{kind}"), r.out_sems.at[4 * index + kind]))
-        if index < 2:
-            name = ("y", "dx")[index]
-            streams[index].wait()
-            stores.append(local(getattr(r, name), getattr(r, name + "_out"), r.stream_sems.at[index]))
+        if turn < 2:
+            name = ("y", "dx")[turn]
+            streams[turn].wait()
+            stores.append(local(getattr(r, name), getattr(r, name + "_out"), r.stream_sems.at[turn]))
     owner = lax.axis_index("dp")
     lane = lax.broadcasted_iota(jnp.int32, (1, 128), 1)
     first = 672 * owner // 128
@@ -1172,8 +1188,9 @@
         for name in ("gz", "gx", "gs", "gm", "rs", "rx", "rz", "ra", "rv", "rq", "rl"):
             setattr(r, name, (getattr(r, name + "_out"), getattr(r, name + "_in")))
     hooks = hooked(r)
-    length = r.x.shape[0]
+    length = r.x_far.shape[0]
     pairs = HEADS // 2
+    get_x = local(r.x_far, r.x, r.out_sems.at[3])
     get_cot = local(r.cot_far, r.cot, r.out_sems.at[2])
 
     def over_rows(body, after=None, size=ROWS):
@@ -1265,6 +1282,7 @@
     def first(rows):
         r.qkv0[rows, :] = first_rows(r.x[rows, :], r.rows, r.wa)
 
+    get_x.wait()
     over_rows(first)
     hooks.after_first()
     attend(0, r.qkv0, r.att0, hooks.after_attend_pair)
@@ -1280,16 +1298,6 @@
     over_rows(middle, size=2 * ROWS)
     finish_saves(0)
     attend(1, r.qkv1, r.att1, nothing)
-
-    def clear(i, carry):
-        for ref in (r.gqkv, r.gproj, r.gup, r.gdown):
-            size = ref.shape[0] // 8
-            ref[span(i * size, size), :] = jnp.zeros((size, ref.shape[1]), F32)
-        return carry
-
-    lax.fori_loop(0, 8, clear, 0)
-    for ref in (r.wide, r.narrow0, r.narrow1, r.bias):
-        ref[...] = jnp.zeros_like(ref)
 
     def turn(rows):
         turn_rows(
@@ -1345,14 +1353,14 @@
     length = inputs.shape[0]
     vmem, hbm, dma = (pltpu.VMEM, pl.ANY, pltpu.SemaphoreType.DMA)
     weights = (ROLLOUT, HEADS, length, length)
-    ins = [("x", inputs, vmem), ("cot_far", cotangent, hbm), *extra_in]
+    ins = [("x_far", inputs, hbm), ("cot_far", cotangent, hbm), *extra_in]
     outs = [
         ("y_far", (length, D), F32, hbm), ("dx_far", (length, D), F32, hbm),
         ("p_far", weights, BF, hbm), *extra_out,
     ]
     scratch = [
         ("wa", vmem((D, FF), BF)), ("wup", vmem((D, FF), BF)), ("wdown", vmem((FF, D), BF)),
-        ("cot", vmem((length, D), BF)), ("qkv0", vmem((length, 3 * D), BF)),
+        ("x", vmem((length, D), BF)), ("cot", vmem((length, D), BF)), ("qkv0", vmem((length, 3 * D), BF)),
         ("qkv1", vmem((length, 3 * D), BF)), ("p", vmem((2, 2, length, length), BF)),
         ("att0", vmem((length, D), BF)), ("att1", vmem((length, D), BF)),
         *[(name, vmem((length, D), F32)) for name in ("f", "x1", "dmid", "y")], ("a", vmem((3 * length, 128), F32)),
@@ -1364,7 +1372,7 @@
         ("narrow0", vmem((8, D), F32)), ("narrow1", vmem((8, D), F32)),
         ("bias", vmem((8, 3 * D), F32)), ("blocks", vmem((UNITS, 2 * HALF, PART), BF)),
         ("rows", vmem((32, D), F32)), ("vec", vmem((VEC, 128), F32)), ("late", vmem((16, 128), F32)),
-        ("in_sems", dma((5,))), ("p_sems", dma((2,))), ("out_sems", dma((3,))),
+        ("in_sems", dma((5,))), ("p_sems", dma((2,))), ("out_sems", dma((4,))),
         *extra_scratch,
     ]
     names = [item[0] for item in (*ins, *outs, *scratch)]

time: 148 us -> 148 us (level)
  no operation moved by 1% of the time
where the time goes in v8:
time: 148 us; the launch traced here: 147 us
  Pallas kernels  146 us (99%)
    pallas_call x1, Pallas kernels, block_call(): pl.pallas_call(functools.partial(block_kernel, names, hooked), in_specs=[...  139 us
    pallas_call x1, Pallas kernels, finish(): pl.pallas_call(functools.partial(finish_kernel, names), in_specs=[pl.Bloc...  7.69 us

profile of v8, /device:TPU:0, one launch (start us, length us, event | category | flops | bytes accessed | tf_op | source)
XLA Modules:
  0.0 147.3 jit_solution(8340631764472605665)
XLA Ops:
  0.7 138.7 %block.1 = (f32[1024,384]{1,0:T(8,128)}, f32[1024,384]{1,0:T(8,128)}, bf16[2,6,1024,1024]{3,2,1,0:T(8,128)(2,1)}, bf16[3,192,384]{2,1,0:T(8,128)(2,1)}, f32[864,...) custom-call(bf16[1024,384]{1,0:T(8,128)(2,1)} %refs_0_.1, bf16[1024,384]{1,0:T(8,128)(2,1)} %refs_1_.1, s32[4]{0:T(128)} %refs_2_.1, ...), custom_call_target="tpu_custom_call" | custom-call | tf_op jit(solution)/shard_map/block/pallas_call | solution.py:1379
  139.4 7.7 %finish.1 = (f32[1,1]{1,0:T(1,128)}, f32[1024,384]{1,0:T(8,128)}, f32[1024,384]{1,0:T(8,128)}, f32[432,128]{1,0:T(8,128)}, f32[144,128]{1,0:T(8,128)}, /*index=5...) custom-call(f32[8,128]{1,0:T(8,128)} %get-tuple-element.60.refs_0_, ...), custom_call_target="tpu_custom_call" | custom-call | tf_op jit(solution)/shard_map/finish/pallas_call | solution.py:1170

commit v9 on v8

--- a/solution.py
+++ b/solution.py
@@ -1283,7 +1283,7 @@
         r.qkv0[rows, :] = first_rows(r.x[rows, :], r.rows, r.wa)
 
     get_x.wait()
-    over_rows(first)
+    over_rows(first, size=2 * ROWS)
     hooks.after_first()
     attend(0, r.qkv0, r.att0, hooks.after_attend_pair)
     hooks.before_middle()

time: 148 us -> 147 us (level)
  no operation moved by 1% of the time
where the time goes in v9:
time: 147 us
  Pallas kernels  146 us (99%)
    pallas_call x1, Pallas kernels, block_call(): pl.pallas_call(functools.partial(block_kernel, names, hooked), in_specs=[...  138 us
    pallas_call x1, Pallas kernels, finish(): pl.pallas_call(functools.partial(finish_kernel, names), in_specs=[pl.Bloc...  7.69 us

profile of v9, /device:TPU:0, one launch (start us, length us, event | category | flops | bytes accessed | tf_op | source)
XLA Modules:
  0.0 146.6 jit_solution(7353759591298466157)
XLA Ops:
  0.7 138.1 %block.1 = (f32[1024,384]{1,0:T(8,128)}, f32[1024,384]{1,0:T(8,128)}, bf16[2,6,1024,1024]{3,2,1,0:T(8,128)(2,1)}, bf16[3,192,384]{2,1,0:T(8,128)(2,1)}, f32[864,...) custom-call(bf16[1024,384]{1,0:T(8,128)(2,1)} %refs_0_.1, bf16[1024,384]{1,0:T(8,128)(2,1)} %refs_1_.1, s32[4]{0:T(128)} %refs_2_.1, ...), custom_call_target="tpu_custom_call" | custom-call | tf_op jit(solution)/shard_map/block/pallas_call | solution.py:1379
  138.7 7.7 %finish.1 = (f32[1,1]{1,0:T(1,128)}, f32[1024,384]{1,0:T(8,128)}, f32[1024,384]{1,0:T(8,128)}, f32[432,128]{1,0:T(8,128)}, f32[144,128]{1,0:T(8,128)}, /*index=5...) custom-call(f32[8,128]{1,0:T(8,128)} %get-tuple-element.60.refs_0_, ...), custom_call_target="tpu_custom_call" | custom-call | tf_op jit(solution)/shard_map/finish/pallas_call | solution.py:1170
